TPU v7x, 32 devices: a whole 2x2x4 slice. The times are simulated.
32 devices in a mesh: wide: 8 (over y, x, core), narrow: 4 (over z).
Axes of the slice: x: 2, y: 2, z: 4, core: 2. Of those that a mesh axis runs over, the one named last changes fastest.
Arguments:
- tokens: bfloat16 [16384, 1024], P(('wide', 'narrow')), may hold values from -32 to 32
- cotangent: bfloat16 [16384, 1024], P(('wide', 'narrow')), may hold values from -6 to 6
- seq_lengths: int32 [8, 3], P('wide'), may hold values from 1 to 1536, 2048 in all within a row
- step_count: int32 [1], replicated, may hold values from 6 to 20
- norm_params: float32 [2, 1024], replicated, may hold values from -1 to 4.5, as said below
- norm_first: float32 [2, 1024], replicated, may hold values from -12 to 12
- norm_second: float32 [2, 1024], replicated, may hold values from 8 to 32
- proj_weight: float32 [1024, 3072], P('narrow', 'wide'), may hold values from -0.1875 to 0.1875
- proj_first: float32 [1024, 3072], P('narrow', 'wide'), may hold values from -6 to 6
- proj_second: float32 [1024, 3072], P('narrow', 'wide'), may hold values from 2.2 to 9
- merge_weight: float32 [1024, 1024], P('narrow', 'wide'), may hold values from -0.75 to 0.75
- merge_first: float32 [1024, 1024], P('narrow', 'wide'), may hold values from -1.2 to 1.2
- merge_second: float32 [1024, 1024], P('narrow', 'wide'), may hold values from 0.09 to 0.36
- up_weight: float32 [1024, 4096], P(None, 'narrow'), may hold values from -0.1875 to 0.1875
- up_first: float32 [1024, 4096], P(None, 'narrow'), may hold values from -1.4 to 1.4
- up_second: float32 [1024, 4096], P(None, 'narrow'), may hold values from 0.12 to 0.5
- down_weight: float32 [4096, 1024], P('narrow'), may hold values from -0.09375 to 0.09375
- down_first: float32 [4096, 1024], P('narrow'), may hold values from -3.4 to 3.4
- down_second: float32 [4096, 1024], P('narrow'), may hold values from 0.7 to 2.9
Outputs:
- layer_out: bfloat16 [16384, 1024], P(('wide', 'narrow'))
- input_grad: float32 [16384, 1024], P(('wide', 'narrow'))
- grad_norm: float32 [1], replicated
- residual_rms: float32 [1], replicated
- norm_grads: float32 [2, 1024], replicated
- new_norm_params: float32 [2, 1024], replicated
- new_norm_first: float32 [2, 1024], replicated
- new_norm_second: float32 [2, 1024], replicated
- new_proj_weight: float32 [1024, 3072], P('narrow', 'wide')
- new_proj_first: float32 [1024, 3072], P('narrow', 'wide')
- new_proj_second: float32 [1024, 3072], P('narrow', 'wide')
- new_merge_weight: float32 [1024, 1024], P('narrow', 'wide')
- new_merge_first: float32 [1024, 1024], P('narrow', 'wide')
- new_merge_second: float32 [1024, 1024], P('narrow', 'wide')
- new_up_weight: float32 [1024, 4096], P(None, 'narrow')
- new_up_first: float32 [1024, 4096], P(None, 'narrow')
- new_up_second: float32 [1024, 4096], P(None, 'narrow')
- new_down_weight: float32 [4096, 1024], P('narrow')
- new_down_first: float32 [4096, 1024], P('narrow')
- new_down_second: float32 [4096, 1024], P('narrow')
- branch_norms: float32 [2], replicated
- new_proj_copy: bfloat16 [1024, 3072], P('narrow', 'wide')
- new_merge_copy: bfloat16 [1024, 1024], P('narrow', 'wide')
- new_up_copy: bfloat16 [1024, 4096], P(None, 'narrow')
- new_down_copy: bfloat16 [4096, 1024], P('narrow')
Inputs may be any that keep to these rules, and one draw needn't show every extreme that they name: `seq_lengths`: row g holds the lengths of the 3 sequences of group g, in order; they sum to 2048, and in every row the longest is exactly 1536. `norm_params`: row 0 holds the gains (positive), row 1 the biases.
All inputs are finite; a program needn't handle non-finite values.
Results may differ from a plain program's by a relative error of at most 0.02.
Values may be sent and summed in bfloat16 or wider, within the bound.
A program may use at most 320 MiB of HBM per device.

v0:
```python
from functools import partial
import math

import jax
import jax.numpy as jnp
from jax import lax
from jax.experimental import pallas as pl
from jax.experimental.pallas import tpu as pltpu
from jax.sharding import PartitionSpec as P

HEADS = 16
HEAD = 64
D = 1024
ROT = 16
LANES = 128
ROW_BLOCK = 512
NPARAMS = 12584960


norm_eps = 1e-05
adam_eps = 1e-08
beta_first = 0.5
beta_second = 0.5
decay_rate = 0.01
matrix_rate = 0.1
norm_rate = 1.0
warmup_steps = 20.0
masked_score = -1e30
short = pl.CostEstimate(flops=0, bytes_accessed=0, transcendentals=0)


def dot_last(left_side, right_side):
    return lax.dot_general(
        left_side, right_side, (((1,), (1,)), ((), ())), preferred_element_type=jnp.float32
    )


def dot_plain(left_side, right_side):
    return lax.dot_general(
        left_side, right_side, (((1,), (0,)), ((), ())), preferred_element_type=jnp.float32
    )


def dot_first(left_side, right_side):
    return lax.dot_general(
        left_side, right_side, (((0,), (0,)), ((), ())), preferred_element_type=jnp.float32
    )


def locate(lengths, token_index):
    seq_ends = jnp.cumsum(lengths)
    starts = seq_ends - lengths
    segment = jnp.sum(
        (seq_ends[None, :] <= token_index[:, None]).astype(jnp.int32), axis=1, dtype=jnp.int32
    )
    choose = segment[:, None] == jnp.arange(lengths.shape[0], dtype=jnp.int32)[None, :]
    seq_start = jnp.sum(jnp.where(choose, starts[None, :], 0), axis=1, dtype=jnp.int32)
    seq_end = jnp.sum(jnp.where(choose, seq_ends[None, :], 0), axis=1, dtype=jnp.int32)
    return (seq_start, seq_end)


def rotary_tables(position):
    half_rot = ROT // 2
    frequency = jnp.power(10000.0, -2.0 * jnp.arange(half_rot, dtype=jnp.float32) / ROT)
    row = jnp.concatenate([frequency, frequency, jnp.zeros((HEAD - ROT,), jnp.float32)])
    row = jnp.tile(row, LANES // HEAD)
    sign = jnp.where(jnp.arange(LANES) % HEAD < half_rot, -1.0, 1.0)
    phases = position.astype(jnp.float32)[:, None] * row[None, :]
    return (jnp.cos(phases), jnp.sin(phases) * sign[None, :])


def partner(field):
    half_rot = ROT // 2
    lane = lax.broadcasted_iota(jnp.int32, field.shape, 1) % HEAD
    return jnp.where(
        lane < half_rot,
        pltpu.roll(field, LANES - half_rot, 1),
        pltpu.roll(field, half_rot, 1),
    )


def project_kernel(rows_ref, weight_ref, cos_ref, sin_ref, out_ref):
    width = out_ref.shape[1]
    projected = dot_plain(rows_ref[...], weight_ref[...])
    for first in range(0, width, LANES):
        piece = projected[:, first : first + LANES]
        part = first // LANES % 3
        if part < 2:
            piece = piece * cos_ref[...] + partner(piece) * sin_ref[...]
        if part == 0:
            piece = piece * HEAD ** (-0.5)
        out_ref[:, first : first + LANES] = piece.astype(jnp.bfloat16)


def project(rows, weight, cosine, sine):
    count, depth = rows.shape
    width = weight.shape[1]
    block = min(ROW_BLOCK, count)
    return pl.pallas_call(
        project_kernel,
        out_shape=jax.ShapeDtypeStruct((count, width), jnp.bfloat16),
        grid=(count // block,),
        in_specs=[
            pl.BlockSpec((block, depth), lambda i: (i, 0)),
            pl.BlockSpec((depth, width), lambda i: (0, 0)),
            pl.BlockSpec((block, LANES), lambda i: (i, 0)),
            pl.BlockSpec((block, LANES), lambda i: (i, 0)),
        ],
        out_specs=pl.BlockSpec((block, width), lambda i: (i, 0)),
        cost_estimate=short,
        name="project",
    )(rows, weight, cosine, sine)


def normalize(tokens):
    residual = tokens.astype(jnp.float32)
    center = residual - jnp.mean(residual, axis=1, keepdims=True)
    inv_std = lax.rsqrt(jnp.mean(center * center, axis=1, keepdims=True) + norm_eps)
    return (center * inv_std, inv_std)


def feed_kernel(tokens_ref, params_ref, weight_ref, *refs):
    normed_ref, act_ref, slope_ref = refs[-3:]
    unit, unused = normalize(tokens_ref[...])
    normed_ref[...] = (unit * params_ref[0:1, :] + params_ref[1:2, :]).astype(jnp.bfloat16)
    width = act_ref.shape[1]
    step = min(256, width)
    for first in range(0, width, step):
        hidden = dot_plain(normed_ref[...], weight_ref[:, first : first + step])
        share = 0.5 + 0.5 * lax.erf(hidden * math.sqrt(0.5))
        bell = jnp.exp(hidden * hidden * -0.5) * (1.0 / math.sqrt(2.0 * math.pi))
        act_ref[:, first : first + step] = (hidden * share).astype(jnp.bfloat16)
        slope_ref[:, first : first + step] = share + hidden * bell


def feed(slot, slots, tokens, params, weight, held):
    rows, depth = tokens.shape
    width = weight.shape[1]
    whole = pl.BlockSpec(memory_space=pl.ANY)
    return pl.pallas_call(
        feed_kernel,
        out_shape=(
            jax.ShapeDtypeStruct((slots * rows, depth), jnp.bfloat16),
            jax.ShapeDtypeStruct((slots * rows, width), jnp.bfloat16),
            jax.ShapeDtypeStruct((slots * rows, width), jnp.float32),
        ),
        grid=(2,),
        in_specs=[
            pl.BlockSpec((rows // 2, depth), lambda i: (i, 0)),
            pl.BlockSpec((2, depth), lambda i: (0, 0)),
            pl.BlockSpec((depth, width), lambda i: (0, 0)),
        ]
        + [whole] * len(held),
        out_specs=(
            pl.BlockSpec((rows // 2, depth), lambda i: (2 * slot + i, 0)),
            pl.BlockSpec((rows // 2, width), lambda i: (2 * slot + i, 0)),
            pl.BlockSpec((rows // 2, width), lambda i: (2 * slot + i, 0)),
        ),
        input_output_aliases={3 + k: k for k in range(len(held))},
        cost_estimate=short,
        name="feed",
    )(tokens, params, weight, *held)


def push_kernel(index_ref, grad_ref, slope_ref, down_ref, merge_ref, *refs):
    all_ref, hidden_ref, attended_ref, merge_own = refs[-4:]

    @pl.when(pl.program_id(0) == 0)
    def _():
        if len(merge_ref.shape) == 4:
            for w in range(merge_ref.shape[0]):
                merge_own[:, w * LANES : (w + 1) * LANES] = merge_ref[w, 0]
        else:
            merge_own[...] = merge_ref[...]

    grads = grad_ref[...]
    all_ref[...] = grads
    hidden_ref[...] = (dot_last(grads, down_ref[...]) * slope_ref[...]).astype(jnp.bfloat16)
    attended_ref[...] = dot_last(grads, merge_own[...]).astype(jnp.bfloat16)


def push(slot, slots, grads, slope, down, merge, span_index, held):
    rows, depth = grads.shape
    width = slope.shape[1]
    half = rows // 2
    whole = pl.BlockSpec(memory_space=pl.ANY)
    if merge.ndim == 4:
        own = merge.shape[2]
        merge_spec = pl.BlockSpec(
            (merge.shape[0], 1, own, LANES), lambda i, index_ref: (0, index_ref[0], 0, 0)
        )
    else:
        own = merge.shape[0]
        merge_spec = pl.BlockSpec(merge.shape, lambda i, index_ref: (0, 0))

    def place(i, index_ref):
        return (2 * slot + i, 0)

    return pl.pallas_call(
        push_kernel,
        out_shape=(
            jax.ShapeDtypeStruct((slots * rows, depth), jnp.bfloat16),
            jax.ShapeDtypeStruct((slots * rows, width), jnp.bfloat16),
            jax.ShapeDtypeStruct((slots * rows, own), jnp.bfloat16),
        ),
        grid_spec=pltpu.PrefetchScalarGridSpec(
            num_scalar_prefetch=1,
            grid=(2,),
            in_specs=[
                pl.BlockSpec((half, depth), lambda i, index_ref: (i, 0)),
                pl.BlockSpec((half, width), place),
                pl.BlockSpec(down.shape, lambda i, index_ref: (0, 0)),
                merge_spec,
            ]
            + [whole] * len(held),
            out_specs=(
                pl.BlockSpec((half, depth), place),
                pl.BlockSpec((half, width), place),
                pl.BlockSpec((half, own), place),
            ),
            scratch_shapes=[pltpu.VMEM((own, depth), jnp.bfloat16)],
        ),
        input_output_aliases={5 + k: k for k in range(len(held))},
        cost_estimate=short,
        name="push",
    )(span_index.reshape(1), grads, slope, down, merge, *held)


def pull_kernel(mixed_ref, hidden_ref, proj_ref, up_ref, tokens_ref, out_ref, sums_ref):
    partial_grad = dot_last(mixed_ref[...], proj_ref[...]) + dot_last(hidden_ref[...], up_ref[...])
    out_ref[...] = partial_grad
    unit, unused = normalize(tokens_ref[...])
    gain = jnp.sum(partial_grad * unit, axis=0, keepdims=True)
    bias = jnp.sum(partial_grad, axis=0, keepdims=True)
    both = jnp.concatenate([gain, bias], axis=0)

    @pl.when(pl.program_id(0) == 0)
    def _():
        sums_ref[...] = both

    @pl.when(pl.program_id(0) > 0)
    def _():
        sums_ref[...] += both


def pull(slot, mixed, hidden_grad, proj, up, tokens):
    rows, depth = tokens.shape
    half = rows // 2
    return pl.pallas_call(
        pull_kernel,
        out_shape=(
            jax.ShapeDtypeStruct((rows, depth), jnp.float32),
            jax.ShapeDtypeStruct((2, depth), jnp.float32),
        ),
        grid=(2,),
        in_specs=[
            pl.BlockSpec((half, mixed.shape[1]), lambda i: (2 * slot + i, 0)),
            pl.BlockSpec((half, hidden_grad.shape[1]), lambda i: (2 * slot + i, 0)),
            pl.BlockSpec(proj.shape, lambda i: (0, 0)),
            pl.BlockSpec(up.shape, lambda i: (0, 0)),
            pl.BlockSpec((half, depth), lambda i: (i, 0)),
        ],
        out_specs=(
            pl.BlockSpec((half, depth), lambda i: (i, 0)),
            pl.BlockSpec((2, depth), lambda i: (0, 0)),
        ),
        cost_estimate=short,
        name="pull",
    )(mixed, hidden_grad, proj, up, tokens)


def project_all_kernel(index_ref, rows_ref, cos_ref, sin_ref, *refs):
    unit_refs, (out_ref, weight_ref) = refs[:-2], refs[-2:]

    @pl.when(pl.program_id(0) == 0)
    def _():
        for c, unit_ref in enumerate(unit_refs):
            weight_ref[:, c * LANES : (c + 1) * LANES] = unit_ref[...].reshape(D, LANES)

    project_kernel(rows_ref, weight_ref, cos_ref, sin_ref, out_ref)


def project_all(rows, weight_all, span_index, own_width, cosine, sine):
    count, depth = rows.shape
    shards, narrow_count, shard_rows, cols = weight_all.shape
    units = own_width // LANES
    width = 3 * own_width
    per_shard = cols // LANES
    per_part = D // LANES
    block = min(ROW_BLOCK, count)

    def source(c, i, index_ref):
        unit = (c % 3) * per_part + index_ref[0] * units + c // 3
        return (unit // per_shard, 0, 0, unit % per_shard)

    return pl.pallas_call(
        project_all_kernel,
        out_shape=(
            jax.ShapeDtypeStruct((count, width), jnp.bfloat16),
            jax.ShapeDtypeStruct((D, width), jnp.bfloat16),
        ),
        grid_spec=pltpu.PrefetchScalarGridSpec(
            num_scalar_prefetch=1,
            grid=(count // block,),
            in_specs=[
                pl.BlockSpec((block, depth), lambda i, index_ref: (i, 0)),
                pl.BlockSpec((block, LANES), lambda i, index_ref: (i, 0)),
                pl.BlockSpec((block, LANES), lambda i, index_ref: (i, 0)),
            ]
            + [
                pl.BlockSpec((1, narrow_count, shard_rows, LANES), partial(source, c))
                for c in range(3 * units)
            ],
            out_specs=(
                pl.BlockSpec((block, width), lambda i, index_ref: (i, 0)),
                pl.BlockSpec((D, width), lambda i, index_ref: (0, 0)),
            ),
        ),
        cost_estimate=short,
        name="project_all",
    )(span_index.reshape(1), rows, cosine, sine, *[weight_all] * (3 * units))


def turn_kernel(slots_ref, all_ref, out_ref):
    unused, narrow_count, rows, cols = all_ref.shape
    for t in range(narrow_count):
        out_ref[t * rows : (t + 1) * rows, :] = all_ref[0, slots_ref[t]]


def pick_merge(weight_all, slots, own_width):
    shards, narrow_count, rows, cols = weight_all.shape
    return pl.pallas_call(
        turn_kernel,
        out_shape=jax.ShapeDtypeStruct((D, D), jnp.bfloat16),
        grid_spec=pltpu.PrefetchScalarGridSpec(
            num_scalar_prefetch=1,
            grid=(shards,),
            in_specs=[
                pl.BlockSpec(
                    (1, narrow_count, rows, LANES),
                    lambda j, slots_ref: (j, 0, 0, 0),
                )
            ],
            out_specs=pl.BlockSpec((D, LANES), lambda j, slots_ref: (0, j)),
        ),
        cost_estimate=short,
        name="pick_merge",
    )(slots, weight_all)


def head_lanes(field, head):
    lane = lax.broadcasted_iota(jnp.int32, field.shape, 1)
    keep = (lane >= head * HEAD) & (lane < (head + 1) * HEAD)
    return jnp.where(keep, field, jnp.zeros_like(field))


def pair_allowed(start_row, key_first, key_count, query_first, query_count):
    key_index = key_first + lax.broadcasted_iota(jnp.int32, (key_count, query_count), 0)
    query_index = query_first + lax.broadcasted_iota(jnp.int32, (key_count, query_count), 1)
    return (key_index >= start_row) & (key_index <= query_index)


def attend_kernel(
    block_q,
    block_k,
    heads_in,
    slots_ref,
    first_ref,
    last_ref,
    start_ref,
    query_ref,
    key_ref,
    value_ref,
    *refs,
):
    out_ref, tall_ref, log_ref, turned, best, total, summed = refs[-7:]
    index = pl.program_id(0)
    key_blocks = key_ref.shape[0] // block_k

    @pl.when(index == 0)
    def _():
        for j in range(key_blocks):
            piece = value_ref[j * block_k : (j + 1) * block_k, :].astype(jnp.float32)
            turned[:, j * block_k : (j + 1) * block_k] = piece.T.astype(jnp.bfloat16)

    query_first = index * block_q
    low = first_ref[index] // block_k
    high = (query_first + block_q - 1) // block_k + 1
    start_row = start_ref[...]
    queries = [head_lanes(query_ref[...], head) for head in range(heads_in)]
    best[...] = jnp.full_like(best, masked_score)
    total[...] = jnp.zeros_like(total)
    summed[...] = jnp.zeros_like(summed)

    def visit(j, masked):
        key_rows = pl.ds(pl.multiple_of(slots_ref[j] * block_k, block_k), block_k)
        keys = key_ref[key_rows, :]
        if masked:
            allowed = pair_allowed(start_row, j * block_k, block_k, query_first, block_q)
        for head in range(heads_in):
            scores = dot_last(keys, queries[head])
            if masked:
                scores = jnp.where(allowed, scores, masked_score)
            old = best[head : head + 1, :]
            new = jnp.maximum(old, jnp.max(scores, axis=0, keepdims=True))
            weights = jnp.exp(scores - new)
            if masked:
                weights = jnp.where(allowed, weights, 0.0)
            factor = jnp.exp(old - new)
            best[head : head + 1, :] = new
            total[head : head + 1, :] = total[head : head + 1, :] * factor + jnp.sum(
                weights, axis=0, keepdims=True
            )
            rows = slice(head * HEAD, (head + 1) * HEAD)
            summed[rows, :] = summed[rows, :] * factor + dot_plain(
                turned[rows, key_rows], weights.astype(jnp.bfloat16)
            )

    def step(j, carry):
        whole = (j * block_k >= last_ref[index]) & ((j + 1) * block_k - 1 <= query_first)

        @pl.when(whole)
        def _():
            visit(j, False)

        @pl.when(jnp.logical_not(whole))
        def _():
            visit(j, True)

        return carry

    lax.fori_loop(low, high, step, 0)
    for head in range(heads_in):
        rows = slice(head * HEAD, (head + 1) * HEAD)
        weight = total[head : head + 1, :]
        tall_ref[rows, :] = summed[rows, :] / weight
        log_ref[0, head : head + 1, :] = best[head : head + 1, :] + jnp.log(weight)
    if heads_in * HEAD < LANES:
        tall_ref[heads_in * HEAD :, :] = jnp.zeros_like(tall_ref[heads_in * HEAD :, :])
    log_ref[0, heads_in:, :] = jnp.zeros_like(log_ref[0, heads_in:, :])
    out_ref[...] = tall_ref[...].T.astype(jnp.bfloat16)


def attend(pair, packed, slots, first, last, starts, heads_in, block_q, block_k, held):
    count, width = packed.shape
    pairs = width // 3 // LANES
    whole = pl.BlockSpec(memory_space=pl.ANY)
    return pl.pallas_call(
        partial(attend_kernel, block_q, block_k, heads_in),
        out_shape=(
            jax.ShapeDtypeStruct((count, pairs * LANES), jnp.bfloat16),
            jax.ShapeDtypeStruct((pairs * LANES, count), jnp.float32),
            jax.ShapeDtypeStruct((pairs, 8, count), jnp.float32),
        ),
        grid_spec=pltpu.PrefetchScalarGridSpec(
            num_scalar_prefetch=3,
            grid=(count // block_q,),
            in_specs=[
                pl.BlockSpec((1, block_q), lambda i, slots_ref, *_: (0, slots_ref[i])),
                pl.BlockSpec((block_q, LANES), lambda i, slots_ref, *_: (slots_ref[i], 3 * pair)),
                pl.BlockSpec((count, LANES), lambda i, *_: (0, 3 * pair + 1)),
                pl.BlockSpec((count, LANES), lambda i, *_: (0, 3 * pair + 2)),
            ]
            + [whole] * len(held),
            out_specs=(
                pl.BlockSpec((block_q, LANES), lambda i, slots_ref, *_: (slots_ref[i], pair)),
                pl.BlockSpec((LANES, block_q), lambda i, slots_ref, *_: (pair, slots_ref[i])),
                pl.BlockSpec((1, 8, block_q), lambda i, slots_ref, *_: (pair, 0, slots_ref[i])),
            ),
            scratch_shapes=[
                pltpu.VMEM((LANES, count), jnp.bfloat16),
                pltpu.VMEM((8, block_q), jnp.float32),
                pltpu.VMEM((8, block_q), jnp.float32),
                pltpu.VMEM((LANES, block_q), jnp.float32),
            ],
        ),
        input_output_aliases={7 + k: k for k in range(len(held))},
        cost_estimate=short,
        name="attend",
    )(slots, first, last, starts.reshape(1, count), packed, packed, packed, *held)


def attend_back_kernel(
    block_q,
    block_k,
    heads_in,
    slots_ref,
    last_ref,
    end_ref,
    start_ref,
    cos_ref,
    sin_ref,
    query_ref,
    key_ref,
    value_ref,
    tall_ref,
    log_ref,
    grad_ref,
    out_ref,
    turned,
    masked_q,
    masked_g,
    delta,
    tall_q,
    key_sum,
    value_sum,
):
    index = pl.program_id(1)
    count = query_ref.shape[0]

    def turn_back(field, rows):
        return field * cos_ref[rows, :] - partner(field) * sin_ref[rows, :]

    @pl.when(index == 0)
    def _():
        def prepare(j, carry):
            rows = pl.ds(pl.multiple_of(j * block_k, block_k), block_k)
            turned[:, rows] = key_ref[rows, :].astype(jnp.float32).T.astype(jnp.bfloat16)
            grads = grad_ref[rows, :]
            product = grads.astype(jnp.float32).T * tall_ref[:, rows]
            for head in range(heads_in):
                masked_q[head, rows, :] = head_lanes(query_ref[rows, :], head)
                masked_g[head, rows, :] = head_lanes(grads, head)
                delta[head : head + 1, rows] = jnp.sum(
                    product[head * HEAD : (head + 1) * HEAD, :], axis=0, keepdims=True
                )
            tall_q[:, rows] = jnp.zeros((LANES, block_k), jnp.float32)
            return carry

        lax.fori_loop(0, count // block_k, prepare, 0)

    key_first = index * block_k
    key_rows = pl.ds(pl.multiple_of(slots_ref[index] * block_k, block_k), block_k)
    keys = key_ref[key_rows, :]
    values = value_ref[key_rows, :]
    key_sum[...] = jnp.zeros_like(key_sum)
    value_sum[...] = jnp.zeros_like(value_sum)

    def visit(i, masked):
        query_first = i * block_q
        rows = pl.ds(pl.multiple_of(slots_ref[i] * block_q, block_q), block_q)
        if masked:
            allowed = pair_allowed(
                start_ref[0:1, rows], key_first, block_k, query_first, block_q
            )
        for head in range(heads_in):
            queries = masked_q[head, rows, :]
            grads = masked_g[head, rows, :]
            scores = dot_last(keys, queries)
            probs = jnp.exp(scores - log_ref[0, head : head + 1, rows])
            if masked:
                probs = jnp.where(allowed, probs, 0.0)
            value_sum[...] += dot_plain(probs.astype(jnp.bfloat16), grads)
            prob_grad = dot_last(values, grads)
            score_grad = (probs * (prob_grad - delta[head : head + 1, rows])).astype(jnp.bfloat16)
            key_sum[...] += dot_plain(score_grad, queries)
            lanes = slice(head * HEAD, (head + 1) * HEAD)
            tall_q[lanes, rows] += dot_plain(turned[lanes, key_rows], score_grad)

    def step(i, carry):
        whole = (key_first >= last_ref[i]) & (key_first + block_k - 1 <= i * block_q)

        @pl.when(whole)
        def _():
            visit(i, False)

        @pl.when(jnp.logical_not(whole))
        def _():
            visit(i, True)

        return carry

    lax.fori_loop(key_first // block_q, (end_ref[index] - 1) // block_q + 1, step, 0)
    out_ref[key_rows, LANES : 2 * LANES] = turn_back(key_sum[...], key_rows).astype(jnp.bfloat16)
    out_ref[key_rows, 2 * LANES :] = value_sum[...].astype(jnp.bfloat16)

    @pl.when(index == pl.num_programs(1) - 1)
    def _():
        def finish(j, carry):
            rows = pl.ds(pl.multiple_of(j * block_k, block_k), block_k)
            field = tall_q[:, rows].T * HEAD ** (-0.5)
            out_ref[rows, :LANES] = turn_back(field, rows).astype(jnp.bfloat16)
            return carry

        lax.fori_loop(0, count // block_k, finish, 0)


def attend_back(
    packed, slots, last, end, starts, cosine, sine, tall, logs, grads, heads_in, block_q, block_k
):
    count, width = packed.shape
    pairs = width // 3 // LANES
    return pl.pallas_call(
        partial(attend_back_kernel, block_q, block_k, heads_in),
        out_shape=jax.ShapeDtypeStruct((count, width), jnp.bfloat16),
        grid_spec=pltpu.PrefetchScalarGridSpec(
            num_scalar_prefetch=3,
            grid=(pairs, count // block_k),
            in_specs=[
                pl.BlockSpec((1, count), lambda p, i, *_: (0, 0)),
                pl.BlockSpec((count, LANES), lambda p, i, *_: (0, 0)),
                pl.BlockSpec((count, LANES), lambda p, i, *_: (0, 0)),
                pl.BlockSpec((count, LANES), lambda p, i, *_: (0, 3 * p)),
                pl.BlockSpec((count, LANES), lambda p, i, *_: (0, 3 * p + 1)),
                pl.BlockSpec((count, LANES), lambda p, i, *_: (0, 3 * p + 2)),
                pl.BlockSpec((LANES, count), lambda p, i, *_: (p, 0)),
                pl.BlockSpec((1, 8, count), lambda p, i, *_: (p, 0, 0)),
                pl.BlockSpec((count, LANES), lambda p, i, *_: (0, p)),
            ],
            out_specs=pl.BlockSpec((count, 3 * LANES), lambda p, i, *_: (0, p)),
            scratch_shapes=[
                pltpu.VMEM((LANES, count), jnp.bfloat16),
                pltpu.VMEM((heads_in, count, LANES), jnp.bfloat16),
                pltpu.VMEM((heads_in, count, LANES), jnp.bfloat16),
                pltpu.VMEM((8, count), jnp.float32),
                pltpu.VMEM((LANES, count), jnp.float32),
                pltpu.VMEM((block_k, LANES), jnp.float32),
                pltpu.VMEM((block_k, LANES), jnp.float32),
            ],
        ),
        compiler_params=pltpu.CompilerParams(vmem_limit_bytes=60 << 20),
        cost_estimate=short,
        name="attend_back",
    )(
        slots, last, end, starts.reshape(1, count), cosine, sine,
        packed, packed, packed, tall, logs, grads,
    )


def finish_kernel(narrow_count, wide_count, own_units, per_shard, entries, *refs):
    exchange = own_units > 0
    if exchange:
        (
            parts_ref, piece_ref, feed_ref, total_ref, stats_ref, block_ref, mine, near, far, near_sum,
            send_near, recv_near, send_far, recv_far, send_piece, recv_piece,
        ) = refs
    else:
        (
            parts_ref, piece_ref, feed_ref, total_ref, stats_ref, mine, near, far, near_sum,
            send_near, recv_near, send_far, recv_far,
        ) = refs
    narrow_me = lax.axis_index("narrow")
    wide_me = lax.axis_index("wide")

    def place(narrow_at, wide_at):
        return {"narrow": narrow_at, "wide": wide_at}

    def square_sum(value):
        value = value.astype(jnp.float32)
        return jnp.sum(
            jnp.sum(value * value, axis=0, keepdims=True), axis=1, keepdims=True
        )

    norm_rows = 2 * D // LANES
    row_at = lax.broadcasted_iota(jnp.int32, mine.shape, 0)
    lane_at = lax.broadcasted_iota(jnp.int32, mine.shape, 1)
    mine[...] = parts_ref[...] + jnp.where(
        (row_at == norm_rows) & (lane_at == 0),
        square_sum(piece_ref[...]) + square_sum(feed_ref[...]),
        0.0,
    )
    mesh_ids = pl.DeviceIdType.MESH
    barrier = pltpu.get_barrier_semaphore()
    greeted = 0
    for ahead in range(narrow_count):
        for across in range(wide_count):
            if (ahead > 0) + (across > 0) == 0 or (not exchange and ahead > 0 and across > 0):
                continue
            greeted += 1
            pl.semaphore_signal(
                barrier,
                inc=1,
                device_id=place(
                    lax.rem(narrow_me + ahead, narrow_count), lax.rem(wide_me + across, wide_count)
                ),
                device_id_type=mesh_ids,
            )
    pl.semaphore_wait(barrier, greeted)
    near_copies = []
    for ahead in range(1, narrow_count):
        copy = pltpu.make_async_remote_copy(
            src_ref=mine,
            dst_ref=near.at[narrow_me],
            send_sem=send_near.at[ahead - 1],
            recv_sem=recv_near.at[ahead - 1],
            device_id=place(lax.rem(narrow_me + ahead, narrow_count), wide_me),
            device_id_type=mesh_ids,
        )
        copy.start()
        near_copies.append(copy)
    near[narrow_me] = mine[...]
    if exchange:
        rows = piece_ref.shape[0]
        halves = block_ref.shape[0] // rows
        half_me = lax.rem(wide_me, halves)
        narrow_to = lax.div(wide_me, halves)
        moves = []
        for unit in range(3 * own_units):
            whole_unit = (unit % 3) * (D // LANES) + narrow_me * own_units + unit // 3
            wide_to = lax.div(whole_unit, per_shard)
            column = lax.rem(whole_unit, per_shard)
            source = piece_ref.at[:, unit * LANES : (unit + 1) * LANES]
            target = block_ref.at[
                pl.ds(pl.multiple_of(half_me * rows, rows), rows),
                pl.ds(pl.multiple_of(column * LANES, LANES), LANES),
            ]
            arrived = recv_piece.at[half_me * per_shard + column]
            remote = pltpu.make_async_remote_copy(
                src_ref=source,
                dst_ref=target,
                send_sem=send_piece.at[unit],
                recv_sem=arrived,
                device_id=place(narrow_to, wide_to),
                device_id_type=mesh_ids,
            )
            here = pltpu.make_async_copy(source, target, arrived)
            stays = (narrow_to == narrow_me) & (wide_to == wide_me)
            pl.when(jnp.logical_not(stays))(remote.start)
            pl.when(stays)(here.start)
            moves.append((stays, remote))
    for copy in near_copies:
        copy.wait()
    value = near[0]
    for k in range(1, narrow_count):
        value = value + near[k]
    near_sum[...] = value
    far_copies = []
    for across in range(1, wide_count):
        copy = pltpu.make_async_remote_copy(
            src_ref=near_sum,
            dst_ref=far.at[wide_me],
            send_sem=send_far.at[across - 1],
            recv_sem=recv_far.at[across - 1],
            device_id=place(narrow_me, lax.rem(wide_me + across, wide_count)),
            device_id_type=mesh_ids,
        )
        copy.start()
        far_copies.append(copy)
    far[wide_me] = value
    for copy in far_copies:
        copy.wait()
    value = far[0]
    for k in range(1, wide_count):
        value = value + far[k]
    total_ref[...] = value
    grad_norm = jnp.sqrt(square_sum(value[:norm_rows]) + value[norm_rows : norm_rows + 1, 0:1])
    stats = [jnp.minimum(1.0, math.sqrt(NPARAMS) / grad_norm), grad_norm] + [
        jnp.sqrt(value[norm_rows : norm_rows + 1, k : k + 1] / entries) for k in (1, 2, 3)
    ]
    stats_ref[...] = jnp.zeros_like(stats_ref)
    for row, stat in enumerate(stats):
        stats_ref[row : row + 1, :] = jnp.broadcast_to(stat, (1, LANES))
    if exchange:
        for stays, remote in moves:
            pl.when(jnp.logical_not(stays))(remote.wait_send)
        for half in range(halves):
            for column in range(per_shard):
                pltpu.make_async_copy(
                    piece_ref.at[:, 0:LANES],
                    block_ref.at[
                        half * rows : (half + 1) * rows, column * LANES : (column + 1) * LANES
                    ],
                    recv_piece.at[half * per_shard + column],
                ).wait()


def finish(
    parts, piece, feed_piece, exchange, narrow_count, wide_count, own_width, proj_cols, entries
):
    shape = parts.shape
    own_units = own_width // LANES if exchange else 0
    per_shard = proj_cols // LANES
    vmem = pl.BlockSpec(memory_space=pltpu.VMEM)
    shapes = [
        jax.ShapeDtypeStruct(shape, jnp.float32),
        jax.ShapeDtypeStruct((8, LANES), jnp.float32),
    ]
    scratch = [
        pltpu.VMEM(shape, jnp.float32),
        pltpu.VMEM((narrow_count,) + shape, jnp.float32),
        pltpu.VMEM((wide_count,) + shape, jnp.float32),
        pltpu.VMEM(shape, jnp.float32),
        pltpu.SemaphoreType.DMA((narrow_count - 1,)),
        pltpu.SemaphoreType.DMA((narrow_count - 1,)),
        pltpu.SemaphoreType.DMA((wide_count - 1,)),
        pltpu.SemaphoreType.DMA((wide_count - 1,)),
    ]
    if exchange:
        shapes.append(jax.ShapeDtypeStruct((D // narrow_count, proj_cols), jnp.bfloat16))
        scratch += [
            pltpu.SemaphoreType.DMA((3 * own_units,)),
            pltpu.SemaphoreType.DMA((3 * own_units,)),
        ]
    return pl.pallas_call(
        partial(finish_kernel, narrow_count, wide_count, own_units, per_shard, entries),
        out_shape=tuple(shapes),
        in_specs=[vmem] * 3,
        out_specs=(vmem,) * len(shapes),
        scratch_shapes=scratch,
        compiler_params=pltpu.CompilerParams(collective_id=0, has_side_effects=True),
        name="finish",
    )(parts, piece, feed_piece)


def adam_update(
    weight, first_moment, second_moment, grad_value, step_rate, decay_coef, first_fix, second_fix
):
    new_first = beta_first * first_moment + (1.0 - beta_first) * grad_value
    new_second = beta_second * second_moment + (1.0 - beta_second) * grad_value * grad_value
    step_ratio = new_first / first_fix / (jnp.sqrt(new_second / second_fix) + adam_eps)
    return (weight - step_rate * (step_ratio + decay_coef * weight), new_first, new_second)


def adam_step(weight, first_moment, second_moment, gradient, step_rate, decay_coef, scales):
    new_first = beta_first * first_moment + (1.0 - beta_first) * gradient
    new_second = beta_second * second_moment + (1.0 - beta_second) * gradient * gradient
    ratio = new_first * scales[0] / (jnp.sqrt(new_second * scales[1]) + adam_eps)
    return (weight - step_rate * (ratio + decay_coef * weight), new_first, new_second)


def adam_kernel(scale_ref, stats_ref, grads_ref, total_ref, proj_ref, merge_ref, *refs):
    states, outs = refs[:15], refs[15:-1]
    norm_grads = refs[-1]
    matrix_step, norm_step = scale_ref[0, 0], scale_ref[0, 1]
    scales = (scale_ref[0, 2], scale_ref[0, 3])
    clip_factor = stats_ref[0:1, 0:1]

    def update(matrix, gradient, step_rate, decay_coef):
        state = [ref[...] for ref in states[3 * matrix : 3 * matrix + 3]]
        new = adam_step(*state, gradient * clip_factor, step_rate, decay_coef, scales)
        for out_ref, value in zip(outs[4 * matrix : 4 * matrix + 3], new):
            out_ref[...] = value
        return new[0]

    for matrix in range(2):
        gradient = grads_ref[0, matrix].astype(jnp.float32)
        weight = update(matrix, gradient, matrix_step, decay_rate)
        outs[4 * matrix + 3][...] = weight.astype(jnp.bfloat16)

    @pl.when(pl.program_id(0) == 0)
    def _():
        for matrix, gradient in (
            (2, proj_ref[...].astype(jnp.float32)),
            (3, merge_ref[...].astype(jnp.float32).T),
        ):
            weight = update(matrix, gradient, matrix_step, decay_rate)
            outs[4 * matrix + 3][...] = weight.astype(jnp.bfloat16)
        per_row = D // LANES
        for k in range(2 * per_row):
            at = k % per_row
            norm_grads[k // per_row : k // per_row + 1, at * LANES : (at + 1) * LANES] = total_ref[
                k : k + 1, :
            ]
        update(4, norm_grads[...], norm_step, 0.0)
        outs[19][...] = norm_grads[...] * clip_factor


def adam_all(scales, stats, grads_all, total, proj_block, heads_part, own_width, states):
    count, matrices, rows, cols = grads_all.shape
    block = pl.BlockSpec((rows, cols), lambda i: (i, 0))

    def same(array):
        return pl.BlockSpec(array.shape, lambda i: (0, 0))

    feed_out = jax.ShapeDtypeStruct((count * rows, cols), jnp.float32)
    feed_copy = jax.ShapeDtypeStruct((count * rows, cols), jnp.bfloat16)
    shapes = [feed_out, feed_out, feed_out, feed_copy] * 2
    specs = [block] * 8
    for state in states[6::3]:
        full = jax.ShapeDtypeStruct(state.shape, jnp.float32)
        copy = jax.ShapeDtypeStruct(
            state.shape, jnp.float32 if state is states[12] else jnp.bfloat16
        )
        shapes += [full, full, full, copy]
        specs += [same(state)] * 4
    return pl.pallas_call(
        adam_kernel,
        out_shape=tuple(shapes),
        grid=(count,),
        in_specs=[
            pl.BlockSpec(memory_space=pltpu.SMEM),
            same(stats),
            pl.BlockSpec((1, matrices, rows, cols), lambda i: (i, 0, 0, 0)),
            same(total),
            same(proj_block),
            pl.BlockSpec((heads_part.shape[0], own_width), lambda i: (0, 3)),
        ]
        + [block] * 6
        + [same(state) for state in states[6:]],
        out_specs=tuple(specs),
        scratch_shapes=[pltpu.VMEM((2, D), jnp.float32)],
        cost_estimate=short,
        name="adam_all",
    )(scales, stats, grads_all, total, proj_block, heads_part, *states)


def shards(
    tokens,
    cotangent,
    seq_lengths,
    step_count,
    norm_params,
    norm_first,
    norm_second,
    proj_weight,
    proj_first,
    proj_second,
    merge_weight,
    merge_first,
    merge_second,
    up_weight,
    up_first,
    up_second,
    down_weight,
    down_first,
    down_second,
):
    tok_rows = tokens.shape[0]
    narrow_count = lax.axis_size("narrow")
    wide_count = lax.axis_size("wide")
    span_index = lax.axis_index("narrow")
    group_rows = tok_rows * narrow_count
    own_width = HEADS // narrow_count * HEAD
    held_width = max(own_width, LANES)
    heads_in = min(own_width, LANES) // HEAD
    shard_rows = D // narrow_count
    proj_cols = proj_weight.shape[1]
    lengths = seq_lengths[0]
    onward = [(i, (i + 1) % narrow_count) for i in range(narrow_count)]
    slots = lax.rem(
        span_index + narrow_count - jnp.arange(narrow_count, dtype=jnp.int32), narrow_count
    )

    def pad_lanes(array, axis):
        extra = [(0, 0)] * array.ndim
        extra[axis] = (0, held_width - own_width)
        return jnp.pad(array, extra) if held_width > own_width else array

    def meet(*values):
        return lax.optimization_barrier(values)

    def send_on(array):
        return lax.ppermute(array, "narrow", onward)

    def rows_of(array, slot):
        return array[slot * tok_rows : (slot + 1) * tok_rows]

    direct = own_width % LANES == 0 and proj_cols % LANES == 0 and merge_weight.shape[1] == LANES
    weight_part = jnp.concatenate(
        [proj_weight.astype(jnp.bfloat16), merge_weight.astype(jnp.bfloat16)], axis=1
    )
    weight_rows = lax.all_gather(weight_part, "narrow", axis=0, tiled=True)
    up_slice = up_weight.astype(jnp.bfloat16)
    down_slice = down_weight.astype(jnp.bfloat16)

    def wide_all(array):
        return lax.all_gather(array, "wide", axis=0).reshape(
            wide_count, narrow_count, shard_rows, -1
        )

    def down_term(rows, slot):
        return dot_plain(rows_of(rows, slot), down_slice)

    order = list(range(1, narrow_count)) + [0]
    pairs = held_width // LANES
    token_blocks = [tokens]
    held = ()
    for slot in range(narrow_count - 1):
        moving = send_on(token_blocks[slot])
        held = feed(slot, narrow_count, token_blocks[slot], norm_params, up_slice, held)
        if slot != 2:
            moving, held = meet(moving, held)
        if slot == 0:
            lengths, slots, moving, weight_rows = meet(lengths, slots, moving, weight_rows)
            proj_all = wide_all(weight_rows[:, :proj_cols])
            merge_all = wide_all(weight_rows[:, proj_cols:])
        if slot == 1:
            places = (
                slots[:, None] * tok_rows + jnp.arange(tok_rows, dtype=jnp.int32)[None, :]
            ).reshape(group_rows)
            seq_start, unused = locate(lengths, places)
            cosine, sine = rotary_tables(places - seq_start)
            block_first = jnp.arange(narrow_count, dtype=jnp.int32) * tok_rows
            first_start, unused = locate(lengths, block_first)
            last_start, last_end = locate(lengths, block_first + (tok_rows - 1))
            moving, cosine, sine, first_start, last_start, last_end = meet(
                moving, cosine, sine, first_start, last_start, last_end
            )
        elif slot == 2:
            first_term = down_term(held[1], 1).astype(jnp.bfloat16)
            next_term = down_term(held[1], order[1])
            moving, held, down_slice, first_term, next_term = meet(
                moving, held, down_slice, first_term, next_term
            )
        token_blocks.append(moving)
    grad_first, last_block = meet(cotangent, token_blocks[-1])
    token_blocks[-1] = last_block
    grad_blocks = [grad_first]

    moving = send_on(grad_first)
    gathered, activated, slope = feed(
        narrow_count - 1, narrow_count, last_block, norm_params, up_slice, held
    )
    if direct:
        packed, proj_own = project_all(
            gathered, proj_all, span_index, own_width, cosine, sine
        )
        merge_own = merge_all
    else:
        proj_copy = jnp.transpose(proj_all, (1, 2, 0, 3)).reshape(
            D, 3, narrow_count, own_width
        )
        proj_own = pad_lanes(
            lax.dynamic_index_in_dim(proj_copy, span_index, axis=2, keepdims=False), 2
        ).reshape(D, 3 * held_width)
        merge_copy = jnp.transpose(merge_all, (1, 2, 0, 3)).reshape(
            narrow_count, own_width, D
        )
        merge_own = pad_lanes(
            lax.dynamic_index_in_dim(merge_copy, span_index, axis=0, keepdims=False), 0
        )
        packed = project(gathered, proj_own, cosine, sine)

    def push_slot(slot, push_held):
        return push(
            slot, narrow_count, grad_blocks[slot], slope, down_slice, merge_own, span_index,
            push_held,
        )

    push_held = push_slot(0, ())
    moving, packed, activated, slope, push_held = meet(
        moving, packed, activated, slope, push_held
    )
    grad_blocks.append(moving)

    def wide_sum(grad):
        return lax.psum_scatter(grad, "wide", scatter_dimension=0, tiled=True)

    def attend_pair(pair, attended_held):
        return attend(
            pair, packed, slots, first_start, last_start, seq_start,
            heads_in, tok_rows, tok_rows, attended_held,
        )

    attended_held = ()
    for hop in range(2, narrow_count):
        moving = send_on(grad_blocks[-1])
        if hop - 2 < pairs:
            attended_held = attend_pair(hop - 2, attended_held)
        push_held = push_slot(hop - 1, push_held)
        moving, attended_held, push_held = meet(moving, attended_held, push_held)
        grad_blocks.append(moving)
    for pair in range(narrow_count - 2, pairs):
        attended_held = attend_pair(pair, attended_held)
    attended, tall, logs = attended_held

    moving = send_on(first_term)
    push_held = push_slot(narrow_count - 1, push_held)
    grads_all, hidden_grad, attended_grad = push_held
    part_rows = D // wide_count
    down_grad = dot_first(activated, grads_all).astype(jnp.bfloat16)
    up_grad = dot_first(gathered, hidden_grad).astype(jnp.bfloat16)
    pieces = [
        rows_of(attended, (narrow_count - ahead) % narrow_count)[:, :own_width]
        for ahead in range(narrow_count)
    ]
    moving, pieces, up_grad, down_grad, attended_grad = meet(
        moving, pieces, up_grad, down_grad, attended_grad
    )
    feed_grad = jnp.concatenate(
        [
            up_grad.reshape(wide_count, part_rows, -1),
            down_grad.reshape(wide_count, part_rows, -1),
        ],
        axis=1,
    ).reshape(2 * D, -1)
    feed_part = wide_sum(feed_grad)

    def heads_back():
        mixed = attend_back(
            packed, slots, last_start, last_end, seq_start, cosine, sine,
            tall, logs, attended_grad, heads_in, tok_rows, tok_rows,
        )
        proj_grad = dot_first(gathered, mixed).astype(jnp.bfloat16)
        merge_grad = dot_first(grads_all, attended).astype(jnp.bfloat16)
        if not direct:
            proj_grad = proj_grad.reshape(D, 3, held_width)[:, :, :own_width].reshape(D, -1)
            merge_grad = merge_grad[:, :own_width]
        return (mixed, proj_grad, merge_grad)

    for ahead in range(1, narrow_count):
        pieces[ahead] = lax.ppermute(
            pieces[ahead],
            "narrow",
            [(i, (i + ahead) % narrow_count) for i in range(narrow_count)],
        )
    terms = []
    norm_part = jnp.zeros((2, D), jnp.float32)

    def pull_more(count, mixed, norm_part):
        for slot in order[len(terms) : len(terms) + count]:
            term, sums = pull(slot, mixed, hidden_grad, proj_own, up_slice, token_blocks[slot])
            terms.append(term)
            norm_part = norm_part + sums
        return norm_part

    for place, slot in enumerate(order[1:-1]):
        moving = send_on((moving.astype(jnp.float32) + next_term).astype(jnp.bfloat16))
        next_term = down_term(activated, order[place + 2])
        if place == 0:
            mixed_grad, *heads_grads = heads_back()
            moving, pieces, mixed_grad, heads_grads, next_term, feed_part = meet(
                moving, pieces, mixed_grad, heads_grads, next_term, feed_part
            )
            feed_all = lax.all_gather(feed_part, "wide", axis=0).reshape(
                wide_count, 2, part_rows, -1
            )
            heads_part = wide_sum(jnp.concatenate(heads_grads, axis=1))
        else:
            norm_part = pull_more(3, mixed_grad, norm_part)
            moving, terms, norm_part, next_term = meet(moving, terms, norm_part, next_term)
        if slot == narrow_count - 1:
            moving, merge_all, slots = meet(moving, merge_all, slots)
    norm_part = pull_more(narrow_count, mixed_grad, norm_part)
    branch_moving = moving
    moving = send_on(terms[0].astype(jnp.bfloat16))
    branch = branch_moving.astype(jnp.float32) + next_term
    if direct:
        merge_turn = pick_merge(merge_all, slots, own_width)
    else:
        merge_turn = jnp.take(
            jnp.transpose(merge_all, (1, 2, 0, 3)).reshape(narrow_count, own_width, D),
            slots,
            axis=0,
        ).reshape(D, D)
    merged = dot_plain(jnp.concatenate(pieces, axis=1), merge_turn)
    unit_rows, inv_std = normalize(tokens)
    output_rows = tokens.astype(jnp.float32) + merged + branch
    layer_out = output_rows.astype(jnp.bfloat16)

    def squares(array):
        value = array.astype(jnp.float32)
        return jnp.sum(value * value)

    row_squares = [squares(output_rows), squares(merged), squares(branch)]
    scalars = jnp.stack([jnp.zeros((), jnp.float32)] + row_squares)
    parts = jnp.concatenate(
        [norm_part.reshape(2 * D // LANES, LANES), jnp.pad(scalars, (0, LANES - 4))[None, :]]
    )
    parts = jnp.pad(parts, ((0, 7), (0, 0)))
    step_value = step_count[0].astype(jnp.float32)
    first_fix = 1.0 - jnp.power(beta_first, step_value)
    second_fix = 1.0 - jnp.power(beta_second, step_value)
    ramp = jnp.minimum(1.0, step_value / warmup_steps)
    scales = jnp.stack(
        [matrix_rate * ramp, norm_rate * ramp, 1.0 / first_fix, 1.0 / second_fix]
    ).reshape(1, 4)
    entries = wide_count * group_rows * D
    for place in range(1, narrow_count - 1):
        last = place == narrow_count - 2
        if last:
            moving, parts, heads_part, scales = meet(moving, parts, heads_part, scales)
        sent = (moving.astype(jnp.float32) + terms[place]).astype(jnp.bfloat16)
        if last:
            sent, parts = meet(sent, parts)
            summed = finish(
                parts, heads_part, feed_part, direct, narrow_count, wide_count, own_width,
                proj_cols, entries,
            )
            sent, summed = meet(sent, summed)
        moving = send_on(sent)

    stats = summed[1]
    if direct:
        total, stats, proj_block = summed
        updated = adam_all(
            scales, stats, feed_all, total, proj_block, heads_part, own_width,
            [
                up_weight, up_first, up_second, down_weight, down_first, down_second,
                proj_weight, proj_first, proj_second, merge_weight, merge_first, merge_second,
                norm_params, norm_first, norm_second,
            ],
        )
    else:
        total, stats = summed
        clip_factor = stats[0, 0:1]
        cross = lax.all_gather(heads_part[:, : 3 * own_width], "narrow", axis=0).reshape(
            narrow_count, part_rows, 3, own_width
        )
        cross = jnp.transpose(cross, (1, 2, 0, 3)).reshape(part_rows, wide_count, proj_cols)
        cross = lax.all_to_all(jnp.transpose(cross, (1, 0, 2)), "wide", 0, 0)
        proj_block = lax.dynamic_slice_in_dim(
            cross.reshape(D, proj_cols), span_index * shard_rows, shard_rows, axis=0
        )
        merge_block = heads_part[:, 3 * own_width :].T
        norm_total = total[: 2 * D // LANES].reshape(2, D)
        feed_sums = feed_all.astype(jnp.float32)
        updated = []
        for state, gradient, step_rate, decay_coef in (
            ((up_weight, up_first, up_second), feed_sums[:, 0], matrix_rate, decay_rate),
            ((down_weight, down_first, down_second), feed_sums[:, 1], matrix_rate, decay_rate),
            ((proj_weight, proj_first, proj_second), proj_block, matrix_rate, decay_rate),
            ((merge_weight, merge_first, merge_second), merge_block, matrix_rate, decay_rate),
            ((norm_params, norm_first, norm_second), norm_total, norm_rate, 0.0),
        ):
            clipped = gradient.reshape(state[0].shape).astype(jnp.float32) * clip_factor
            new = adam_update(
                *state, clipped, step_rate * ramp, decay_coef, first_fix, second_fix
            )
            updated += [*new, clipped if state[0] is norm_params else new[0].astype(jnp.bfloat16)]
    new_up, new_down, new_proj, new_merge, new_norm = [
        updated[4 * k : 4 * k + 4] for k in range(5)
    ]
    moving, new_up = meet(moving, new_up)
    normed_grad = moving.astype(jnp.float32) + terms[-1]
    unit_grad = normed_grad * norm_params[0]
    input_grad = cotangent.astype(jnp.float32) + inv_std * (
        unit_grad
        - jnp.mean(unit_grad, axis=1, keepdims=True)
        - unit_rows * jnp.mean(unit_grad * unit_rows, axis=1, keepdims=True)
    )
    return (
        layer_out,
        input_grad,
        stats[1, 0:1],
        stats[2, 0:1],
        new_norm[3],
        new_norm[0],
        new_norm[1],
        new_norm[2],
        new_proj[0],
        new_proj[1],
        new_proj[2],
        new_merge[0],
        new_merge[1],
        new_merge[2],
        new_up[0],
        new_up[1],
        new_up[2],
        new_down[0],
        new_down[1],
        new_down[2],
        stats[3:5, 0],
        new_proj[3],
        new_merge[3],
        new_up[3],
        new_down[3],
    )


def solution(mesh):
    placed = (
        P(("wide", "narrow"), None),
        P(("wide", "narrow"), None),
        P("wide", None),
        P(),
        P(),
        P(),
        P(),
        P("narrow", "wide"),
        P("narrow", "wide"),
        P("narrow", "wide"),
        P("narrow", "wide"),
        P("narrow", "wide"),
        P("narrow", "wide"),
        P(None, "narrow"),
        P(None, "narrow"),
        P(None, "narrow"),
        P("narrow", None),
        P("narrow", None),
        P("narrow", None),
    )
    return jax.shard_map(
        shards,
        mesh=mesh,
        in_specs=placed,
        out_specs=(
            P(("wide", "narrow"), None),
            P(("wide", "narrow"), None),
            P(),
            P(),
            P(),
            P(),
            P(),
            P(),
            P("narrow", "wide"),
            P("narrow", "wide"),
            P("narrow", "wide"),
            P("narrow", "wide"),
            P("narrow", "wide"),
            P("narrow", "wide"),
            P(None, "narrow"),
            P(None, "narrow"),
            P(None, "narrow"),
            P("narrow", None),
            P("narrow", None),
            P("narrow", None),
            P(),
            P("narrow", "wide"),
            P("narrow", "wide"),
            P(None, "narrow"),
            P("narrow", None),
        ),
        check_vma=False,
    )
```

profile of v0, /device:TPU:0, one launch (start us, length us, event | category | flops | bytes accessed | tf_op | source)
XLA Modules:
  0.0 438.5 jit_solution(9235745260289861112)
XLA Ops:
  22.5 30.4 %collective-permute-done.tokens_ref = bf16[512,1024]{1,0:T(8,128)(2,1)S(1)} collective-permute-done((bf16[512,1024]{1,0:T(8,128)(2,1)}, bf16[512,1024]{1,0:T(8,128)(2,1)S(1)}, u32[]{:S(2)}, u32[]{:S(2)}) %collective-permute-start) | collective-permute-done | bytes 1048608 | tf_op jit(solution)/shard_map/ppermute | solution.py:943
  60.2 5.6 %feed.5 = (bf16[2048,1024]{1,0:T(8,128)(2,1)}, bf16[2048,1024]{1,0:T(8,128)(2,1)}, f32[2048,1024]{1,0:T(8,128)}) custom-call(bf16[512,1024]{1,0:T(8,128)(2,1)} %copy-done.7, f32[2,1024]{1,0:T(2,128)} %refs_12_.1, bf16[1024,1024]{1,0:T(8,128)(2,1)} %convert_element_type.95.weight_ref.up_ref, ...), custom_call_target="tpu_custom_call", output_to_operand_aliasing={{0}: (3, {}), {1}: (4, {}), {2}: (5, {})} | custom-call | tf_op jit(solution)/shard_map/feed/pallas_call | solution.py:140
  67.6 5.6 %fusion.10 = (f32[2048,128]{1,0:T(8,128)}, f32[2048,128]{1,0:T(8,128)}) fusion(f32[128]{0:T(128)S(1)} %compare_select_fusion.2, f32[128]{0:T(128)S(1)} %mul.89, f32[2048]{0:T(1024)S(1)} %subtract_convert_fusion), kind=kLoop, calls=%fused_computation.31 | loop fusion | flops 524288 | bytes 2106368 | tf_op jit(solution)/shard_map/mul | solution.py:69
  73.2 13.6 %collective-permute-done.1.tokens_ref = bf16[512,1024]{1,0:T(8,128)(2,1)} collective-permute-done((bf16[512,1024]{1,0:T(8,128)(2,1)S(1)}, bf16[512,1024]{1,0:T(8,128)(2,1)}, u32[]{:S(2)}, u32[]{:S(2)}) %collective-permute-start.1) | collective-permute-done | bytes 1048608 | tf_op jit(solution)/shard_map/ppermute | solution.py:943
  89.4 6.3 %feed.6 = (bf16[2048,1024]{1,0:T(8,128)(2,1)}, bf16[2048,1024]{1,0:T(8,128)(2,1)}, f32[2048,1024]{1,0:T(8,128)}) custom-call(bf16[512,1024]{1,0:T(8,128)(2,1)} %collective-permute-done.1.tokens_ref, f32[2,1024]{1,0:T(2,128)} %refs_12_.1, ...), custom_call_target="tpu_custom_call", output_to_operand_aliasing={{0}: (3, {}), {1}: (4, {}), {2}: (5, {})} | custom-call | tf_op jit(solution)/shard_map/feed/pallas_call | solution.py:140
  103.0 10.1 %collective-permute-done.2.tokens_ref = bf16[512,1024]{1,0:T(8,128)(2,1)S(1)} collective-permute-done((bf16[512,1024]{1,0:T(8,128)(2,1)}, bf16[512,1024]{1,0:T(8,128)(2,1)S(1)}, u32[]{:S(2)}, u32[]{:S(2)}) %collective-permute-start.2) | collective-permute-done | bytes 1048608 | tf_op jit(solution)/shard_map/ppermute | solution.py:943
  114.1 5.7 %feed.7 = (bf16[2048,1024]{1,0:T(8,128)(2,1)}, bf16[2048,1024]{1,0:T(8,128)(2,1)}, f32[2048,1024]{1,0:T(8,128)}) custom-call(bf16[512,1024]{1,0:T(8,128)(2,1)} %copy-done.8, f32[2,1024]{1,0:T(2,128)} %refs_12_.1, bf16[1024,1024]{1,0:T(8,128)(2,1)} %convert_element_type.95.weight_ref.up_ref, ...), custom_call_target="tpu_custom_call", output_to_operand_aliasing={{0}: (3, {}), {1}: (4, {}), {2}: (5, {})} | custom-call | tf_op jit(solution)/shard_map/feed/pallas_call | solution.py:140
  124.8 7.7 %all-gather.10.cloned.1.call-done = bf16[8192,384]{1,0:T(8,128)(2,1)} async-done(((bf16[1024,384]{1,0:T(8,128)(2,1)}), bf16[8192,384]{1,0:T(8,128)(2,1)}) %all-gather.10.cloned.1.call-update) | async-done | bytes 6291472 | tf_op jit(solution)/shard_map/all_gather | solution.py:957
  132.5 8.4 %project_all.1 = (bf16[2048,768]{1,0:T(8,128)(2,1)}, bf16[1024,768]{1,0:T(8,128)(2,1)}) custom-call(s32[1]{0:T(128)} %bitcast.3.index_ref, bf16[2048,1024]{1,0:T(8,128)(2,1)} %get-tuple-element.206.rows_ref, f32[2048,128]{1,0:T(8,128)} %get-tuple-element.207.cos_ref, f32[2048,128]{1,0:T(8,128)} %get-tuple-element.208.sin_ref, ...), custom_call_target="tpu_custom_call" | custom-call | tf_op jit(solution)/shard_map/project_all/pallas_call | solution.py:296
  147.8 14.1 %attend.2 = (bf16[2048,256]{1,0:T(8,128)(2,1)}, f32[256,2048]{1,0:T(8,128)}, f32[2,8,2048]{2,1,0:T(8,128)}) custom-call(s32[4]{0:T(128)} %copy-done.23, s32[4]{0:T(128)} %select_reduce_fusion.3.first_ref, s32[4]{0:T(128)} %get-tuple-element.219.last_ref, s32[1,2048]{1,0:T(1,128)} %bitcast.53, ...), custom_call_target="tpu_custom_call" | custom-call | tf_op jit(solution)/shard_map/attend/pallas_call | solution.py:448
  161.9 6.5 %collective-permute-done.5.grad_ref = bf16[512,1024]{1,0:T(8,128)(2,1)S(1)} collective-permute-done((bf16[512,1024]{1,0:T(8,128)(2,1)S(1)}, bf16[512,1024]{1,0:T(8,128)(2,1)S(1)}, u32[]{:S(2)}, u32[]{:S(2)}) %collective-permute-start.5) | collective-permute-done | bytes 1048608 | tf_op jit(solution)/shard_map/ppermute | solution.py:943
  174.6 14.1 %attend.3 = (bf16[2048,256]{1,0:T(8,128)(2,1)}, f32[256,2048]{1,0:T(8,128)}, f32[2,8,2048]{2,1,0:T(8,128)}) custom-call(s32[4]{0:T(128)} %copy-done.23, s32[4]{0:T(128)} %select_reduce_fusion.3.first_ref, s32[4]{0:T(128)} %get-tuple-element.219.last_ref, s32[1,2048]{1,0:T(1,128)} %bitcast.54, ...), custom_call_target="tpu_custom_call", output_to_operand_aliasing={{0}: (7, {}), {1}: (8, {}), {2}: (9, {})} | custom-call | tf_op jit(solution)/shard_map/attend/pallas_call | solution.py:448
  188.6 7.6 %collective-permute-done.6.grad_ref = bf16[512,1024]{1,0:T(8,128)(2,1)S(1)} collective-permute-done((bf16[512,1024]{1,0:T(8,128)(2,1)S(1)}, bf16[512,1024]{1,0:T(8,128)(2,1)S(1)}, u32[]{:S(2)}, u32[]{:S(2)}) %collective-permute-start.6) | collective-permute-done | bytes 1048608 | tf_op jit(solution)/shard_map/ppermute | solution.py:943
  202.2 8.2 %convolution_convert_fusion.1 = bf16[1024,1024]{1,0:T(8,128)(2,1)S(1)} fusion(bf16[2048,1024]{1,0:T(8,128)(2,1)} %get-tuple-element.206.rows_ref, bf16[2048,1024]{1,0:T(8,128)(2,1)} %get-tuple-element.249.hidden_ref), kind=kOutput, calls=%fused_computation.25 | convolution fusion | flops 4296015872 | bytes 10485760 | tf_op jit(solution)/shard_map/dot_general | solution.py:45
  232.6 33.7 %attend_back.1.mixed_ref = bf16[2048,768]{1,0:T(8,128)(2,1)} custom-call(s32[4]{0:T(128)} %copy-done.23, s32[4]{0:T(128)} %get-tuple-element.219.last_ref, s32[4]{0:T(128)} %get-tuple-element.259.end_ref, s32[1,2048]{1,0:T(1,128)} %bitcast.55, f32[2048,128]{1,0:T(8,128)} %get-tuple-element.207.cos_ref, f32[2048,128]{1,0:T(8,128)} %get-tuple-element.208.sin_ref, ...), custom_call_target="tpu_custom_call" | custom-call | tf_op jit(solution)/shard_map/attend_back/pallas_call | solution.py:593
  266.3 8.1 %convolution_convert_fusion.2 = bf16[1024,768]{1,0:T(8,128)(2,1)} fusion(bf16[2048,1024]{1,0:T(8,128)(2,1)} %get-tuple-element.206.rows_ref, bf16[2048,768]{1,0:T(8,128)(2,1)} %attend_back.1.mixed_ref), kind=kOutput, calls=%fused_computation.26 | convolution fusion | flops 3222011904 | bytes 8912896 | tf_op jit(solution)/shard_map/dot_general | solution.py:45
  291.2 6.1 %pull.6 = (f32[512,1024]{1,0:T(8,128)}, f32[2,1024]{1,0:T(2,128)}) custom-call(bf16[2048,768]{1,0:T(8,128)(2,1)} %attend_back.1.mixed_ref, bf16[2048,1024]{1,0:T(8,128)(2,1)} %get-tuple-element.249.hidden_ref, bf16[1024,768]{1,0:T(8,128)(2,1)} %get-tuple-element.272.proj_ref, bf16[1024,1024]{1,0:T(8,128)(2,1)} %convert_element_type.95.weight_ref.up_ref, ...), custom_call_target="tpu_custom_call" | custom-call | tf_op jit(solution)/shard_map/pull/pallas_call | solution.py:249
  297.3 6.4 %pull.5 = (f32[512,1024]{1,0:T(8,128)}, f32[2,1024]{1,0:T(2,128)}) custom-call(bf16[2048,768]{1,0:T(8,128)(2,1)} %attend_back.1.mixed_ref, bf16[2048,1024]{1,0:T(8,128)(2,1)} %get-tuple-element.249.hidden_ref, bf16[1024,768]{1,0:T(8,128)(2,1)} %get-tuple-element.272.proj_ref, bf16[1024,1024]{1,0:T(8,128)(2,1)} %convert_element_type.95.weight_ref.up_ref, ...), custom_call_target="tpu_custom_call" | custom-call | tf_op jit(solution)/shard_map/pull/pallas_call | solution.py:249
  303.7 6.1 %pull.4 = (f32[512,1024]{1,0:T(8,128)}, f32[2,1024]{1,0:T(2,128)}) custom-call(bf16[2048,768]{1,0:T(8,128)(2,1)} %attend_back.1.mixed_ref, bf16[2048,1024]{1,0:T(8,128)(2,1)} %get-tuple-element.249.hidden_ref, bf16[1024,768]{1,0:T(8,128)(2,1)} %get-tuple-element.272.proj_ref, bf16[1024,1024]{1,0:T(8,128)(2,1)} %convert_element_type.95.weight_ref.up_ref, ...), custom_call_target="tpu_custom_call" | custom-call | tf_op jit(solution)/shard_map/pull/pallas_call | solution.py:249
  313.7 21.0 %collective-permute-done.12 = bf16[512,1024]{1,0:T(8,128)(2,1)S(1)} collective-permute-done((bf16[512,1024]{1,0:T(8,128)(2,1)S(1)}, bf16[512,1024]{1,0:T(8,128)(2,1)S(1)}, u32[]{:S(2)}, u32[]{:S(2)}) %collective-permute-start.12) | collective-permute-done | bytes 1048608 | tf_op jit(solution)/shard_map/ppermute | solution.py:943
  336.8 6.2 %pull.7 = (f32[512,1024]{1,0:T(8,128)}, f32[2,1024]{1,0:T(2,128)}) custom-call(bf16[2048,768]{1,0:T(8,128)(2,1)} %attend_back.1.mixed_ref, bf16[2048,1024]{1,0:T(8,128)(2,1)} %get-tuple-element.249.hidden_ref, bf16[1024,768]{1,0:T(8,128)(2,1)} %get-tuple-element.272.proj_ref, bf16[1024,1024]{1,0:T(8,128)(2,1)} %convert_element_type.95.weight_ref.up_ref, ...), custom_call_target="tpu_custom_call" | custom-call | tf_op jit(solution)/shard_map/pull/pallas_call | solution.py:249
  343.7 6.3 %pick_merge.1 = bf16[1024,1024]{1,0:T(8,128)(2,1)} custom-call(s32[4]{0:T(128)} %copy-done.23, bf16[8,4,256,128]{3,2,1,0:T(8,128)(2,1)} %bitcast.48), custom_call_target="tpu_custom_call" | custom-call | tf_op jit(solution)/shard_map/pick_merge/pallas_call | solution.py:332
  362.0 30.0 %finish.1 = (f32[24,128]{1,0:T(8,128)}, f32[8,128]{1,0:T(8,128)}, bf16[256,384]{1,0:T(8,128)(2,1)}) custom-call(f32[24,128]{1,0:T(8,128)} %select_maximum_fusion.refs_0_, bf16[128,1024]{1,0:T(8,128)(2,1)} %reduce-scatter.5.cloned.1.call-done.refs_1_.merge_ref, bf16[256,1024]{1,0:T(8,128)(2,1)} %reduce-scatter.3.cloned.1.call-done.refs_2_), custom_call_target="tpu_custom_call" | custom-call | tf_op jit(solution)/shard_map/finish/pallas_call | solution.py:794
  398.2 27.1 %adam_all.1 = (f32[1024,1024]{1,0:T(8,128)}, f32[1024,1024]{1,0:T(8,128)}, f32[1024,1024]{1,0:T(8,128)}, bf16[1024,1024]{1,0:T(8,128)(2,1)}, f32[1024,1024]{1,0:...) custom-call(f32[1,4]{1,0:T(1,128)} %maximum_bitcast_fusion.scale_ref, ...), custom_call_target="tpu_custom_call" | custom-call | tf_op jit(solution)/shard_map/adam_all/pallas_call | solution.py:876
  (158 shorter events, 127.8 us)
Async XLA Ops:
  7.2 48.5 %all-gather.8.cloned.1.call-start = ((), (), s32[]{:S(2)}) async-start(), calls=%async_computation.2 | async-start | bytes 1310720 | tf_op jit(solution)/shard_map/all_gather | solution.py:952
  9.9 109.8 %all-gather.12.cloned.1.call-start = ((), (), s32[]{:S(2)}) async-start(), calls=%async_computation.6 | async-start | bytes 2359296 | tf_op jit(solution)/shard_map/all_gather | solution.py:957
  10.0 42.9 %collective-permute-start = (bf16[512,1024]{1,0:T(8,128)(2,1)}, bf16[512,1024]{1,0:T(8,128)(2,1)S(1)}, u32[]{:S(2)}, u32[]{:S(2)}) collective-permute-start(bf16[512,1024]{1,0:T(8,128)(2,1)} %tokens_ref.3), channel_id=1, source_target_pairs={{0,1},{1,2},{2,3},{3,0},{4,5},{5,6},{6,7},{7,4},{8,9},{9,10},{10,1... | collective-permute-start | bytes 3145736 | tf_op jit(solution)/shard_map/ppermute | solution.py:943
  22.5 37.5 %copy-start.26 = (s32[1,3]{1,0:T(1,128)S(1)}, s32[1,3]{1,0:T(1,128)}, u32[]{:S(2)}) copy-start(s32[1,3]{1,0:T(1,128)} %param.21) | copy-start | bytes 40
  22.5 43.3 %copy-start.23 = (s32[4]{0:T(128)}, s32[4]{0:T(128)S(1)}, u32[]{:S(2)}) copy-start(s32[4]{0:T(128)S(1)} %compare_select_fusion.slots_ref) | copy-start | bytes 52
  57.4 75.0 %all-gather.10.cloned.1.call-start = ((), (), s32[]{:S(2)}) async-start(), calls=%async_computation.5 | async-start | bytes 7077888 | tf_op jit(solution)/shard_map/all_gather | solution.py:957
  59.6 216.9 %reduce-scatter.3.cloned.1.call-start = ((), (), s32[]{:S(2)}) async-start(), calls=%async_computation.3 | async-start | bytes 4718592 | tf_op jit(solution)/shard_map/reduce_scatter | solution.py:1037
  59.8 27.0 %collective-permute-start.1 = (bf16[512,1024]{1,0:T(8,128)(2,1)S(1)}, bf16[512,1024]{1,0:T(8,128)(2,1)}, u32[]{:S(2)}, u32[]{:S(2)}) collective-permute-start(bf16[512,1024]{1,0:T(8,128)(2,1)S(1)} %collective-permute-done.tokens_ref), channel_id=1, source_target_pairs={{0,1},{1,2},{2,3},{3,0},{4,5},{5,6},{6,7},{7,4},{8,9},{9,10},{10,1... | collective-permute-start | bytes 3145736 | tf_op jit(solution)/shard_map/ppermute | solution.py:943
  86.9 26.2 %collective-permute-start.2 = (bf16[512,1024]{1,0:T(8,128)(2,1)}, bf16[512,1024]{1,0:T(8,128)(2,1)S(1)}, u32[]{:S(2)}, u32[]{:S(2)}) collective-permute-start(bf16[512,1024]{1,0:T(8,128)(2,1)} %collective-permute-done.1.tokens_ref), channel_id=1, source_target_pairs={{0,1},{1,2},{2,3},{3,0},{4,5},{5,6},{6,7},{7,4},{8,9},{9,10},{10,1... | collective-permute-start | bytes 3145736 | tf_op jit(solution)/shard_map/ppermute | solution.py:943
  113.1 27.8 %collective-permute-start.4 = (bf16[512,1024]{1,0:T(8,128)(2,1)}, bf16[512,1024]{1,0:T(8,128)(2,1)S(1)}, u32[]{:S(2)}, u32[]{:S(2)}) collective-permute-start(bf16[512,1024]{1,0:T(8,128)(2,1)} %grad_ref), channel_id=1, source_target_pairs={{0,1},{1,2},{2,3},{3,0},{4,5},{5,6},{6,7},{7,4},{8,9},{9,10},{10,1... | collective-permute-start | bytes 3145736 | tf_op jit(solution)/shard_map/ppermute | solution.py:943
  140.9 27.5 %collective-permute-start.5 = (bf16[512,1024]{1,0:T(8,128)(2,1)S(1)}, bf16[512,1024]{1,0:T(8,128)(2,1)S(1)}, u32[]{:S(2)}, u32[]{:S(2)}) collective-permute-start(bf16[512,1024]{1,0:T(8,128)(2,1)S(1)} %collective-permute-done.4.grad_ref), channel_id=1, source_target_pairs={{0,1},{1,2},{2,3},{3,0},{4,5},{5,6},{6,7},{7,4},{8,9},{9,10},{10,1... | collective-permute-start | bytes 3145736 | tf_op jit(solution)/shard_map/ppermute | solution.py:943
  168.4 27.8 %collective-permute-start.6 = (bf16[512,1024]{1,0:T(8,128)(2,1)S(1)}, bf16[512,1024]{1,0:T(8,128)(2,1)S(1)}, u32[]{:S(2)}, u32[]{:S(2)}) collective-permute-start(bf16[512,1024]{1,0:T(8,128)(2,1)S(1)} %collective-permute-done.5.grad_ref), channel_id=1, source_target_pairs={{0,1},{1,2},{2,3},{3,0},{4,5},{5,6},{6,7},{7,4},{8,9},{9,10},{10,1... | collective-permute-start | bytes 3145736 | tf_op jit(solution)/shard_map/ppermute | solution.py:943
  168.4 49.0 %collective-permute-start.3 = (bf16[512,1024]{1,0:T(8,128)(2,1)}, bf16[512,1024]{1,0:T(8,128)(2,1)}, u32[]{:S(2)}, u32[]{:S(2)}) collective-permute-start(bf16[512,1024]{1,0:T(8,128)(2,1)} %convolution_convert_fusion.3), channel_id=1, source_target_pairs={{0,1},{1,2},{2,3},{3,0},{4,5},{5,6},{6,7},{7,4},{8,9},{9,10},{10,1... | collective-permute-start | bytes 3145736 | tf_op jit(solution)/shard_map/ppermute | solution.py:943
  219.9 138.7 %reduce-scatter.5.cloned.1.call-start = ((), (), s32[]{:S(2)}) async-start(), calls=%async_computation.4 | async-start | bytes 2359296 | tf_op jit(solution)/shard_map/reduce_scatter | solution.py:1037
  228.2 48.3 %collective-permute-start.7 = (bf16[512,1024]{1,0:T(8,128)(2,1)}, bf16[512,1024]{1,0:T(8,128)(2,1)}, u32[]{:S(2)}, u32[]{:S(2)}) collective-permute-start(bf16[512,1024]{1,0:T(8,128)(2,1)} %add_convert_fusion.3), channel_id=1, source_target_pairs={{0,1},{1,2},{2,3},{3,0},{4,5},{5,6},{6,7},{7,4},{8,9},{9,10},{10,1... | collective-permute-start | bytes 3145736 | tf_op jit(solution)/shard_map/ppermute | solution.py:943
  228.2 48.3 %collective-permute-start.10 = (bf16[512,256]{1,0:T(8,128)(2,1)}, bf16[512,256]{1,0:T(8,128)(2,1)}, u32[]{:S(2)}, u32[]{:S(2)}) collective-permute-start(bf16[512,256]{1,0:T(8,128)(2,1)} %get-tuple-element.258), channel_id=1, source_target_pairs={{0,3},{1,0},{2,1},{3,2},{4,7},{5,4},{6,5},{7,6},{8,11},{9,8},{10,9... | collective-permute-start | bytes 786440 | tf_op jit(solution)/shard_map/ppermute | solution.py:1092
  232.0 44.5 %collective-permute-start.8 = (bf16[512,256]{1,0:T(8,128)(2,1)S(1)}, bf16[512,256]{1,0:T(8,128)(2,1)}, u32[]{:S(2)}, u32[]{:S(2)}) collective-permute-start(bf16[512,256]{1,0:T(8,128)(2,1)S(1)} %copy-done.20), channel_id=1, source_target_pairs={{0,1},{1,2},{2,3},{3,0},{4,5},{5,6},{6,7},{7,4},{8,9},{9,10},{10,1... | collective-permute-start | bytes 786440 | tf_op jit(solution)/shard_map/ppermute | solution.py:1092
  232.0 44.4 %collective-permute-start.9 = (bf16[512,256]{1,0:T(8,128)(2,1)S(1)}, bf16[512,256]{1,0:T(8,128)(2,1)}, u32[]{:S(2)}, u32[]{:S(2)}) collective-permute-start(bf16[512,256]{1,0:T(8,128)(2,1)S(1)} %copy-done.19), channel_id=1, source_target_pairs={{0,2},{1,3},{2,0},{3,1},{4,6},{5,7},{6,4},{7,5},{8,10},{9,11},{10,... | collective-permute-start | bytes 786440 | tf_op jit(solution)/shard_map/ppermute | solution.py:1092
  279.7 118.5 %all-gather.14.cloned.1.call-start = ((), (), s32[]{:S(2)}) async-start(), calls=%async_computation.7 | async-start | bytes 4718592 | tf_op jit(solution)/shard_map/all_gather | solution.py:1115
  283.5 27.2 %collective-permute-start.11 = (bf16[512,1024]{1,0:T(8,128)(2,1)}, bf16[512,1024]{1,0:T(8,128)(2,1)S(1)}, u32[]{:S(2)}, u32[]{:S(2)}) collective-permute-start(bf16[512,1024]{1,0:T(8,128)(2,1)} %add_convert_fusion.2), channel_id=1, source_target_pairs={{0,1},{1,2},{2,3},{3,0},{4,5},{5,6},{6,7},{7,4},{8,9},{9,10},{10,1... | collective-permute-start | bytes 3145736 | tf_op jit(solution)/shard_map/ppermute | solution.py:943
  312.9 21.9 %collective-permute-start.12 = (bf16[512,1024]{1,0:T(8,128)(2,1)S(1)}, bf16[512,1024]{1,0:T(8,128)(2,1)S(1)}, u32[]{:S(2)}, u32[]{:S(2)}) collective-permute-start(bf16[512,1024]{1,0:T(8,128)(2,1)S(1)} %convert_element_type.115), channel_id=1, source_target_pairs={{0,1},{1,2},{2,3},{3,0},{4,5},{5,6},{6,7},{7,4},{8,9},{9,10},{10,1... | collective-permute-start | bytes 3145736 | tf_op jit(solution)/shard_map/ppermute | solution.py:943
  336.1 23.3 %collective-permute-start.13 = (bf16[512,1024]{1,0:T(8,128)(2,1)}, bf16[512,1024]{1,0:T(8,128)(2,1)}, u32[]{:S(2)}, u32[]{:S(2)}) collective-permute-start(bf16[512,1024]{1,0:T(8,128)(2,1)} %add_convert_fusion.1), channel_id=1, source_target_pairs={{0,1},{1,2},{2,3},{3,0},{4,5},{5,6},{6,7},{7,4},{8,9},{9,10},{10,1... | collective-permute-start | bytes 3145736 | tf_op jit(solution)/shard_map/ppermute | solution.py:943
  358.6 36.6 %copy-start.21 = (f32[2,1024]{1,0:T(2,128)S(1)}, f32[2,1024]{1,0:T(2,128)}, u32[]{:S(2)}) copy-start(f32[2,1024]{1,0:T(2,128)} %refs_12_.1) | copy-start | bytes 24580
  392.0 33.4 %collective-permute-start.14 = (bf16[512,1024]{1,0:T(8,128)(2,1)}, bf16[512,1024]{1,0:T(8,128)(2,1)}, u32[]{:S(2)}, u32[]{:S(2)}) collective-permute-start(bf16[512,1024]{1,0:T(8,128)(2,1)} %add_convert_fusion), channel_id=1, source_target_pairs={{0,1},{1,2},{2,3},{3,0},{4,5},{5,6},{6,7},{7,4},{8,9},{9,10},{10,1... | collective-permute-start | bytes 3145736 | tf_op jit(solution)/shard_map/ppermute | solution.py:943
  (24 other events, 203.2 us)
Sparse Core Ops, SparseCore 0:
  10.2 45.5 all-gather.7
  58.2 26.3 all-gather.11
  87.0 45.3 all-gather.9
  220.0 48.8 reduce-scatter.2
  279.8 51.0 reduce-scatter.4
  332.7 36.5 all-gather.13
where the time goes:
time: 447 us; the launch traced here: 438 us
  Pallas kernels  202 us (45%)
  waiting for transfers between devices  103 us (23%)
  other arithmetic  48.2 us (11%)
  matrix products  41.4 us (9%)
  starting transfers between devices  18.2 us (4%)
  between operations  15.6 us (3%)
  local copies, waits for them, and re-layouts  10.8 us (2%)
    ppermute x12, waiting for transfers between devices, send_on(): return lax.ppermute(array, 'narrow', onward)  91.4 us
    pallas_call x1, Pallas kernels, attend_back(): pl.pallas_call(partial(attend_back_kernel, block_q, block_k, heads_in), o...  33.7 us
    pallas_call x1, Pallas kernels, finish(): pl.pallas_call(partial(finish_kernel, narrow_count, wide_count, own_units...  30 us
    pallas_call x2, Pallas kernels, attend(): pl.pallas_call(partial(attend_kernel, block_q, block_k, heads_in), out_sh...  28.2 us
    pallas_call x1, Pallas kernels, adam_all(): pl.pallas_call(adam_kernel, out_shape=tuple(shapes), grid=(count,), in_sp...  27.1 us
    pallas_call x4, Pallas kernels, pull(): pl.pallas_call(pull_kernel, out_shape=(jax.ShapeDtypeStruct((rows, depth)...  24.8 us
    pallas_call x4, Pallas kernels, feed(): pl.pallas_call(feed_kernel, out_shape=(jax.ShapeDtypeStruct((slots * rows...  23.2 us
    dot_general x4, matrix products, dot_first(): lax.dot_general(left_side, right_side, (((0,), (0,)), ((), ())), preferre...  23.1 us
  transfers between devices with their start and end apart: 21, of which 10 were waited for; matrix products, arithmetic and copies ran while one was open for 19% of the time, Pallas kernels for 46%

commit v1 on v0

--- a/solution.py
+++ b/solution.py
@@ -160,6 +160,55 @@
         cost_estimate=short,
         name="feed",
     )(tokens, params, weight, *held)
+
+
+def outer_kernel(split, first_left, first_right, second_left, second_right, out_ref, first, second):
+    step = pl.program_id(0)
+    for left_ref, right_ref, total in (
+        (first_left, first_right, first),
+        (second_left, second_right, second),
+    ):
+        term = dot_first(left_ref[...], right_ref[...])
+
+        @pl.when(step == 0)
+        def _():
+            total[...] = term
+
+        @pl.when(step > 0)
+        def _():
+            total[...] += term
+
+    @pl.when(step == pl.num_programs(0) - 1)
+    def _():
+        if split:
+            blocks, unused, rows, cols = out_ref.shape
+            for matrix, total in enumerate((first, second)):
+                for block in range(blocks):
+                    out_ref[block, matrix] = total[block * rows : (block + 1) * rows, :].astype(
+                        jnp.bfloat16
+                    )
+        else:
+            width = first.shape[1]
+            out_ref[:, :width] = first[...].astype(jnp.bfloat16)
+            out_ref[:, width:] = second[...].astype(jnp.bfloat16)
+
+
+def outer(blocks, first_left, first_right, second_left, second_right):
+    count, depth = first_left.shape
+    rows = min(ROW_BLOCK, count)
+    widths = [first_right.shape[1], second_right.shape[1]]
+    shape = (blocks, 2, depth // blocks, widths[0]) if blocks else (depth, sum(widths))
+    operands = (first_left, first_right, second_left, second_right)
+    return pl.pallas_call(
+        partial(outer_kernel, bool(blocks)),
+        out_shape=jax.ShapeDtypeStruct(shape, jnp.bfloat16),
+        grid=(count // rows,),
+        in_specs=[pl.BlockSpec((rows, array.shape[1]), lambda k: (k, 0)) for array in operands],
+        out_specs=pl.BlockSpec(shape, lambda k: (0,) * len(shape)),
+        scratch_shapes=[pltpu.VMEM((depth, width), jnp.float32) for width in widths],
+        cost_estimate=short,
+        name="outer",
+    )(*operands)
 
 
 def push_kernel(index_ref, grad_ref, slope_ref, down_ref, merge_ref, *refs):
@@ -631,13 +680,14 @@
     exchange = own_units > 0
     if exchange:
         (
-            parts_ref, piece_ref, feed_ref, total_ref, stats_ref, block_ref, mine, near, far, near_sum,
-            send_near, recv_near, send_far, recv_far, send_piece, recv_piece,
+            parts_ref, piece_ref, feed_ref, sent_ref, total_ref, stats_ref, arrived_ref, block_ref,
+            mine, near, far, near_sum, send_near, recv_near, send_far, recv_far, send_ring, recv_ring,
+            send_piece, recv_piece,
         ) = refs
     else:
         (
-            parts_ref, piece_ref, feed_ref, total_ref, stats_ref, mine, near, far, near_sum,
-            send_near, recv_near, send_far, recv_far,
+            parts_ref, piece_ref, feed_ref, sent_ref, total_ref, stats_ref, arrived_ref,
+            mine, near, far, near_sum, send_near, recv_near, send_far, recv_far, send_ring, recv_ring,
         ) = refs
     narrow_me = lax.axis_index("narrow")
     wide_me = lax.axis_index("wide")
@@ -720,6 +770,15 @@
             moves.append((stays, remote))
     for copy in near_copies:
         copy.wait()
+    ring = pltpu.make_async_remote_copy(
+        src_ref=sent_ref,
+        dst_ref=arrived_ref,
+        send_sem=send_ring,
+        recv_sem=recv_ring,
+        device_id=place(lax.rem(narrow_me + 1, narrow_count), wide_me),
+        device_id_type=mesh_ids,
+    )
+    ring.start()
     value = near[0]
     for k in range(1, narrow_count):
         value = value + near[k]
@@ -762,10 +821,11 @@
                     ],
                     recv_piece.at[half * per_shard + column],
                 ).wait()
+    ring.wait()
 
 
 def finish(
-    parts, piece, feed_piece, exchange, narrow_count, wide_count, own_width, proj_cols, entries
+    parts, piece, feed_piece, sent, exchange, narrow_count, wide_count, own_width, proj_cols, entries
 ):
     shape = parts.shape
     own_units = own_width // LANES if exchange else 0
@@ -774,7 +834,9 @@
     shapes = [
         jax.ShapeDtypeStruct(shape, jnp.float32),
         jax.ShapeDtypeStruct((8, LANES), jnp.float32),
+        jax.ShapeDtypeStruct(sent.shape, sent.dtype),
     ]
+    whole = pl.BlockSpec(memory_space=pl.ANY)
     scratch = [
         pltpu.VMEM(shape, jnp.float32),
         pltpu.VMEM((narrow_count,) + shape, jnp.float32),
@@ -784,6 +846,8 @@
         pltpu.SemaphoreType.DMA((narrow_count - 1,)),
         pltpu.SemaphoreType.DMA((wide_count - 1,)),
         pltpu.SemaphoreType.DMA((wide_count - 1,)),
+        pltpu.SemaphoreType.DMA,
+        pltpu.SemaphoreType.DMA,
     ]
     if exchange:
         shapes.append(jax.ShapeDtypeStruct((D // narrow_count, proj_cols), jnp.bfloat16))
@@ -794,12 +858,12 @@
     return pl.pallas_call(
         partial(finish_kernel, narrow_count, wide_count, own_units, per_shard, entries),
         out_shape=tuple(shapes),
-        in_specs=[vmem] * 3,
-        out_specs=(vmem,) * len(shapes),
+        in_specs=[vmem] * 3 + [whole],
+        out_specs=(vmem, vmem, whole) + (vmem,) * (len(shapes) - 3),
         scratch_shapes=scratch,
         compiler_params=pltpu.CompilerParams(collective_id=0, has_side_effects=True),
         name="finish",
-    )(parts, piece, feed_piece)
+    )(parts, piece, feed_piece, sent)
 
 
 def adam_update(
@@ -968,12 +1032,19 @@
     for slot in range(narrow_count - 1):
         moving = send_on(token_blocks[slot])
         held = feed(slot, narrow_count, token_blocks[slot], norm_params, up_slice, held)
-        if slot != 2:
+        if slot > 0:
+            ready = [slot - 1, slot] if slot == narrow_count - 2 else [slot - 1]
+            for block in ready:
+                term = down_term(held[1], block)
+                branch_terms.append(term.astype(jnp.bfloat16) if block == 1 else term)
+            moving, held, branch_terms, down_slice = meet(moving, held, branch_terms, down_slice)
+        else:
             moving, held = meet(moving, held)
         if slot == 0:
             lengths, slots, moving, weight_rows = meet(lengths, slots, moving, weight_rows)
             proj_all = wide_all(weight_rows[:, :proj_cols])
             merge_all = wide_all(weight_rows[:, proj_cols:])
+            branch_terms = []
         if slot == 1:
             places = (
                 slots[:, None] * tok_rows + jnp.arange(tok_rows, dtype=jnp.int32)[None, :]
@@ -986,12 +1057,6 @@
             moving, cosine, sine, first_start, last_start, last_end = meet(
                 moving, cosine, sine, first_start, last_start, last_end
             )
-        elif slot == 2:
-            first_term = down_term(held[1], 1).astype(jnp.bfloat16)
-            next_term = down_term(held[1], order[1])
-            moving, held, down_slice, first_term, next_term = meet(
-                moving, held, down_slice, first_term, next_term
-            )
         token_blocks.append(moving)
     grad_first, last_block = meet(cotangent, token_blocks[-1])
     token_blocks[-1] = last_block
@@ -1028,8 +1093,9 @@
         )
 
     push_held = push_slot(0, ())
-    moving, packed, activated, slope, push_held = meet(
-        moving, packed, activated, slope, push_held
+    branch_terms.append(down_term(activated, narrow_count - 1))
+    moving, packed, activated, slope, push_held, branch_terms = meet(
+        moving, packed, activated, slope, push_held, branch_terms
     )
     grad_blocks.append(moving)
 
@@ -1054,39 +1120,29 @@
         attended_held = attend_pair(pair, attended_held)
     attended, tall, logs = attended_held
 
-    moving = send_on(first_term)
+    moving = send_on(branch_terms[1])
     push_held = push_slot(narrow_count - 1, push_held)
     grads_all, hidden_grad, attended_grad = push_held
     part_rows = D // wide_count
-    down_grad = dot_first(activated, grads_all).astype(jnp.bfloat16)
-    up_grad = dot_first(gathered, hidden_grad).astype(jnp.bfloat16)
+    if direct:
+        feed_grad = outer(wide_count, gathered, hidden_grad, activated, grads_all)
+    else:
+        down_grad = dot_first(activated, grads_all).astype(jnp.bfloat16)
+        up_grad = dot_first(gathered, hidden_grad).astype(jnp.bfloat16)
+        feed_grad = jnp.stack(
+            [
+                up_grad.reshape(wide_count, part_rows, -1),
+                down_grad.reshape(wide_count, part_rows, -1),
+            ],
+            axis=1,
+        )
+    feed_grad = feed_grad.reshape(2 * D, -1)
     pieces = [
         rows_of(attended, (narrow_count - ahead) % narrow_count)[:, :own_width]
         for ahead in range(narrow_count)
     ]
-    moving, pieces, up_grad, down_grad, attended_grad = meet(
-        moving, pieces, up_grad, down_grad, attended_grad
-    )
-    feed_grad = jnp.concatenate(
-        [
-            up_grad.reshape(wide_count, part_rows, -1),
-            down_grad.reshape(wide_count, part_rows, -1),
-        ],
-        axis=1,
-    ).reshape(2 * D, -1)
+    moving, pieces, feed_grad, attended_grad = meet(moving, pieces, feed_grad, attended_grad)
     feed_part = wide_sum(feed_grad)
-
-    def heads_back():
-        mixed = attend_back(
-            packed, slots, last_start, last_end, seq_start, cosine, sine,
-            tall, logs, attended_grad, heads_in, tok_rows, tok_rows,
-        )
-        proj_grad = dot_first(gathered, mixed).astype(jnp.bfloat16)
-        merge_grad = dot_first(grads_all, attended).astype(jnp.bfloat16)
-        if not direct:
-            proj_grad = proj_grad.reshape(D, 3, held_width)[:, :, :own_width].reshape(D, -1)
-            merge_grad = merge_grad[:, :own_width]
-        return (mixed, proj_grad, merge_grad)
 
     for ahead in range(1, narrow_count):
         pieces[ahead] = lax.ppermute(
@@ -1105,26 +1161,38 @@
         return norm_part
 
     for place, slot in enumerate(order[1:-1]):
-        moving = send_on((moving.astype(jnp.float32) + next_term).astype(jnp.bfloat16))
-        next_term = down_term(activated, order[place + 2])
+        moving = send_on((moving.astype(jnp.float32) + branch_terms[slot]).astype(jnp.bfloat16))
         if place == 0:
-            mixed_grad, *heads_grads = heads_back()
-            moving, pieces, mixed_grad, heads_grads, next_term, feed_part = meet(
-                moving, pieces, mixed_grad, heads_grads, next_term, feed_part
+            mixed_grad = attend_back(
+                packed, slots, last_start, last_end, seq_start, cosine, sine,
+                tall, logs, attended_grad, heads_in, tok_rows, tok_rows,
             )
+            if direct:
+                heads_grad = outer(0, gathered, mixed_grad, grads_all, attended)
+            else:
+                proj_grad = dot_first(gathered, mixed_grad).astype(jnp.bfloat16)
+                merge_grad = dot_first(grads_all, attended).astype(jnp.bfloat16)
+                proj_grad = proj_grad.reshape(D, 3, held_width)[:, :, :own_width]
+                heads_grad = jnp.concatenate(
+                    [proj_grad.reshape(D, 3 * own_width), merge_grad[:, :own_width]], axis=1
+                )
+            moving, pieces, mixed_grad, heads_grad, feed_part = meet(
+                moving, pieces, mixed_grad, heads_grad, feed_part
+            )
+            heads_part = wide_sum(heads_grad)
+        else:
+            norm_part = pull_more(3, mixed_grad, norm_part)
+            moving, terms, norm_part, merge_all, slots, feed_part = meet(
+                moving, terms, norm_part, merge_all, slots, feed_part
+            )
+        if place == narrow_count - 3:
             feed_all = lax.all_gather(feed_part, "wide", axis=0).reshape(
                 wide_count, 2, part_rows, -1
             )
-            heads_part = wide_sum(jnp.concatenate(heads_grads, axis=1))
-        else:
-            norm_part = pull_more(3, mixed_grad, norm_part)
-            moving, terms, norm_part, next_term = meet(moving, terms, norm_part, next_term)
-        if slot == narrow_count - 1:
-            moving, merge_all, slots = meet(moving, merge_all, slots)
-    norm_part = pull_more(narrow_count, mixed_grad, norm_part)
     branch_moving = moving
     moving = send_on(terms[0].astype(jnp.bfloat16))
-    branch = branch_moving.astype(jnp.float32) + next_term
+    norm_part = pull_more(narrow_count, mixed_grad, norm_part)
+    branch = branch_moving.astype(jnp.float32) + branch_terms[0]
     if direct:
         merge_turn = pick_merge(merge_all, slots, own_width)
     else:
@@ -1157,24 +1225,22 @@
     ).reshape(1, 4)
     entries = wide_count * group_rows * D
     for place in range(1, narrow_count - 1):
-        last = place == narrow_count - 2
-        if last:
+        if place == narrow_count - 3:
             moving, parts, heads_part, scales = meet(moving, parts, heads_part, scales)
         sent = (moving.astype(jnp.float32) + terms[place]).astype(jnp.bfloat16)
-        if last:
-            sent, parts = meet(sent, parts)
-            summed = finish(
-                parts, heads_part, feed_part, direct, narrow_count, wide_count, own_width,
+        if place == narrow_count - 3:
+            total, stats, moving, *proj_block = finish(
+                parts, heads_part, feed_part, sent, direct, narrow_count, wide_count, own_width,
                 proj_cols, entries,
             )
-            sent, summed = meet(sent, summed)
+            continue
+        if place == narrow_count - 2:
+            sent, total, stats, proj_block = meet(sent, total, stats, proj_block)
         moving = send_on(sent)
 
-    stats = summed[1]
     if direct:
-        total, stats, proj_block = summed
         updated = adam_all(
-            scales, stats, feed_all, total, proj_block, heads_part, own_width,
+            scales, stats, feed_all, total, proj_block[0], heads_part, own_width,
             [
                 up_weight, up_first, up_second, down_weight, down_first, down_second,
                 proj_weight, proj_first, proj_second, merge_weight, merge_first, merge_second,
@@ -1182,7 +1248,6 @@
             ],
         )
     else:
-        total, stats = summed
         clip_factor = stats[0, 0:1]
         cross = lax.all_gather(heads_part[:, : 3 * own_width], "narrow", axis=0).reshape(
             narrow_count, part_rows, 3, own_width

time: 447 us -> 443 us (level)
  Pallas kernels: 202 us -> 275 us
  waiting for transfers between devices: 103 us -> 58.7 us
  matrix products: 41.4 us -> 18.2 us
  other arithmetic: 48.2 us -> 41.6 us
    ppermute x12 -> x11, waiting for transfers between devices: 91.4 us -> 54.3 us  [send_on(): return lax.ppermute(array, 'narrow', onward)]
    pallas_call x0 -> x2, Pallas kernels: none -> 30.9 us  [outer(): pl.pallas_call(partial(outer_kernel, bool(blocks)), out_shape=jax.ShapeDt...]
    dot_general x4 -> x0, matrix products: 23.1 us -> none  [dot_first(): lax.dot_general(left_side, right_side, (((0,), (0,)), ((), ())), preferre...]
    pallas_call x1, Pallas kernels: 30 us -> 50.6 us  [finish(): pl.pallas_call(partial(finish_kernel, narrow_count, wide_count, own_units...]
    pallas_call x2, Pallas kernels: 28.2 us -> 40.4 us  [attend(): pl.pallas_call(partial(attend_kernel, block_q, block_k, heads_in), out_sh...]
    pallas_call x1, Pallas kernels: 33.7 us -> 43.6 us  [attend_back(): pl.pallas_call(partial(attend_back_kernel, block_q, block_k, heads_in), o...]
    all_gather x2, waiting for transfers between devices: 7.69 us -> 1.43 us  [wide_all(): lax.all_gather(array, 'wide', axis=0)]
    concatenate x2 -> x0, other arithmetic: 5.64 us -> none  [the longest x1 3.19 us: shards(): heads_part = wide_sum(jnp.concatenate(heads_grads, axis=1))]
  transfers between devices with their start and end apart: 21 -> 20, of which waited for: 10 -> 8; matrix products, arithmetic and copies ran while one was open for 19% -> 13% of each run, Pallas kernels for 46% -> 63%
where the time goes in v1:
time: 443 us; the launch traced here: 438 us
  Pallas kernels  275 us (62%)
  waiting for transfers between devices  58.7 us (13%)
  other arithmetic  41.6 us (9%)
  starting transfers between devices  18.4 us (4%)
  matrix products  18.2 us (4%)
  between operations  15.4 us (3%)
  local copies, waits for them, and re-layouts  10.8 us (2%)
    ppermute x11, waiting for transfers between devices, send_on(): return lax.ppermute(array, 'narrow', onward)  54.3 us
    pallas_call x1, Pallas kernels, finish(): pl.pallas_call(partial(finish_kernel, narrow_count, wide_count, own_units...  50.6 us
    pallas_call x1, Pallas kernels, attend_back(): pl.pallas_call(partial(attend_back_kernel, block_q, block_k, heads_in), o...  43.6 us
    pallas_call x2, Pallas kernels, attend(): pl.pallas_call(partial(attend_kernel, block_q, block_k, heads_in), out_sh...  40.4 us
    pallas_call x2, Pallas kernels, outer(): pl.pallas_call(partial(outer_kernel, bool(blocks)), out_shape=jax.ShapeDt...  30.9 us
    pallas_call x1, Pallas kernels, adam_all(): pl.pallas_call(adam_kernel, out_shape=tuple(shapes), grid=(count,), in_sp...  27.1 us
    pallas_call x4, Pallas kernels, pull(): pl.pallas_call(pull_kernel, out_shape=(jax.ShapeDtypeStruct((rows, depth)...  24.9 us
    pallas_call x4, Pallas kernels, feed(): pl.pallas_call(feed_kernel, out_shape=(jax.ShapeDtypeStruct((slots * rows...  22.8 us
  transfers between devices with their start and end apart: 20, of which 8 were waited for; matrix products, arithmetic and copies ran while one was open for 13% of the time, Pallas kernels for 63%

profile of v1, /device:TPU:0, one launch (start us, length us, event | category | flops | bytes accessed | tf_op | source)
XLA Modules:
  0.0 438.0 jit_solution(17423954597343205858)
XLA Ops:
  16.9 5.6 %feed.4 = (bf16[2048,1024]{1,0:T(8,128)(2,1)}, bf16[2048,1024]{1,0:T(8,128)(2,1)}, f32[2048,1024]{1,0:T(8,128)}) custom-call(bf16[512,1024]{1,0:T(8,128)(2,1)} %tokens_ref.3, f32[2,1024]{1,0:T(2,128)} %refs_12_.1, bf16[1024,1024]{1,0:T(8,128)(2,1)} %convert_element_type.83.weight_ref.up_ref), custom_call_target="tpu_custom_call" | custom-call | tf_op jit(solution)/shard_map/feed/pallas_call | solution.py:140
  22.5 30.4 %collective-permute-done.tokens_ref = bf16[512,1024]{1,0:T(8,128)(2,1)S(1)} collective-permute-done((bf16[512,1024]{1,0:T(8,128)(2,1)}, bf16[512,1024]{1,0:T(8,128)(2,1)S(1)}, u32[]{:S(2)}, u32[]{:S(2)}) %collective-permute-start) | collective-permute-done | bytes 1048608 | tf_op jit(solution)/shard_map/ppermute | solution.py:1007
  62.7 5.9 %feed.5 = (bf16[2048,1024]{1,0:T(8,128)(2,1)}, bf16[2048,1024]{1,0:T(8,128)(2,1)}, f32[2048,1024]{1,0:T(8,128)}) custom-call(bf16[512,1024]{1,0:T(8,128)(2,1)} %copy-done.4, f32[2,1024]{1,0:T(2,128)} %refs_12_.1, bf16[1024,1024]{1,0:T(8,128)(2,1)} %convert_element_type.83.weight_ref.up_ref, ...), custom_call_target="tpu_custom_call", output_to_operand_aliasing={{0}: (3, {}), {1}: (4, {}), {2}: (5, {})} | custom-call | tf_op jit(solution)/shard_map/feed/pallas_call | solution.py:140
  74.3 5.5 %fusion.10 = (f32[2048,128]{1,0:T(8,128)}, f32[2048,128]{1,0:T(8,128)}) fusion(f32[128]{0:T(128)S(1)} %compare_select_fusion.2, f32[128]{0:T(128)S(1)} %mul.89, f32[2048]{0:T(1024)S(1)} %subtract_convert_fusion), kind=kLoop, calls=%fused_computation.25 | loop fusion | flops 524288 | bytes 2106368 | tf_op jit(solution)/shard_map/mul | solution.py:69
  79.8 9.6 %collective-permute-done.1.tokens_ref = bf16[512,1024]{1,0:T(8,128)(2,1)} collective-permute-done((bf16[512,1024]{1,0:T(8,128)(2,1)S(1)}, bf16[512,1024]{1,0:T(8,128)(2,1)}, u32[]{:S(2)}, u32[]{:S(2)}) %collective-permute-start.1) | collective-permute-done | bytes 1048608 | tf_op jit(solution)/shard_map/ppermute | solution.py:1007
  89.4 5.6 %feed.6 = (bf16[2048,1024]{1,0:T(8,128)(2,1)}, bf16[2048,1024]{1,0:T(8,128)(2,1)}, f32[2048,1024]{1,0:T(8,128)}) custom-call(bf16[512,1024]{1,0:T(8,128)(2,1)} %collective-permute-done.1.tokens_ref, f32[2,1024]{1,0:T(2,128)} %refs_12_.1, ...), custom_call_target="tpu_custom_call", output_to_operand_aliasing={{0}: (3, {}), {1}: (4, {}), {2}: (5, {})} | custom-call | tf_op jit(solution)/shard_map/feed/pallas_call | solution.py:140
  102.4 13.2 %collective-permute-done.2.tokens_ref = bf16[512,1024]{1,0:T(8,128)(2,1)S(1)} collective-permute-done((bf16[512,1024]{1,0:T(8,128)(2,1)}, bf16[512,1024]{1,0:T(8,128)(2,1)S(1)}, u32[]{:S(2)}, u32[]{:S(2)}) %collective-permute-start.2) | collective-permute-done | bytes 1048608 | tf_op jit(solution)/shard_map/ppermute | solution.py:1007
  116.6 5.7 %feed.7 = (bf16[2048,1024]{1,0:T(8,128)(2,1)}, bf16[2048,1024]{1,0:T(8,128)(2,1)}, f32[2048,1024]{1,0:T(8,128)}) custom-call(bf16[512,1024]{1,0:T(8,128)(2,1)} %copy-done.5, f32[2,1024]{1,0:T(2,128)} %refs_12_.1, bf16[1024,1024]{1,0:T(8,128)(2,1)} %convert_element_type.83.weight_ref.up_ref, ...), custom_call_target="tpu_custom_call", output_to_operand_aliasing={{0}: (3, {}), {1}: (4, {}), {2}: (5, {})} | custom-call | tf_op jit(solution)/shard_map/feed/pallas_call | solution.py:140
  126.1 5.1 %push.4 = (bf16[2048,1024]{1,0:T(8,128)(2,1)}, bf16[2048,1024]{1,0:T(8,128)(2,1)}, bf16[2048,256]{1,0:T(8,128)(2,1)}) custom-call(s32[1]{0:T(128)} %bitcast.3.index_ref, bf16[512,1024]{1,0:T(8,128)(2,1)} %grad_ref, f32[2048,1024]{1,0:T(8,128)} %get-tuple-element.231.slope_ref, bf16[1024,1024]{1,0:T(8,128)(2,1)} %copy-done, bf16[8,4,256,128]{3,2,1,0:T(8,128)(2,1)} %bitcast.34), custom_call_target="tpu_custom_call" | custom-call | tf_op jit(solution)/shard_map/push/pallas_call | solution.py:248
  132.6 8.4 %project_all.1 = (bf16[2048,768]{1,0:T(8,128)(2,1)}, bf16[1024,768]{1,0:T(8,128)(2,1)}) custom-call(s32[1]{0:T(128)} %bitcast.3.index_ref, bf16[2048,1024]{1,0:T(8,128)(2,1)} %get-tuple-element.209.rows_ref.first_left, f32[2048,128]{1,0:T(8,128)} %get-tuple-element.210.cos_ref, f32[2048,128]{1,0:T(8,128)} %get-tuple-element.211.sin_ref, ...), custom_call_target="tpu_custom_call" | custom-call | tf_op jit(solution)/shard_map/project_all/pallas_call | solution.py:345
  142.6 4.9 %push.5 = (bf16[2048,1024]{1,0:T(8,128)(2,1)}, bf16[2048,1024]{1,0:T(8,128)(2,1)}, bf16[2048,256]{1,0:T(8,128)(2,1)}) custom-call(s32[1]{0:T(128)} %bitcast.3.index_ref, bf16[512,1024]{1,0:T(8,128)(2,1)} %collective-permute-done.3.grad_ref, f32[2048,1024]{1,0:T(8,128)} %get-tuple-element.231.slope_ref, ...), custom_call_target="tpu_custom_call", output_to_operand_aliasing={{0}: (5, {}), {1}: (6, {}), {2}: (7, {})} | custom-call | tf_op jit(solution)/shard_map/push/pallas_call | solution.py:248
  147.5 20.2 %attend.2 = (bf16[2048,256]{1,0:T(8,128)(2,1)}, f32[256,2048]{1,0:T(8,128)}, f32[2,8,2048]{2,1,0:T(8,128)}) custom-call(s32[4]{0:T(128)} %copy-done.14, s32[4]{0:T(128)} %select_reduce_fusion.3.first_ref, s32[4]{0:T(128)} %get-tuple-element.226.last_ref, s32[1,2048]{1,0:T(1,128)} %bitcast.41, ...), custom_call_target="tpu_custom_call" | custom-call | tf_op jit(solution)/shard_map/attend/pallas_call | solution.py:497
  170.9 5.0 %push.6 = (bf16[2048,1024]{1,0:T(8,128)(2,1)}, bf16[2048,1024]{1,0:T(8,128)(2,1)}, bf16[2048,256]{1,0:T(8,128)(2,1)}) custom-call(s32[1]{0:T(128)} %bitcast.3.index_ref, bf16[512,1024]{1,0:T(8,128)(2,1)} %copy-done.10, f32[2048,1024]{1,0:T(8,128)} %get-tuple-element.231.slope_ref, ...), custom_call_target="tpu_custom_call", output_to_operand_aliasing={{0}: (5, {}), {1}: (6, {}), {2}: (7, {})} | custom-call | tf_op jit(solution)/shard_map/push/pallas_call | solution.py:248
  175.9 20.2 %attend.3 = (bf16[2048,256]{1,0:T(8,128)(2,1)}, f32[256,2048]{1,0:T(8,128)}, f32[2,8,2048]{2,1,0:T(8,128)}) custom-call(s32[4]{0:T(128)} %copy-done.14, s32[4]{0:T(128)} %select_reduce_fusion.3.first_ref, s32[4]{0:T(128)} %get-tuple-element.226.last_ref, s32[1,2048]{1,0:T(1,128)} %bitcast.42, ...), custom_call_target="tpu_custom_call", output_to_operand_aliasing={{0}: (7, {}), {1}: (8, {}), {2}: (9, {})} | custom-call | tf_op jit(solution)/shard_map/attend/pallas_call | solution.py:497
  202.2 18.0 %outer.2 = bf16[8,2,128,1024]{3,2,1,0:T(8,128)(2,1)} custom-call(bf16[2048,1024]{1,0:T(8,128)(2,1)} %get-tuple-element.209.rows_ref.first_left, bf16[2048,1024]{1,0:T(8,128)(2,1)} %get-tuple-element.256.first_right.hidden_ref, bf16[2048,1024]{1,0:T(8,128)(2,1)} %get-tuple-element.257.second_left, bf16[2048,1024]{1,0:T(8,128)(2,1)} %get-tuple-element.258.second_right.second_left), custom_call_target="tpu_custom_call" | custom-call | tf_op jit(solution)/shard_map/outer/pallas_call | solution.py:202
  229.2 43.6 %attend_back.1.first_right.mixed_ref = bf16[2048,768]{1,0:T(8,128)(2,1)} custom-call(s32[4]{0:T(128)} %copy-done.14, s32[4]{0:T(128)} %get-tuple-element.226.last_ref, s32[4]{0:T(128)} %get-tuple-element.266.end_ref, s32[1,2048]{1,0:T(1,128)} %bitcast.43, f32[2048,128]{1,0:T(8,128)} %get-tuple-element.210.cos_ref, f32[2048,128]{1,0:T(8,128)} %get-tuple-element.211.sin_ref, ...), custom_call_target="tpu_custom_call" | custom-call | tf_op jit(solution)/shard_map/attend_back/pallas_call | solution.py:642
  272.9 12.9 %outer.3 = bf16[1024,1024]{1,0:T(8,128)(2,1)} custom-call(bf16[2048,1024]{1,0:T(8,128)(2,1)} %get-tuple-element.209.rows_ref.first_left, bf16[2048,768]{1,0:T(8,128)(2,1)} %attend_back.1.first_right.mixed_ref, bf16[2048,1024]{1,0:T(8,128)(2,1)} %get-tuple-element.258.second_right.second_left, bf16[2048,256]{1,0:T(8,128)(2,1)} %get-tuple-element.251.second_right), custom_call_target="tpu_custom_call" | custom-call | tf_op jit(solution)/shard_map/outer/pallas_call | solution.py:202
  291.8 6.4 %pull.6 = (f32[512,1024]{1,0:T(8,128)}, f32[2,1024]{1,0:T(2,128)}) custom-call(bf16[2048,768]{1,0:T(8,128)(2,1)} %attend_back.1.first_right.mixed_ref, bf16[2048,1024]{1,0:T(8,128)(2,1)} %get-tuple-element.256.first_right.hidden_ref, bf16[1024,768]{1,0:T(8,128)(2,1)} %get-tuple-element.278.proj_ref, ...), custom_call_target="tpu_custom_call" | custom-call | tf_op jit(solution)/shard_map/pull/pallas_call | solution.py:298
  298.3 6.2 %pull.5 = (f32[512,1024]{1,0:T(8,128)}, f32[2,1024]{1,0:T(2,128)}) custom-call(bf16[2048,768]{1,0:T(8,128)(2,1)} %attend_back.1.first_right.mixed_ref, bf16[2048,1024]{1,0:T(8,128)(2,1)} %get-tuple-element.256.first_right.hidden_ref, bf16[1024,768]{1,0:T(8,128)(2,1)} %get-tuple-element.278.proj_ref, ...), custom_call_target="tpu_custom_call" | custom-call | tf_op jit(solution)/shard_map/pull/pallas_call | solution.py:298
  304.4 6.2 %pull.4 = (f32[512,1024]{1,0:T(8,128)}, f32[2,1024]{1,0:T(2,128)}) custom-call(bf16[2048,768]{1,0:T(8,128)(2,1)} %attend_back.1.first_right.mixed_ref, bf16[2048,1024]{1,0:T(8,128)(2,1)} %get-tuple-element.256.first_right.hidden_ref, bf16[1024,768]{1,0:T(8,128)(2,1)} %get-tuple-element.278.proj_ref, ...), custom_call_target="tpu_custom_call" | custom-call | tf_op jit(solution)/shard_map/pull/pallas_call | solution.py:298
  315.7 6.1 %pull.7 = (f32[512,1024]{1,0:T(8,128)}, f32[2,1024]{1,0:T(2,128)}) custom-call(bf16[2048,768]{1,0:T(8,128)(2,1)} %attend_back.1.first_right.mixed_ref, bf16[2048,1024]{1,0:T(8,128)(2,1)} %get-tuple-element.256.first_right.hidden_ref, bf16[1024,768]{1,0:T(8,128)(2,1)} %get-tuple-element.278.proj_ref, ...), custom_call_target="tpu_custom_call" | custom-call | tf_op jit(solution)/shard_map/pull/pallas_call | solution.py:298
  322.5 6.3 %pick_merge.1 = bf16[1024,1024]{1,0:T(8,128)(2,1)} custom-call(s32[4]{0:T(128)} %copy-done.14, bf16[8,4,256,128]{3,2,1,0:T(8,128)(2,1)} %bitcast.38), custom_call_target="tpu_custom_call" | custom-call | tf_op jit(solution)/shard_map/pick_merge/pallas_call | solution.py:381
  340.7 50.6 %finish.1 = (f32[24,128]{1,0:T(8,128)}, f32[8,128]{1,0:T(8,128)}, bf16[512,1024]{1,0:T(8,128)(2,1)}, bf16[256,384]{1,0:T(8,128)(2,1)}) custom-call(f32[24,128]{1,0:T(8,128)} %select_maximum_fusion.refs_0_, bf16[128,1024]{1,0:T(8,128)(2,1)} %reduce-scatter.5.cloned.1.call-done.refs_1_.merge_ref, bf16[256,1024]{1,0:T(8,128)(2,1)} %reduce-scatter.3.cloned.1.call-done.refs_2_, ...), custom_call_target="tpu_custom_call" | custom-call | tf_op jit(solution)/shard_map/finish/pallas_call | solution.py:858
  398.0 27.1 %adam_all.1 = (f32[1024,1024]{1,0:T(8,128)}, f32[1024,1024]{1,0:T(8,128)}, f32[1024,1024]{1,0:T(8,128)}, bf16[1024,1024]{1,0:T(8,128)(2,1)}, f32[1024,1024]{1,0:...) custom-call(f32[1,4]{1,0:T(1,128)} %maximum_bitcast_fusion.scale_ref, ...), custom_call_target="tpu_custom_call" | custom-call | tf_op jit(solution)/shard_map/adam_all/pallas_call | solution.py:940
  (136 shorter events, 93.8 us)
Async XLA Ops:
  7.2 48.5 %all-gather.8.cloned.1.call-start = ((), (), s32[]{:S(2)}) async-start(), calls=%async_computation.2 | async-start | bytes 1310720 | tf_op jit(solution)/shard_map/all_gather | solution.py:1016
  9.9 116.2 %all-gather.12.cloned.1.call-start = ((), (), s32[]{:S(2)}) async-start(), calls=%async_computation.6 | async-start | bytes 2359296 | tf_op jit(solution)/shard_map/all_gather | solution.py:1021
  10.0 42.9 %collective-permute-start = (bf16[512,1024]{1,0:T(8,128)(2,1)}, bf16[512,1024]{1,0:T(8,128)(2,1)S(1)}, u32[]{:S(2)}, u32[]{:S(2)}) collective-permute-start(bf16[512,1024]{1,0:T(8,128)(2,1)} %tokens_ref.3), channel_id=1, source_target_pairs={{0,1},{1,2},{2,3},{3,0},{4,5},{5,6},{6,7},{7,4},{8,9},{9,10},{10,1... | collective-permute-start | bytes 3145736 | tf_op jit(solution)/shard_map/ppermute | solution.py:1007
  22.5 40.0 %copy-start.14 = (s32[4]{0:T(128)}, s32[4]{0:T(128)S(1)}, u32[]{:S(2)}) copy-start(s32[4]{0:T(128)S(1)} %compare_select_fusion.slots_ref) | copy-start | bytes 52
  57.4 75.2 %all-gather.10.cloned.1.call-start = ((), (), s32[]{:S(2)}) async-start(), calls=%async_computation.5 | async-start | bytes 7077888 | tf_op jit(solution)/shard_map/all_gather | solution.py:1021
  59.6 226.2 %reduce-scatter.3.cloned.1.call-start = ((), (), s32[]{:S(2)}) async-start(), calls=%async_computation.3 | async-start | bytes 4718592 | tf_op jit(solution)/shard_map/reduce_scatter | solution.py:1103
  62.2 60.2 %copy-start = (bf16[1024,1024]{1,0:T(8,128)(2,1)}, bf16[1024,1024]{1,0:T(8,128)(2,1)S(1)}, u32[]{:S(2)}) copy-start(bf16[1024,1024]{1,0:T(8,128)(2,1)S(1)} %convert_element_type.86.down_ref) | copy-start | bytes 6291460
  62.4 27.0 %collective-permute-start.1 = (bf16[512,1024]{1,0:T(8,128)(2,1)S(1)}, bf16[512,1024]{1,0:T(8,128)(2,1)}, u32[]{:S(2)}, u32[]{:S(2)}) collective-permute-start(bf16[512,1024]{1,0:T(8,128)(2,1)S(1)} %collective-permute-done.tokens_ref), channel_id=1, source_target_pairs={{0,1},{1,2},{2,3},{3,0},{4,5},{5,6},{6,7},{7,4},{8,9},{9,10},{10,1... | collective-permute-start | bytes 3145736 | tf_op jit(solution)/shard_map/ppermute | solution.py:1007
  89.4 26.2 %collective-permute-start.2 = (bf16[512,1024]{1,0:T(8,128)(2,1)}, bf16[512,1024]{1,0:T(8,128)(2,1)S(1)}, u32[]{:S(2)}, u32[]{:S(2)}) collective-permute-start(bf16[512,1024]{1,0:T(8,128)(2,1)} %collective-permute-done.1.tokens_ref), channel_id=1, source_target_pairs={{0,1},{1,2},{2,3},{3,0},{4,5},{5,6},{6,7},{7,4},{8,9},{9,10},{10,1... | collective-permute-start | bytes 3145736 | tf_op jit(solution)/shard_map/ppermute | solution.py:1007
  115.6 25.6 %collective-permute-start.3 = (bf16[512,1024]{1,0:T(8,128)(2,1)}, bf16[512,1024]{1,0:T(8,128)(2,1)}, u32[]{:S(2)}, u32[]{:S(2)}) collective-permute-start(bf16[512,1024]{1,0:T(8,128)(2,1)} %grad_ref), channel_id=1, source_target_pairs={{0,1},{1,2},{2,3},{3,0},{4,5},{5,6},{6,7},{7,4},{8,9},{9,10},{10,1... | collective-permute-start | bytes 3145736 | tf_op jit(solution)/shard_map/ppermute | solution.py:1007
  141.3 27.1 %collective-permute-start.5 = (bf16[512,1024]{1,0:T(8,128)(2,1)}, bf16[512,1024]{1,0:T(8,128)(2,1)S(1)}, u32[]{:S(2)}, u32[]{:S(2)}) collective-permute-start(bf16[512,1024]{1,0:T(8,128)(2,1)} %collective-permute-done.3.grad_ref), channel_id=1, source_target_pairs={{0,1},{1,2},{2,3},{3,0},{4,5},{5,6},{6,7},{7,4},{8,9},{9,10},{10,1... | collective-permute-start | bytes 3145736 | tf_op jit(solution)/shard_map/ppermute | solution.py:1007
  168.4 27.8 %collective-permute-start.6 = (bf16[512,1024]{1,0:T(8,128)(2,1)S(1)}, bf16[512,1024]{1,0:T(8,128)(2,1)S(1)}, u32[]{:S(2)}, u32[]{:S(2)}) collective-permute-start(bf16[512,1024]{1,0:T(8,128)(2,1)S(1)} %collective-permute-done.5.grad_ref), channel_id=1, source_target_pairs={{0,1},{1,2},{2,3},{3,0},{4,5},{5,6},{6,7},{7,4},{8,9},{9,10},{10,1... | collective-permute-start | bytes 3145736 | tf_op jit(solution)/shard_map/ppermute | solution.py:1007
  169.3 51.8 %collective-permute-start.4 = (bf16[512,1024]{1,0:T(8,128)(2,1)}, bf16[512,1024]{1,0:T(8,128)(2,1)S(1)}, u32[]{:S(2)}, u32[]{:S(2)}) collective-permute-start(bf16[512,1024]{1,0:T(8,128)(2,1)} %convolution_convert_fusion), channel_id=1, source_target_pairs={{0,1},{1,2},{2,3},{3,0},{4,5},{5,6},{6,7},{7,4},{8,9},{9,10},{10,1... | collective-permute-start | bytes 3145736 | tf_op jit(solution)/shard_map/ppermute | solution.py:1007
  221.1 116.3 %reduce-scatter.5.cloned.1.call-start = ((), (), s32[]{:S(2)}) async-start(), calls=%async_computation.4 | async-start | bytes 2359296 | tf_op jit(solution)/shard_map/reduce_scatter | solution.py:1103
  224.0 61.8 %collective-permute-start.7 = (bf16[512,1024]{1,0:T(8,128)(2,1)}, bf16[512,1024]{1,0:T(8,128)(2,1)S(1)}, u32[]{:S(2)}, u32[]{:S(2)}) collective-permute-start(bf16[512,1024]{1,0:T(8,128)(2,1)} %add_convert_fusion.3), channel_id=1, source_target_pairs={{0,1},{1,2},{2,3},{3,0},{4,5},{5,6},{6,7},{7,4},{8,9},{9,10},{10,1... | collective-permute-start | bytes 3145736 | tf_op jit(solution)/shard_map/ppermute | solution.py:1007
  224.6 61.2 %collective-permute-start.10 = (bf16[512,256]{1,0:T(8,128)(2,1)}, bf16[512,256]{1,0:T(8,128)(2,1)}, u32[]{:S(2)}, u32[]{:S(2)}) collective-permute-start(bf16[512,256]{1,0:T(8,128)(2,1)} %get-tuple-element.265), channel_id=1, source_target_pairs={{0,3},{1,0},{2,1},{3,2},{4,7},{5,4},{6,5},{7,6},{8,11},{9,8},{10,9... | collective-permute-start | bytes 786440 | tf_op jit(solution)/shard_map/ppermute | solution.py:1148
  227.8 58.0 %collective-permute-start.8 = (bf16[512,256]{1,0:T(8,128)(2,1)}, bf16[512,256]{1,0:T(8,128)(2,1)}, u32[]{:S(2)}, u32[]{:S(2)}) collective-permute-start(bf16[512,256]{1,0:T(8,128)(2,1)} %get-tuple-element.263), channel_id=1, source_target_pairs={{0,1},{1,2},{2,3},{3,0},{4,5},{5,6},{6,7},{7,4},{8,9},{9,10},{10,1... | collective-permute-start | bytes 786440 | tf_op jit(solution)/shard_map/ppermute | solution.py:1148
  228.2 57.6 %collective-permute-start.9 = (bf16[512,256]{1,0:T(8,128)(2,1)}, bf16[512,256]{1,0:T(8,128)(2,1)}, u32[]{:S(2)}, u32[]{:S(2)}) collective-permute-start(bf16[512,256]{1,0:T(8,128)(2,1)} %get-tuple-element.264), channel_id=1, source_target_pairs={{0,2},{1,3},{2,0},{3,1},{4,6},{5,7},{6,4},{7,5},{8,10},{9,11},{10,... | collective-permute-start | bytes 786440 | tf_op jit(solution)/shard_map/ppermute | solution.py:1148
  285.9 112.1 %all-gather.14.cloned.1.call-start = ((), (), s32[]{:S(2)}) async-start(), calls=%async_computation.7 | async-start | bytes 4718592 | tf_op jit(solution)/shard_map/all_gather | solution.py:1189
  288.7 22.7 %collective-permute-start.11 = (bf16[512,1024]{1,0:T(8,128)(2,1)}, bf16[512,1024]{1,0:T(8,128)(2,1)S(1)}, u32[]{:S(2)}, u32[]{:S(2)}) collective-permute-start(bf16[512,1024]{1,0:T(8,128)(2,1)} %add_convert_fusion.2), channel_id=1, source_target_pairs={{0,1},{1,2},{2,3},{3,0},{4,5},{5,6},{6,7},{7,4},{8,9},{9,10},{10,1... | collective-permute-start | bytes 3145736 | tf_op jit(solution)/shard_map/ppermute | solution.py:1007
  314.8 22.5 %collective-permute-start.12 = (bf16[512,1024]{1,0:T(8,128)(2,1)}, bf16[512,1024]{1,0:T(8,128)(2,1)}, u32[]{:S(2)}, u32[]{:S(2)}) collective-permute-start(bf16[512,1024]{1,0:T(8,128)(2,1)} %convert_element_type.99), channel_id=1, source_target_pairs={{0,1},{1,2},{2,3},{3,0},{4,5},{5,6},{6,7},{7,4},{8,9},{9,10},{10,1... | collective-permute-start | bytes 3145736 | tf_op jit(solution)/shard_map/ppermute | solution.py:1007
  337.4 54.0 %copy-start.9 = (f32[512,1024]{1,0:T(8,128)S(1)}, f32[512,1024]{1,0:T(8,128)}, u32[]{:S(2)}) copy-start(f32[512,1024]{1,0:T(8,128)} %get-tuple-element.300) | copy-start | bytes 6291460
  393.9 31.2 %collective-permute-start.13 = (bf16[512,1024]{1,0:T(8,128)(2,1)}, bf16[512,1024]{1,0:T(8,128)(2,1)}, u32[]{:S(2)}, u32[]{:S(2)}) collective-permute-start(bf16[512,1024]{1,0:T(8,128)(2,1)} %add_convert_fusion), channel_id=1, source_target_pairs={{0,1},{1,2},{2,3},{3,0},{4,5},{5,6},{6,7},{7,4},{8,9},{9,10},{10,1... | collective-permute-start | bytes 3145736 | tf_op jit(solution)/shard_map/ppermute | solution.py:1007
  398.0 27.2 %copy-start.3 = (f32[512,1024]{1,0:T(8,128)S(1)}, f32[512,1024]{1,0:T(8,128)}, u32[]{:S(2)}) copy-start(f32[512,1024]{1,0:T(8,128)} %get-tuple-element.314) | copy-start | bytes 6291460
  (15 other events, 71.4 us)
Sparse Core Ops, SparseCore 0:
  10.2 45.5 all-gather.7
  58.2 26.5 all-gather.11
  87.2 45.3 all-gather.9
  221.2 50.0 reduce-scatter.2
  286.0 41.0 reduce-scatter.4
  328.9 36.7 all-gather.13

commit v2 on v1

--- a/solution.py
+++ b/solution.py
@@ -45,6 +45,14 @@
     return lax.dot_general(
         left_side, right_side, (((0,), (0,)), ((), ())), preferred_element_type=jnp.float32
     )
+
+
+def in_chunks(total, chunk, body):
+    def step(index, carry):
+        body(pl.ds(pl.multiple_of(index * chunk, chunk), chunk))
+        return carry
+
+    lax.fori_loop(0, total // chunk, step, 0)
 
 
 def locate(lengths, token_index):
@@ -124,13 +132,15 @@
     unit, unused = normalize(tokens_ref[...])
     normed_ref[...] = (unit * params_ref[0:1, :] + params_ref[1:2, :]).astype(jnp.bfloat16)
     width = act_ref.shape[1]
-    step = min(256, width)
-    for first in range(0, width, step):
-        hidden = dot_plain(normed_ref[...], weight_ref[:, first : first + step])
+
+    def column(cols):
+        hidden = dot_plain(normed_ref[...], weight_ref[:, cols])
         share = 0.5 + 0.5 * lax.erf(hidden * math.sqrt(0.5))
         bell = jnp.exp(hidden * hidden * -0.5) * (1.0 / math.sqrt(2.0 * math.pi))
-        act_ref[:, first : first + step] = (hidden * share).astype(jnp.bfloat16)
-        slope_ref[:, first : first + step] = share + hidden * bell
+        act_ref[:, cols] = (hidden * share).astype(jnp.bfloat16)
+        slope_ref[:, cols] = share + hidden * bell
+
+    in_chunks(width, min(256, width), column)
 
 
 def feed(slot, slots, tokens, params, weight, held):
@@ -162,35 +172,64 @@
     )(tokens, params, weight, *held)
 
 
+def down_kernel(active_ref, down_ref, out_ref):
+    def column(cols):
+        out_ref[:, cols] = dot_plain(active_ref[...], down_ref[:, cols]).astype(out_ref.dtype)
+
+    in_chunks(out_ref.shape[1], 256, column)
+
+
+def down_term(slot, slots, activated, down, kept):
+    rows = activated.shape[0] // slots
+    width, depth = down.shape
+    half = rows // 2
+    return pl.pallas_call(
+        down_kernel,
+        out_shape=jax.ShapeDtypeStruct((rows, depth), kept),
+        grid=(2,),
+        in_specs=[
+            pl.BlockSpec((half, width), lambda i: (2 * slot + i, 0)),
+            pl.BlockSpec((width, depth), lambda i: (0, 0)),
+        ],
+        out_specs=pl.BlockSpec((half, depth), lambda i: (i, 0)),
+        cost_estimate=short,
+        name="down_term",
+    )(activated, down)
+
+
 def outer_kernel(split, first_left, first_right, second_left, second_right, out_ref, first, second):
-    step = pl.program_id(0)
+    begun = pl.program_id(0) > 0
     for left_ref, right_ref, total in (
         (first_left, first_right, first),
         (second_left, second_right, second),
     ):
-        term = dot_first(left_ref[...], right_ref[...])
-
-        @pl.when(step == 0)
-        def _():
-            total[...] = term
-
-        @pl.when(step > 0)
-        def _():
-            total[...] += term
-
-    @pl.when(step == pl.num_programs(0) - 1)
+
+        def chunk(rows):
+            term = dot_first(left_ref[:, rows], right_ref[...])
+            total[rows, :] = jnp.where(begun, total[rows, :], 0.0) + term
+
+        in_chunks(total.shape[0], 512, chunk)
+
+    @pl.when(pl.program_id(0) == pl.num_programs(0) - 1)
     def _():
         if split:
             blocks, unused, rows, cols = out_ref.shape
-            for matrix, total in enumerate((first, second)):
-                for block in range(blocks):
-                    out_ref[block, matrix] = total[block * rows : (block + 1) * rows, :].astype(
-                        jnp.bfloat16
-                    )
+
+            def write(block, carry):
+                at = pl.ds(pl.multiple_of(block * rows, rows), rows)
+                out_ref[block, 0] = first[at, :].astype(jnp.bfloat16)
+                out_ref[block, 1] = second[at, :].astype(jnp.bfloat16)
+                return carry
+
+            lax.fori_loop(0, blocks, write, 0)
         else:
             width = first.shape[1]
-            out_ref[:, :width] = first[...].astype(jnp.bfloat16)
-            out_ref[:, width:] = second[...].astype(jnp.bfloat16)
+
+            def write_rows(rows):
+                out_ref[rows, :width] = first[rows, :].astype(jnp.bfloat16)
+                out_ref[rows, width:] = second[rows, :].astype(jnp.bfloat16)
+
+            in_chunks(first.shape[0], 128, write_rows)
 
 
 def outer(blocks, first_left, first_right, second_left, second_right):
@@ -224,7 +263,12 @@
 
     grads = grad_ref[...]
     all_ref[...] = grads
-    hidden_ref[...] = (dot_last(grads, down_ref[...]) * slope_ref[...]).astype(jnp.bfloat16)
+
+    def column(cols):
+        hidden = dot_last(grad_ref[...], down_ref[cols, :]) * slope_ref[:, cols]
+        hidden_ref[:, cols] = hidden.astype(jnp.bfloat16)
+
+    in_chunks(down_ref.shape[0], min(512, down_ref.shape[0]), column)
     attended_ref[...] = dot_last(grads, merge_own[...]).astype(jnp.bfloat16)
 
 
@@ -275,30 +319,30 @@
     )(span_index.reshape(1), grads, slope, down, merge, *held)
 
 
-def pull_kernel(mixed_ref, hidden_ref, proj_ref, up_ref, tokens_ref, out_ref, sums_ref):
-    partial_grad = dot_last(mixed_ref[...], proj_ref[...]) + dot_last(hidden_ref[...], up_ref[...])
-    out_ref[...] = partial_grad
-    unit, unused = normalize(tokens_ref[...])
-    gain = jnp.sum(partial_grad * unit, axis=0, keepdims=True)
-    bias = jnp.sum(partial_grad, axis=0, keepdims=True)
-    both = jnp.concatenate([gain, bias], axis=0)
-
-    @pl.when(pl.program_id(0) == 0)
-    def _():
-        sums_ref[...] = both
-
-    @pl.when(pl.program_id(0) > 0)
-    def _():
-        sums_ref[...] += both
-
-
-def pull(slot, mixed, hidden_grad, proj, up, tokens):
+def pull_kernel(mixed_ref, hidden_ref, proj_ref, up_ref, tokens_ref, out_ref, sums_ref, unit_ref):
+    unit_ref[...] = normalize(tokens_ref[...])[0]
+    begun = pl.program_id(0) > 0
+
+    def column(cols):
+        partial_grad = dot_last(mixed_ref[...], proj_ref[cols, :]) + dot_last(
+            hidden_ref[...], up_ref[cols, :]
+        )
+        out_ref[:, cols] = partial_grad.astype(out_ref.dtype)
+        gain = jnp.sum(partial_grad * unit_ref[:, cols], axis=0, keepdims=True)
+        bias = jnp.sum(partial_grad, axis=0, keepdims=True)
+        both = jnp.concatenate([gain, bias], axis=0)
+        sums_ref[:, cols] = jnp.where(begun, sums_ref[:, cols], 0.0) + both
+
+    in_chunks(proj_ref.shape[0], 256, column)
+
+
+def pull(slot, mixed, hidden_grad, proj, up, tokens, kept):
     rows, depth = tokens.shape
     half = rows // 2
     return pl.pallas_call(
         pull_kernel,
         out_shape=(
-            jax.ShapeDtypeStruct((rows, depth), jnp.float32),
+            jax.ShapeDtypeStruct((rows, depth), kept),
             jax.ShapeDtypeStruct((2, depth), jnp.float32),
         ),
         grid=(2,),
@@ -313,6 +357,7 @@
             pl.BlockSpec((half, depth), lambda i: (i, 0)),
             pl.BlockSpec((2, depth), lambda i: (0, 0)),
         ),
+        scratch_shapes=[pltpu.VMEM((half, depth), jnp.float32)],
         cost_estimate=short,
         name="pull",
     )(mixed, hidden_grad, proj, up, tokens)
@@ -889,33 +934,35 @@
     scales = (scale_ref[0, 2], scale_ref[0, 3])
     clip_factor = stats_ref[0:1, 0:1]
 
-    def update(matrix, gradient, step_rate, decay_coef):
-        state = [ref[...] for ref in states[3 * matrix : 3 * matrix + 3]]
+    def update(matrix, rows, gradient, step_rate, decay_coef):
+        state = [ref[rows, :] for ref in states[3 * matrix : 3 * matrix + 3]]
         new = adam_step(*state, gradient * clip_factor, step_rate, decay_coef, scales)
         for out_ref, value in zip(outs[4 * matrix : 4 * matrix + 3], new):
-            out_ref[...] = value
-        return new[0]
-
-    for matrix in range(2):
-        gradient = grads_ref[0, matrix].astype(jnp.float32)
-        weight = update(matrix, gradient, matrix_step, decay_rate)
-        outs[4 * matrix + 3][...] = weight.astype(jnp.bfloat16)
+            out_ref[rows, :] = value
+        if matrix < 4:
+            outs[4 * matrix + 3][rows, :] = new[0].astype(jnp.bfloat16)
+
+    def feed_rows(rows):
+        for matrix in range(2):
+            gradient = grads_ref[0, matrix, rows, :].astype(jnp.float32)
+            update(matrix, rows, gradient, matrix_step, decay_rate)
+
+    in_chunks(states[0].shape[0], 32, feed_rows)
 
     @pl.when(pl.program_id(0) == 0)
     def _():
-        for matrix, gradient in (
-            (2, proj_ref[...].astype(jnp.float32)),
-            (3, merge_ref[...].astype(jnp.float32).T),
-        ):
-            weight = update(matrix, gradient, matrix_step, decay_rate)
-            outs[4 * matrix + 3][...] = weight.astype(jnp.bfloat16)
+        def proj_rows(rows):
+            update(2, rows, proj_ref[rows, :].astype(jnp.float32), matrix_step, decay_rate)
+
+        in_chunks(proj_ref.shape[0], 64, proj_rows)
+        update(3, slice(None), merge_ref[...].astype(jnp.float32).T, matrix_step, decay_rate)
         per_row = D // LANES
         for k in range(2 * per_row):
             at = k % per_row
             norm_grads[k // per_row : k // per_row + 1, at * LANES : (at + 1) * LANES] = total_ref[
                 k : k + 1, :
             ]
-        update(4, norm_grads[...], norm_step, 0.0)
+        update(4, slice(None), norm_grads[...], norm_step, 0.0)
         outs[19][...] = norm_grads[...] * clip_factor
 
 
@@ -956,6 +1003,30 @@
         cost_estimate=short,
         name="adam_all",
     )(scales, stats, grads_all, total, proj_block, heads_part, *states)
+
+
+def settle_kernel(arrived_ref, term_ref, tokens_ref, cotangent_ref, params_ref, out_ref):
+    unit, inv_std = normalize(tokens_ref[...])
+    unit_grad = (arrived_ref[...].astype(jnp.float32) + term_ref[...]) * params_ref[0:1, :]
+    out_ref[...] = cotangent_ref[...].astype(jnp.float32) + inv_std * (
+        unit_grad
+        - jnp.mean(unit_grad, axis=1, keepdims=True)
+        - unit * jnp.mean(unit_grad * unit, axis=1, keepdims=True)
+    )
+
+
+def settle(arrived, term, tokens, cotangent, params):
+    rows, depth = tokens.shape
+    block = pl.BlockSpec((rows // 8, depth), lambda i: (i, 0))
+    return pl.pallas_call(
+        settle_kernel,
+        out_shape=jax.ShapeDtypeStruct((rows, depth), jnp.float32),
+        grid=(8,),
+        in_specs=[block] * 4 + [pl.BlockSpec((2, depth), lambda i: (0, 0))],
+        out_specs=block,
+        cost_estimate=short,
+        name="settle",
+    )(arrived, term, tokens, cotangent, params)
 
 
 def shards(
@@ -1022,9 +1093,6 @@
             wide_count, narrow_count, shard_rows, -1
         )
 
-    def down_term(rows, slot):
-        return dot_plain(rows_of(rows, slot), down_slice)
-
     order = list(range(1, narrow_count)) + [0]
     pairs = held_width // LANES
     token_blocks = [tokens]
@@ -1035,13 +1103,27 @@
         if slot > 0:
             ready = [slot - 1, slot] if slot == narrow_count - 2 else [slot - 1]
             for block in ready:
-                term = down_term(held[1], block)
-                branch_terms.append(term.astype(jnp.bfloat16) if block == 1 else term)
+                kept = jnp.bfloat16 if block == 1 else jnp.float32
+                branch_terms.append(down_term(block, narrow_count, held[1], down_slice, kept))
+            if slot == 2:
+                if direct:
+                    merge_turn = pick_merge(merge_all, slots, own_width)
+                else:
+                    merge_turn = jnp.take(
+                        jnp.transpose(merge_all, (1, 2, 0, 3)).reshape(
+                            narrow_count, own_width, D
+                        ),
+                        slots,
+                        axis=0,
+                    ).reshape(D, D)
+                moving, merge_turn = meet(moving, merge_turn)
             moving, held, branch_terms, down_slice = meet(moving, held, branch_terms, down_slice)
         else:
             moving, held = meet(moving, held)
         if slot == 0:
-            lengths, slots, moving, weight_rows = meet(lengths, slots, moving, weight_rows)
+            lengths, slots, moving, weight_rows, down_slice = meet(
+                lengths, slots, moving, weight_rows, down_slice
+            )
             proj_all = wide_all(weight_rows[:, :proj_cols])
             merge_all = wide_all(weight_rows[:, proj_cols:])
             branch_terms = []
@@ -1093,7 +1175,9 @@
         )
 
     push_held = push_slot(0, ())
-    branch_terms.append(down_term(activated, narrow_count - 1))
+    branch_terms.append(
+        down_term(narrow_count - 1, narrow_count, activated, down_slice, jnp.float32)
+    )
     moving, packed, activated, slope, push_held, branch_terms = meet(
         moving, packed, activated, slope, push_held, branch_terms
     )
@@ -1155,7 +1239,10 @@
 
     def pull_more(count, mixed, norm_part):
         for slot in order[len(terms) : len(terms) + count]:
-            term, sums = pull(slot, mixed, hidden_grad, proj_own, up_slice, token_blocks[slot])
+            kept = jnp.float32 if terms else jnp.bfloat16
+            term, sums = pull(
+                slot, mixed, hidden_grad, proj_own, up_slice, token_blocks[slot], kept
+            )
             terms.append(term)
             norm_part = norm_part + sums
         return norm_part
@@ -1182,27 +1269,16 @@
             heads_part = wide_sum(heads_grad)
         else:
             norm_part = pull_more(3, mixed_grad, norm_part)
-            moving, terms, norm_part, merge_all, slots, feed_part = meet(
-                moving, terms, norm_part, merge_all, slots, feed_part
-            )
+            moving, terms, norm_part, feed_part = meet(moving, terms, norm_part, feed_part)
         if place == narrow_count - 3:
             feed_all = lax.all_gather(feed_part, "wide", axis=0).reshape(
                 wide_count, 2, part_rows, -1
             )
     branch_moving = moving
-    moving = send_on(terms[0].astype(jnp.bfloat16))
+    moving = send_on(terms[0])
     norm_part = pull_more(narrow_count, mixed_grad, norm_part)
     branch = branch_moving.astype(jnp.float32) + branch_terms[0]
-    if direct:
-        merge_turn = pick_merge(merge_all, slots, own_width)
-    else:
-        merge_turn = jnp.take(
-            jnp.transpose(merge_all, (1, 2, 0, 3)).reshape(narrow_count, own_width, D),
-            slots,
-            axis=0,
-        ).reshape(D, D)
     merged = dot_plain(jnp.concatenate(pieces, axis=1), merge_turn)
-    unit_rows, inv_std = normalize(tokens)
     output_rows = tokens.astype(jnp.float32) + merged + branch
     layer_out = output_rows.astype(jnp.bfloat16)
 
@@ -1277,13 +1353,7 @@
         updated[4 * k : 4 * k + 4] for k in range(5)
     ]
     moving, new_up = meet(moving, new_up)
-    normed_grad = moving.astype(jnp.float32) + terms[-1]
-    unit_grad = normed_grad * norm_params[0]
-    input_grad = cotangent.astype(jnp.float32) + inv_std * (
-        unit_grad
-        - jnp.mean(unit_grad, axis=1, keepdims=True)
-        - unit_rows * jnp.mean(unit_grad * unit_rows, axis=1, keepdims=True)
-    )
+    input_grad = settle(moving, terms[-1], tokens, cotangent, norm_params)
     return (
         layer_out,
         input_grad,

time: 443 us -> 433 us (0.977)
  Pallas kernels: 275 us -> 298 us
  matrix products: 18.2 us -> 4.55 us
  waiting for transfers between devices: 58.7 us -> 49.4 us
  other arithmetic: 41.6 us -> 35.1 us
    pallas_call x0 -> x5, Pallas kernels: none -> 28.7 us  [the longest x4 21.4 us: down_term(): pl.pallas_call(down_kernel, out_shape=jax.ShapeDtypeStruct((rows, depth),...]
    dot_general x5 -> x1, matrix products: 18.2 us -> 4.55 us  [dot_plain(): lax.dot_general(left_side, right_side, (((1,), (0,)), ((), ())), preferre...]
    pallas_call x2, Pallas kernels: 40.4 us -> 28.3 us  [attend(): pl.pallas_call(partial(attend_kernel, block_q, block_k, heads_in), out_sh...]
    pallas_call x1, Pallas kernels: 43.6 us -> 34.1 us  [attend_back(): pl.pallas_call(partial(attend_back_kernel, block_q, block_k, heads_in), o...]
    ppermute x11, waiting for transfers between devices: 54.3 us -> 45.8 us  [send_on(): return lax.ppermute(array, 'narrow', onward)]
    pallas_call x4, Pallas kernels: 24.9 us -> 32.7 us  [pull(): pl.pallas_call(pull_kernel, out_shape=(jax.ShapeDtypeStruct((rows, depth)...]
    pallas_call x4, Pallas kernels: 22.8 us -> 27.7 us  [feed(): pl.pallas_call(feed_kernel, out_shape=(jax.ShapeDtypeStruct((slots * rows...]
  transfers between devices with their start and end apart: 20 -> 20, of which waited for: 8 -> 7; matrix products, arithmetic and copies ran while one was open for 13% -> 10% of each run, Pallas kernels for 63% -> 67%
where the time goes in v2:
time: 433 us; the launch traced here: 432 us
  Pallas kernels  298 us (69%)
  waiting for transfers between devices  49.4 us (11%)
  other arithmetic  35.1 us (8%)
  starting transfers between devices  17 us (4%)
  between operations  15.2 us (4%)
  local copies, waits for them, and re-layouts  12.9 us (3%)
  matrix products  4.55 us (1%)
    pallas_call x1, Pallas kernels, finish(): pl.pallas_call(partial(finish_kernel, narrow_count, wide_count, own_units...  54.8 us
    ppermute x11, waiting for transfers between devices, send_on(): return lax.ppermute(array, 'narrow', onward)  45.8 us
    pallas_call x1, Pallas kernels, attend_back(): pl.pallas_call(partial(attend_back_kernel, block_q, block_k, heads_in), o...  34.1 us
    pallas_call x4, Pallas kernels, pull(): pl.pallas_call(pull_kernel, out_shape=(jax.ShapeDtypeStruct((rows, depth)...  32.7 us
    pallas_call x2, Pallas kernels, outer(): pl.pallas_call(partial(outer_kernel, bool(blocks)), out_shape=jax.ShapeDt...  28.6 us
    pallas_call x2, Pallas kernels, attend(): pl.pallas_call(partial(attend_kernel, block_q, block_k, heads_in), out_sh...  28.3 us
    pallas_call x4, Pallas kernels, feed(): pl.pallas_call(feed_kernel, out_shape=(jax.ShapeDtypeStruct((slots * rows...  27.7 us
    pallas_call x1, Pallas kernels, adam_all(): pl.pallas_call(adam_kernel, out_shape=tuple(shapes), grid=(count,), in_sp...  25.4 us
  transfers between devices with their start and end apart: 20, of which 7 were waited for; matrix products, arithmetic and copies ran while one was open for 10% of the time, Pallas kernels for 67%

profile of v2, /device:TPU:0, one launch (start us, length us, event | category | flops | bytes accessed | tf_op | source)
XLA Modules:
  0.0 432.3 jit_solution(3040710959539429448)
XLA Ops:
  20.8 6.9 %feed.4 = (bf16[2048,1024]{1,0:T(8,128)(2,1)}, bf16[2048,1024]{1,0:T(8,128)(2,1)}, f32[2048,1024]{1,0:T(8,128)}) custom-call(bf16[512,1024]{1,0:T(8,128)(2,1)} %tokens_ref.5, f32[2,1024]{1,0:T(2,128)} %params_ref.9, bf16[1024,1024]{1,0:T(8,128)(2,1)} %convert_element_type.70.weight_ref.up_ref), custom_call_target="tpu_custom_call" | custom-call | tf_op jit(solution)/shard_map/feed/pallas_call | solution.py:150
  27.7 25.3 %collective-permute-done.tokens_ref = bf16[512,1024]{1,0:T(8,128)(2,1)S(1)} collective-permute-done((bf16[512,1024]{1,0:T(8,128)(2,1)}, bf16[512,1024]{1,0:T(8,128)(2,1)S(1)}, u32[]{:S(2)}, u32[]{:S(2)}) %collective-permute-start) | collective-permute-done | bytes 1048608 | tf_op jit(solution)/shard_map/ppermute | solution.py:1078
  60.0 6.9 %feed.5 = (bf16[2048,1024]{1,0:T(8,128)(2,1)}, bf16[2048,1024]{1,0:T(8,128)(2,1)}, f32[2048,1024]{1,0:T(8,128)}) custom-call(bf16[512,1024]{1,0:T(8,128)(2,1)} %copy-done.5, f32[2,1024]{1,0:T(2,128)} %params_ref.9, bf16[1024,1024]{1,0:T(8,128)(2,1)} %convert_element_type.70.weight_ref.up_ref, ...), custom_call_target="tpu_custom_call", output_to_operand_aliasing={{0}: (3, {}), {1}: (4, {}), {2}: (5, {})} | custom-call | tf_op jit(solution)/shard_map/feed/pallas_call | solution.py:150
  79.9 6.9 %collective-permute-done.1.tokens_ref = bf16[512,1024]{1,0:T(8,128)(2,1)S(1)} collective-permute-done((bf16[512,1024]{1,0:T(8,128)(2,1)S(1)}, bf16[512,1024]{1,0:T(8,128)(2,1)S(1)}, u32[]{:S(2)}, u32[]{:S(2)}) %collective-permute-start.1) | collective-permute-done | bytes 1048608 | tf_op jit(solution)/shard_map/ppermute | solution.py:1078
  87.8 6.9 %feed.6 = (bf16[2048,1024]{1,0:T(8,128)(2,1)}, bf16[2048,1024]{1,0:T(8,128)(2,1)}, f32[2048,1024]{1,0:T(8,128)}) custom-call(bf16[512,1024]{1,0:T(8,128)(2,1)} %copy-done.6, f32[2,1024]{1,0:T(2,128)} %params_ref.9, bf16[1024,1024]{1,0:T(8,128)(2,1)} %convert_element_type.70.weight_ref.up_ref, ...), custom_call_target="tpu_custom_call", output_to_operand_aliasing={{0}: (3, {}), {1}: (4, {}), {2}: (5, {})} | custom-call | tf_op jit(solution)/shard_map/feed/pallas_call | solution.py:150
  105.5 6.5 %pick_merge.1 = bf16[1024,1024]{1,0:T(8,128)(2,1)} custom-call(s32[4]{0:T(128)} %copy-done.16, bf16[8,4,256,128]{3,2,1,0:T(8,128)(2,1)} %bitcast.29), custom_call_target="tpu_custom_call" | custom-call | tf_op jit(solution)/shard_map/pick_merge/pallas_call | solution.py:426
  113.7 7.0 %feed.7 = (bf16[2048,1024]{1,0:T(8,128)(2,1)}, bf16[2048,1024]{1,0:T(8,128)(2,1)}, f32[2048,1024]{1,0:T(8,128)}) custom-call(bf16[512,1024]{1,0:T(8,128)(2,1)} %copy-done.7, f32[2,1024]{1,0:T(2,128)} %params_ref.9, bf16[1024,1024]{1,0:T(8,128)(2,1)} %convert_element_type.70.weight_ref.up_ref, ...), custom_call_target="tpu_custom_call", output_to_operand_aliasing={{0}: (3, {}), {1}: (4, {}), {2}: (5, {})} | custom-call | tf_op jit(solution)/shard_map/feed/pallas_call | solution.py:150
  126.1 5.8 %push.4 = (bf16[2048,1024]{1,0:T(8,128)(2,1)}, bf16[2048,1024]{1,0:T(8,128)(2,1)}, bf16[2048,256]{1,0:T(8,128)(2,1)}) custom-call(s32[1]{0:T(128)} %bitcast.4.index_ref, bf16[512,1024]{1,0:T(8,128)(2,1)} %cotangent_ref.1, f32[2048,1024]{1,0:T(8,128)} %get-tuple-element.234.slope_ref, bf16[1024,1024]{1,0:T(8,128)(2,1)} %convert_element_type.73.down_ref, ...), custom_call_target="tpu_custom_call" | custom-call | tf_op jit(solution)/shard_map/push/pallas_call | solution.py:292
  132.6 8.4 %project_all.1 = (bf16[2048,768]{1,0:T(8,128)(2,1)}, bf16[1024,768]{1,0:T(8,128)(2,1)}) custom-call(s32[1]{0:T(128)} %bitcast.4.index_ref, bf16[2048,1024]{1,0:T(8,128)(2,1)} %get-tuple-element.213.rows_ref.first_left, f32[2048,128]{1,0:T(8,128)} %get-tuple-element.214.cos_ref, f32[2048,128]{1,0:T(8,128)} %get-tuple-element.215.sin_ref, ...), custom_call_target="tpu_custom_call" | custom-call | tf_op jit(solution)/shard_map/project_all/pallas_call | solution.py:390
  148.4 14.2 %attend.2 = (bf16[2048,256]{1,0:T(8,128)(2,1)}, f32[256,2048]{1,0:T(8,128)}, f32[2,8,2048]{2,1,0:T(8,128)}) custom-call(s32[4]{0:T(128)} %copy-done.16, s32[4]{0:T(128)} %select_reduce_fusion.3.first_ref, s32[4]{0:T(128)} %get-tuple-element.229.last_ref, s32[1,2048]{1,0:T(1,128)} %bitcast.36, ...), custom_call_target="tpu_custom_call" | custom-call | tf_op jit(solution)/shard_map/attend/pallas_call | solution.py:542
  162.6 5.9 %collective-permute-done.5.grad_ref = bf16[512,1024]{1,0:T(8,128)(2,1)S(1)} collective-permute-done((bf16[512,1024]{1,0:T(8,128)(2,1)}, bf16[512,1024]{1,0:T(8,128)(2,1)S(1)}, u32[]{:S(2)}, u32[]{:S(2)}) %collective-permute-start.5) | collective-permute-done | bytes 1048608 | tf_op jit(solution)/shard_map/ppermute | solution.py:1078
  169.7 5.7 %push.6 = (bf16[2048,1024]{1,0:T(8,128)(2,1)}, bf16[2048,1024]{1,0:T(8,128)(2,1)}, bf16[2048,256]{1,0:T(8,128)(2,1)}) custom-call(s32[1]{0:T(128)} %bitcast.4.index_ref, bf16[512,1024]{1,0:T(8,128)(2,1)} %copy-done.11, f32[2048,1024]{1,0:T(8,128)} %get-tuple-element.234.slope_ref, ...), custom_call_target="tpu_custom_call", output_to_operand_aliasing={{0}: (5, {}), {1}: (6, {}), {2}: (7, {})} | custom-call | tf_op jit(solution)/shard_map/push/pallas_call | solution.py:292
  175.4 14.1 %attend.3 = (bf16[2048,256]{1,0:T(8,128)(2,1)}, f32[256,2048]{1,0:T(8,128)}, f32[2,8,2048]{2,1,0:T(8,128)}) custom-call(s32[4]{0:T(128)} %copy-done.16, s32[4]{0:T(128)} %select_reduce_fusion.3.first_ref, s32[4]{0:T(128)} %get-tuple-element.229.last_ref, s32[1,2048]{1,0:T(1,128)} %bitcast.37, ...), custom_call_target="tpu_custom_call", output_to_operand_aliasing={{0}: (7, {}), {1}: (8, {}), {2}: (9, {})} | custom-call | tf_op jit(solution)/shard_map/attend/pallas_call | solution.py:542
  189.5 6.9 %collective-permute-done.6.grad_ref = bf16[512,1024]{1,0:T(8,128)(2,1)S(1)} collective-permute-done((bf16[512,1024]{1,0:T(8,128)(2,1)S(1)}, bf16[512,1024]{1,0:T(8,128)(2,1)S(1)}, u32[]{:S(2)}, u32[]{:S(2)}) %collective-permute-start.6) | collective-permute-done | bytes 1048608 | tf_op jit(solution)/shard_map/ppermute | solution.py:1078
  203.0 16.9 %outer.2 = bf16[8,2,128,1024]{3,2,1,0:T(8,128)(2,1)} custom-call(bf16[2048,1024]{1,0:T(8,128)(2,1)} %get-tuple-element.213.rows_ref.first_left, bf16[2048,1024]{1,0:T(8,128)(2,1)} %get-tuple-element.259.first_right.hidden_ref, bf16[2048,1024]{1,0:T(8,128)(2,1)} %get-tuple-element.260.active_ref.second_left, ...), custom_call_target="tpu_custom_call" | custom-call | tf_op jit(solution)/shard_map/outer/pallas_call | solution.py:241
  229.3 34.1 %attend_back.1.first_right.mixed_ref = bf16[2048,768]{1,0:T(8,128)(2,1)} custom-call(s32[4]{0:T(128)} %copy-done.16, s32[4]{0:T(128)} %get-tuple-element.229.last_ref, s32[4]{0:T(128)} %get-tuple-element.269.end_ref, s32[1,2048]{1,0:T(1,128)} %bitcast.38, f32[2048,128]{1,0:T(8,128)} %get-tuple-element.214.cos_ref, f32[2048,128]{1,0:T(8,128)} %get-tuple-element.215.sin_ref, ...), custom_call_target="tpu_custom_call" | custom-call | tf_op jit(solution)/shard_map/attend_back/pallas_call | solution.py:687
  263.4 11.7 %outer.3 = bf16[1024,1024]{1,0:T(8,128)(2,1)} custom-call(bf16[2048,1024]{1,0:T(8,128)(2,1)} %get-tuple-element.213.rows_ref.first_left, bf16[2048,768]{1,0:T(8,128)(2,1)} %attend_back.1.first_right.mixed_ref, bf16[2048,1024]{1,0:T(8,128)(2,1)} %get-tuple-element.261.second_right.second_left, bf16[2048,256]{1,0:T(8,128)(2,1)} %get-tuple-element.254.second_right), custom_call_target="tpu_custom_call" | custom-call | tf_op jit(solution)/shard_map/outer/pallas_call | solution.py:241
  281.8 8.1 %pull.6 = (f32[512,1024]{1,0:T(8,128)}, f32[2,1024]{1,0:T(2,128)}) custom-call(bf16[2048,768]{1,0:T(8,128)(2,1)} %attend_back.1.first_right.mixed_ref, bf16[2048,1024]{1,0:T(8,128)(2,1)} %get-tuple-element.259.first_right.hidden_ref, bf16[1024,768]{1,0:T(8,128)(2,1)} %get-tuple-element.282.proj_ref, ...), custom_call_target="tpu_custom_call" | custom-call | tf_op jit(solution)/shard_map/pull/pallas_call | solution.py:342
  289.9 8.3 %pull.5 = (f32[512,1024]{1,0:T(8,128)}, f32[2,1024]{1,0:T(2,128)}) custom-call(bf16[2048,768]{1,0:T(8,128)(2,1)} %attend_back.1.first_right.mixed_ref, bf16[2048,1024]{1,0:T(8,128)(2,1)} %get-tuple-element.259.first_right.hidden_ref, bf16[1024,768]{1,0:T(8,128)(2,1)} %get-tuple-element.282.proj_ref, ...), custom_call_target="tpu_custom_call" | custom-call | tf_op jit(solution)/shard_map/pull/pallas_call | solution.py:342
  298.3 8.1 %pull.4 = (bf16[512,1024]{1,0:T(8,128)(2,1)}, f32[2,1024]{1,0:T(2,128)}) custom-call(bf16[2048,768]{1,0:T(8,128)(2,1)} %attend_back.1.first_right.mixed_ref, bf16[2048,1024]{1,0:T(8,128)(2,1)} %get-tuple-element.259.first_right.hidden_ref, bf16[1024,768]{1,0:T(8,128)(2,1)} %get-tuple-element.282.proj_ref, ...), custom_call_target="tpu_custom_call" | custom-call | tf_op jit(solution)/shard_map/pull/pallas_call | solution.py:342
  308.5 8.2 %pull.7 = (f32[512,1024]{1,0:T(8,128)}, f32[2,1024]{1,0:T(2,128)}) custom-call(bf16[2048,768]{1,0:T(8,128)(2,1)} %attend_back.1.first_right.mixed_ref, bf16[2048,1024]{1,0:T(8,128)(2,1)} %get-tuple-element.259.first_right.hidden_ref, bf16[1024,768]{1,0:T(8,128)(2,1)} %get-tuple-element.282.proj_ref, ...), custom_call_target="tpu_custom_call" | custom-call | tf_op jit(solution)/shard_map/pull/pallas_call | solution.py:342
  331.6 54.8 %finish.1 = (f32[24,128]{1,0:T(8,128)}, f32[8,128]{1,0:T(8,128)}, bf16[512,1024]{1,0:T(8,128)(2,1)}, bf16[256,384]{1,0:T(8,128)(2,1)}) custom-call(f32[24,128]{1,0:T(8,128)} %select_maximum_fusion.refs_0_, bf16[128,1024]{1,0:T(8,128)(2,1)} %reduce-scatter.5.cloned.1.call-done.refs_1_.merge_ref, bf16[256,1024]{1,0:T(8,128)(2,1)} %reduce-scatter.3.cloned.1.call-done.refs_2_, ...), custom_call_target="tpu_custom_call" | custom-call | tf_op jit(solution)/shard_map/finish/pallas_call | solution.py:903
  391.6 25.4 %adam_all.1 = (f32[1024,1024]{1,0:T(8,128)}, f32[1024,1024]{1,0:T(8,128)}, f32[1024,1024]{1,0:T(8,128)}, bf16[1024,1024]{1,0:T(8,128)(2,1)}, f32[1024,1024]{1,0:...) custom-call(f32[1,4]{1,0:T(1,128)} %maximum_bitcast_fusion.scale_ref, ...), custom_call_target="tpu_custom_call" | custom-call | tf_op jit(solution)/shard_map/adam_all/pallas_call | solution.py:987
  418.1 7.3 %settle.1 = f32[512,1024]{1,0:T(8,128)} custom-call(bf16[512,1024]{1,0:T(8,128)(2,1)} %copy-done.14, f32[512,1024]{1,0:T(8,128)} %get-tuple-element.316.term_ref, bf16[512,1024]{1,0:T(8,128)(2,1)} %tokens_ref.5, bf16[512,1024]{1,0:T(8,128)(2,1)} %cotangent_ref.1, f32[2,1024]{1,0:T(2,128)} %params_ref.9), custom_call_target="tpu_custom_call" | custom-call | tf_op jit(solution)/shard_map/settle/pallas_call | solution.py:1021
  (135 shorter events, 106.7 us)
Async XLA Ops:
  7.2 48.5 %all-gather.8.cloned.1.call-start = ((), (), s32[]{:S(2)}) async-start(), calls=%async_computation.2 | async-start | bytes 1310720 | tf_op jit(solution)/shard_map/all_gather | solution.py:1087
  9.9 95.5 %all-gather.10.cloned.1.call-start = ((), (), s32[]{:S(2)}) async-start(), calls=%async_computation.5 | async-start | bytes 2359296 | tf_op jit(solution)/shard_map/all_gather | solution.py:1092
  10.0 42.9 %collective-permute-start = (bf16[512,1024]{1,0:T(8,128)(2,1)}, bf16[512,1024]{1,0:T(8,128)(2,1)S(1)}, u32[]{:S(2)}, u32[]{:S(2)}) collective-permute-start(bf16[512,1024]{1,0:T(8,128)(2,1)} %tokens_ref.5), channel_id=1, source_target_pairs={{0,1},{1,2},{2,3},{3,0},{4,5},{5,6},{6,7},{7,4},{8,9},{9,10},{10,1... | collective-permute-start | bytes 3145736 | tf_op jit(solution)/shard_map/ppermute | solution.py:1078
  27.6 39.3 %copy-start.16 = (s32[4]{0:T(128)}, s32[4]{0:T(128)S(1)}, u32[]{:S(2)}) copy-start(s32[4]{0:T(128)S(1)} %compare_select_fusion.slots_ref) | copy-start | bytes 52
  57.4 75.1 %all-gather.12.cloned.1.call-start = ((), (), s32[]{:S(2)}) async-start(), calls=%async_computation.6 | async-start | bytes 7077888 | tf_op jit(solution)/shard_map/all_gather | solution.py:1092
  59.6 215.6 %reduce-scatter.3.cloned.1.call-start = ((), (), s32[]{:S(2)}) async-start(), calls=%async_computation.3 | async-start | bytes 4718592 | tf_op jit(solution)/shard_map/reduce_scatter | solution.py:1187
  59.8 26.9 %collective-permute-start.1 = (bf16[512,1024]{1,0:T(8,128)(2,1)S(1)}, bf16[512,1024]{1,0:T(8,128)(2,1)S(1)}, u32[]{:S(2)}, u32[]{:S(2)}) collective-permute-start(bf16[512,1024]{1,0:T(8,128)(2,1)S(1)} %collective-permute-done.tokens_ref), channel_id=1, source_target_pairs={{0,1},{1,2},{2,3},{3,0},{4,5},{5,6},{6,7},{7,4},{8,9},{9,10},{10,1... | collective-permute-start | bytes 3145736 | tf_op jit(solution)/shard_map/ppermute | solution.py:1078
  74.2 20.5 %copy-start.15 = (s32[2048]{0:T(1024)}, s32[2048]{0:T(1024)S(1)}, u32[]{:S(2)}) copy-start(s32[2048]{0:T(1024)S(1)} %select_reduce_fusion) | copy-start | bytes 24580
  86.8 26.0 %collective-permute-start.2 = (bf16[512,1024]{1,0:T(8,128)(2,1)S(1)}, bf16[512,1024]{1,0:T(8,128)(2,1)S(1)}, u32[]{:S(2)}, u32[]{:S(2)}) collective-permute-start(bf16[512,1024]{1,0:T(8,128)(2,1)S(1)} %collective-permute-done.1.tokens_ref), channel_id=1, source_target_pairs={{0,1},{1,2},{2,3},{3,0},{4,5},{5,6},{6,7},{7,4},{8,9},{9,10},{10,1... | collective-permute-start | bytes 3145736 | tf_op jit(solution)/shard_map/ppermute | solution.py:1078
  112.8 28.2 %collective-permute-start.3 = (bf16[512,1024]{1,0:T(8,128)(2,1)S(1)}, bf16[512,1024]{1,0:T(8,128)(2,1)}, u32[]{:S(2)}, u32[]{:S(2)}) collective-permute-start(bf16[512,1024]{1,0:T(8,128)(2,1)S(1)} %copy-done.8), channel_id=1, source_target_pairs={{0,1},{1,2},{2,3},{3,0},{4,5},{5,6},{6,7},{7,4},{8,9},{9,10},{10,1... | collective-permute-start | bytes 3145736 | tf_op jit(solution)/shard_map/ppermute | solution.py:1078
  141.0 27.6 %collective-permute-start.5 = (bf16[512,1024]{1,0:T(8,128)(2,1)}, bf16[512,1024]{1,0:T(8,128)(2,1)S(1)}, u32[]{:S(2)}, u32[]{:S(2)}) collective-permute-start(bf16[512,1024]{1,0:T(8,128)(2,1)} %collective-permute-done.3.grad_ref), channel_id=1, source_target_pairs={{0,1},{1,2},{2,3},{3,0},{4,5},{5,6},{6,7},{7,4},{8,9},{9,10},{10,1... | collective-permute-start | bytes 3145736 | tf_op jit(solution)/shard_map/ppermute | solution.py:1078
  148.4 20.2 %copy-start.10 = (bf16[512,1024]{1,0:T(8,128)(2,1)S(1)}, bf16[512,1024]{1,0:T(8,128)(2,1)}, u32[]{:S(2)}) copy-start(bf16[512,1024]{1,0:T(8,128)(2,1)} %down_term.5) | copy-start | bytes 3145732
  168.5 27.8 %collective-permute-start.6 = (bf16[512,1024]{1,0:T(8,128)(2,1)S(1)}, bf16[512,1024]{1,0:T(8,128)(2,1)S(1)}, u32[]{:S(2)}, u32[]{:S(2)}) collective-permute-start(bf16[512,1024]{1,0:T(8,128)(2,1)S(1)} %collective-permute-done.5.grad_ref), channel_id=1, source_target_pairs={{0,1},{1,2},{2,3},{3,0},{4,5},{5,6},{6,7},{7,4},{8,9},{9,10},{10,1... | collective-permute-start | bytes 3145736 | tf_op jit(solution)/shard_map/ppermute | solution.py:1078
  168.5 52.2 %collective-permute-start.4 = (bf16[512,1024]{1,0:T(8,128)(2,1)S(1)}, bf16[512,1024]{1,0:T(8,128)(2,1)}, u32[]{:S(2)}, u32[]{:S(2)}) collective-permute-start(bf16[512,1024]{1,0:T(8,128)(2,1)S(1)} %copy-done.10), channel_id=1, source_target_pairs={{0,1},{1,2},{2,3},{3,0},{4,5},{5,6},{6,7},{7,4},{8,9},{9,10},{10,1... | collective-permute-start | bytes 3145736 | tf_op jit(solution)/shard_map/ppermute | solution.py:1078
  220.8 107.4 %reduce-scatter.5.cloned.1.call-start = ((), (), s32[]{:S(2)}) async-start(), calls=%async_computation.4 | async-start | bytes 2359296 | tf_op jit(solution)/shard_map/reduce_scatter | solution.py:1187
  224.9 50.3 %collective-permute-start.7 = (bf16[512,1024]{1,0:T(8,128)(2,1)}, bf16[512,1024]{1,0:T(8,128)(2,1)S(1)}, u32[]{:S(2)}, u32[]{:S(2)}) collective-permute-start(bf16[512,1024]{1,0:T(8,128)(2,1)} %add_convert_fusion.3), channel_id=1, source_target_pairs={{0,1},{1,2},{2,3},{3,0},{4,5},{5,6},{6,7},{7,4},{8,9},{9,10},{10,1... | collective-permute-start | bytes 3145736 | tf_op jit(solution)/shard_map/ppermute | solution.py:1078
  224.9 50.3 %collective-permute-start.10 = (bf16[512,256]{1,0:T(8,128)(2,1)}, bf16[512,256]{1,0:T(8,128)(2,1)}, u32[]{:S(2)}, u32[]{:S(2)}) collective-permute-start(bf16[512,256]{1,0:T(8,128)(2,1)} %get-tuple-element.268), channel_id=1, source_target_pairs={{0,3},{1,0},{2,1},{3,2},{4,7},{5,4},{6,5},{7,6},{8,11},{9,8},{10,9... | collective-permute-start | bytes 786440 | tf_op jit(solution)/shard_map/ppermute | solution.py:1232
  228.7 46.4 %collective-permute-start.8 = (bf16[512,256]{1,0:T(8,128)(2,1)}, bf16[512,256]{1,0:T(8,128)(2,1)}, u32[]{:S(2)}, u32[]{:S(2)}) collective-permute-start(bf16[512,256]{1,0:T(8,128)(2,1)} %get-tuple-element.266), channel_id=1, source_target_pairs={{0,1},{1,2},{2,3},{3,0},{4,5},{5,6},{6,7},{7,4},{8,9},{9,10},{10,1... | collective-permute-start | bytes 786440 | tf_op jit(solution)/shard_map/ppermute | solution.py:1232
  228.7 46.4 %collective-permute-start.9 = (bf16[512,256]{1,0:T(8,128)(2,1)}, bf16[512,256]{1,0:T(8,128)(2,1)}, u32[]{:S(2)}, u32[]{:S(2)}) collective-permute-start(bf16[512,256]{1,0:T(8,128)(2,1)} %get-tuple-element.267), channel_id=1, source_target_pairs={{0,2},{1,3},{2,0},{3,1},{4,6},{5,7},{6,4},{7,5},{8,10},{9,11},{10,... | collective-permute-start | bytes 786440 | tf_op jit(solution)/shard_map/ppermute | solution.py:1232
  275.3 116.4 %all-gather.14.cloned.1.call-start = ((), (), s32[]{:S(2)}) async-start(), calls=%async_computation.7 | async-start | bytes 4718592 | tf_op jit(solution)/shard_map/all_gather | solution.py:1274
  278.1 29.0 %collective-permute-start.11 = (bf16[512,1024]{1,0:T(8,128)(2,1)}, bf16[512,1024]{1,0:T(8,128)(2,1)S(1)}, u32[]{:S(2)}, u32[]{:S(2)}) collective-permute-start(bf16[512,1024]{1,0:T(8,128)(2,1)} %add_convert_fusion.2), channel_id=1, source_target_pairs={{0,1},{1,2},{2,3},{3,0},{4,5},{5,6},{6,7},{7,4},{8,9},{9,10},{10,1... | collective-permute-start | bytes 3145736 | tf_op jit(solution)/shard_map/ppermute | solution.py:1078
  307.9 20.4 %collective-permute-start.12 = (bf16[512,1024]{1,0:T(8,128)(2,1)}, bf16[512,1024]{1,0:T(8,128)(2,1)}, u32[]{:S(2)}, u32[]{:S(2)}) collective-permute-start(bf16[512,1024]{1,0:T(8,128)(2,1)} %get-tuple-element.292), channel_id=1, source_target_pairs={{0,1},{1,2},{2,3},{3,0},{4,5},{5,6},{6,7},{7,4},{8,9},{9,10},{10,1... | collective-permute-start | bytes 3145736 | tf_op jit(solution)/shard_map/ppermute | solution.py:1078
  328.2 58.1 %copy-start.9 = (f32[512,1024]{1,0:T(8,128)S(1)}, f32[512,1024]{1,0:T(8,128)}, u32[]{:S(2)}) copy-start(f32[512,1024]{1,0:T(8,128)} %get-tuple-element.302) | copy-start | bytes 6291460
  387.9 29.2 %collective-permute-start.13 = (bf16[512,1024]{1,0:T(8,128)(2,1)S(1)}, bf16[512,1024]{1,0:T(8,128)(2,1)S(1)}, u32[]{:S(2)}, u32[]{:S(2)}) collective-permute-start(bf16[512,1024]{1,0:T(8,128)(2,1)S(1)} %add_convert_fusion), channel_id=1, source_target_pairs={{0,1},{1,2},{2,3},{3,0},{4,5},{5,6},{6,7},{7,4},{8,9},{9,10},{10,1... | collective-permute-start | bytes 3145736 | tf_op jit(solution)/shard_map/ppermute | solution.py:1078
  (18 other events, 80.4 us)
Sparse Core Ops, SparseCore 0:
  10.2 45.5 all-gather.7
  58.2 26.4 all-gather.9
  87.1 45.3 all-gather.11
  220.9 51.2 reduce-scatter.2
  275.9 51.3 reduce-scatter.4
  329.0 38.5 all-gather.13

commit v3 on v2

--- a/solution.py
+++ b/solution.py
@@ -88,16 +88,19 @@
 
 
 def project_kernel(rows_ref, weight_ref, cos_ref, sin_ref, out_ref):
-    width = out_ref.shape[1]
-    projected = dot_plain(rows_ref[...], weight_ref[...])
-    for first in range(0, width, LANES):
-        piece = projected[:, first : first + LANES]
-        part = first // LANES % 3
-        if part < 2:
-            piece = piece * cos_ref[...] + partner(piece) * sin_ref[...]
-        if part == 0:
-            piece = piece * HEAD ** (-0.5)
-        out_ref[:, first : first + LANES] = piece.astype(jnp.bfloat16)
+    def pair(index, carry):
+        first = pl.multiple_of(index * 3 * LANES, LANES)
+        projected = dot_plain(rows_ref[...], weight_ref[:, pl.ds(first, 3 * LANES)])
+        for part in range(3):
+            piece = projected[:, part * LANES : (part + 1) * LANES]
+            if part < 2:
+                piece = piece * cos_ref[...] + partner(piece) * sin_ref[...]
+            if part == 0:
+                piece = piece * HEAD ** (-0.5)
+            out_ref[:, pl.ds(first + part * LANES, LANES)] = piece.astype(jnp.bfloat16)
+        return carry
+
+    lax.fori_loop(0, out_ref.shape[1] // (3 * LANES), pair, 0)
 
 
 def project(rows, weight, cosine, sine):
@@ -176,7 +179,7 @@
     def column(cols):
         out_ref[:, cols] = dot_plain(active_ref[...], down_ref[:, cols]).astype(out_ref.dtype)
 
-    in_chunks(out_ref.shape[1], 256, column)
+    in_chunks(out_ref.shape[1], 512, column)
 
 
 def down_term(slot, slots, activated, down, kept):
@@ -263,12 +266,7 @@
 
     grads = grad_ref[...]
     all_ref[...] = grads
-
-    def column(cols):
-        hidden = dot_last(grad_ref[...], down_ref[cols, :]) * slope_ref[:, cols]
-        hidden_ref[:, cols] = hidden.astype(jnp.bfloat16)
-
-    in_chunks(down_ref.shape[0], min(512, down_ref.shape[0]), column)
+    hidden_ref[...] = (dot_last(grads, down_ref[...]) * slope_ref[...]).astype(jnp.bfloat16)
     attended_ref[...] = dot_last(grads, merge_own[...]).astype(jnp.bfloat16)
 
 
@@ -319,48 +317,61 @@
     )(span_index.reshape(1), grads, slope, down, merge, *held)
 
 
-def pull_kernel(mixed_ref, hidden_ref, proj_ref, up_ref, tokens_ref, out_ref, sums_ref, unit_ref):
-    unit_ref[...] = normalize(tokens_ref[...])[0]
-    begun = pl.program_id(0) > 0
-
-    def column(cols):
-        partial_grad = dot_last(mixed_ref[...], proj_ref[cols, :]) + dot_last(
-            hidden_ref[...], up_ref[cols, :]
-        )
-        out_ref[:, cols] = partial_grad.astype(out_ref.dtype)
-        gain = jnp.sum(partial_grad * unit_ref[:, cols], axis=0, keepdims=True)
-        bias = jnp.sum(partial_grad, axis=0, keepdims=True)
-        both = jnp.concatenate([gain, bias], axis=0)
-        sums_ref[:, cols] = jnp.where(begun, sums_ref[:, cols], 0.0) + both
-
-    in_chunks(proj_ref.shape[0], 256, column)
-
-
-def pull(slot, mixed, hidden_grad, proj, up, tokens, kept):
-    rows, depth = tokens.shape
+def pull_kernel(blocks, mixed_ref, hidden_ref, proj_ref, up_ref, *refs):
+    tokens_refs, (lead_ref, out_ref, sums_ref, rows_ref) = refs[:blocks], refs[blocks:]
+    index = pl.program_id(0)
+    for block, tokens_ref in enumerate(tokens_refs):
+
+        @pl.when(index // 2 == block)
+        def _():
+            rows_ref[...] = tokens_ref[...]
+
+    partial_grad = dot_last(mixed_ref[...], proj_ref[...]) + dot_last(hidden_ref[...], up_ref[...])
+    out_ref[...] = partial_grad
+
+    @pl.when(index < 2)
+    def _():
+        lead_ref[...] = partial_grad.astype(jnp.bfloat16)
+
+    unit, unused = normalize(rows_ref[...])
+    gain = jnp.sum(partial_grad * unit, axis=0, keepdims=True)
+    bias = jnp.sum(partial_grad, axis=0, keepdims=True)
+    both = jnp.concatenate([gain, bias], axis=0)
+    sums_ref[...] = jnp.where(index > 0, sums_ref[...], 0.0) + both
+
+
+def pull(slot, mixed, hidden_grad, proj, up, token_blocks):
+    rows, depth = token_blocks[0].shape
+    blocks = len(token_blocks)
     half = rows // 2
+
+    def part(block, i):
+        return (jnp.clip(i - 2 * block, 0, 1), 0)
+
     return pl.pallas_call(
-        pull_kernel,
+        partial(pull_kernel, blocks),
         out_shape=(
-            jax.ShapeDtypeStruct((rows, depth), kept),
+            jax.ShapeDtypeStruct((rows, depth), jnp.bfloat16),
+            jax.ShapeDtypeStruct((blocks * rows, depth), jnp.float32),
             jax.ShapeDtypeStruct((2, depth), jnp.float32),
         ),
-        grid=(2,),
+        grid=(2 * blocks,),
         in_specs=[
             pl.BlockSpec((half, mixed.shape[1]), lambda i: (2 * slot + i, 0)),
             pl.BlockSpec((half, hidden_grad.shape[1]), lambda i: (2 * slot + i, 0)),
             pl.BlockSpec(proj.shape, lambda i: (0, 0)),
             pl.BlockSpec(up.shape, lambda i: (0, 0)),
-            pl.BlockSpec((half, depth), lambda i: (i, 0)),
-        ],
+        ]
+        + [pl.BlockSpec((half, depth), partial(part, block)) for block in range(blocks)],
         out_specs=(
+            pl.BlockSpec((half, depth), partial(part, 0)),
             pl.BlockSpec((half, depth), lambda i: (i, 0)),
             pl.BlockSpec((2, depth), lambda i: (0, 0)),
         ),
-        scratch_shapes=[pltpu.VMEM((half, depth), jnp.float32)],
+        scratch_shapes=[pltpu.VMEM((half, depth), jnp.bfloat16)],
         cost_estimate=short,
         name="pull",
-    )(mixed, hidden_grad, proj, up, tokens)
+    )(mixed, hidden_grad, proj, up, *token_blocks)
 
 
 def project_all_kernel(index_ref, rows_ref, cos_ref, sin_ref, *refs):
@@ -947,14 +958,14 @@
             gradient = grads_ref[0, matrix, rows, :].astype(jnp.float32)
             update(matrix, rows, gradient, matrix_step, decay_rate)
 
-    in_chunks(states[0].shape[0], 32, feed_rows)
+    in_chunks(states[0].shape[0], 16, feed_rows)
 
     @pl.when(pl.program_id(0) == 0)
     def _():
         def proj_rows(rows):
             update(2, rows, proj_ref[rows, :].astype(jnp.float32), matrix_step, decay_rate)
 
-        in_chunks(proj_ref.shape[0], 64, proj_rows)
+        in_chunks(proj_ref.shape[0], 32, proj_rows)
         update(3, slice(None), merge_ref[...].astype(jnp.float32).T, matrix_step, decay_rate)
         per_row = D // LANES
         for k in range(2 * per_row):
@@ -1017,11 +1028,11 @@
 
 def settle(arrived, term, tokens, cotangent, params):
     rows, depth = tokens.shape
-    block = pl.BlockSpec((rows // 8, depth), lambda i: (i, 0))
+    block = pl.BlockSpec((rows // 4, depth), lambda i: (i, 0))
     return pl.pallas_call(
         settle_kernel,
         out_shape=jax.ShapeDtypeStruct((rows, depth), jnp.float32),
-        grid=(8,),
+        grid=(4,),
         in_specs=[block] * 4 + [pl.BlockSpec((2, depth), lambda i: (0, 0))],
         out_specs=block,
         cost_estimate=short,
@@ -1235,15 +1246,25 @@
             [(i, (i + ahead) % narrow_count) for i in range(narrow_count)],
         )
     terms = []
+    term_blocks = []
+
+    def term_at(place):
+        block, at = terms[place]
+        return rows_of(term_blocks[block], at)
+
     norm_part = jnp.zeros((2, D), jnp.float32)
 
-    def pull_more(count, mixed, norm_part):
-        for slot in order[len(terms) : len(terms) + count]:
-            kept = jnp.float32 if terms else jnp.bfloat16
-            term, sums = pull(
-                slot, mixed, hidden_grad, proj_own, up_slice, token_blocks[slot], kept
+    def pull_more(slots_now, norm_part):
+        if slots_now:
+            lead, block, sums = pull(
+                slots_now[0], mixed_grad, hidden_grad, proj_own, up_slice,
+                [token_blocks[slot] for slot in slots_now],
             )
-            terms.append(term)
+            if not term_blocks:
+                term_blocks.append(lead)
+            term_blocks.append(block)
+            for place in range(len(slots_now)):
+                terms.append((len(term_blocks) - 1, place))
             norm_part = norm_part + sums
         return norm_part
 
@@ -1268,15 +1289,18 @@
             )
             heads_part = wide_sum(heads_grad)
         else:
-            norm_part = pull_more(3, mixed_grad, norm_part)
-            moving, terms, norm_part, feed_part = meet(moving, terms, norm_part, feed_part)
+            norm_part = pull_more(order[:-1][len(terms) : len(terms) + 3], norm_part)
+            moving, term_blocks[:], norm_part, feed_part = meet(
+                moving, term_blocks, norm_part, feed_part
+            )
         if place == narrow_count - 3:
             feed_all = lax.all_gather(feed_part, "wide", axis=0).reshape(
                 wide_count, 2, part_rows, -1
             )
     branch_moving = moving
-    moving = send_on(terms[0])
-    norm_part = pull_more(narrow_count, mixed_grad, norm_part)
+    moving = send_on(term_blocks[0])
+    norm_part = pull_more(order[len(terms) : -1], norm_part)
+    norm_part = pull_more([0], norm_part)
     branch = branch_moving.astype(jnp.float32) + branch_terms[0]
     merged = dot_plain(jnp.concatenate(pieces, axis=1), merge_turn)
     output_rows = tokens.astype(jnp.float32) + merged + branch
@@ -1303,7 +1327,7 @@
     for place in range(1, narrow_count - 1):
         if place == narrow_count - 3:
             moving, parts, heads_part, scales = meet(moving, parts, heads_part, scales)
-        sent = (moving.astype(jnp.float32) + terms[place]).astype(jnp.bfloat16)
+        sent = (moving.astype(jnp.float32) + term_at(place)).astype(jnp.bfloat16)
         if place == narrow_count - 3:
             total, stats, moving, *proj_block = finish(
                 parts, heads_part, feed_part, sent, direct, narrow_count, wide_count, own_width,
@@ -1353,7 +1377,7 @@
         updated[4 * k : 4 * k + 4] for k in range(5)
     ]
     moving, new_up = meet(moving, new_up)
-    input_grad = settle(moving, terms[-1], tokens, cotangent, norm_params)
+    input_grad = settle(moving, term_at(-1), tokens, cotangent, norm_params)
     return (
         layer_out,
         input_grad,

time: 433 us -> 423 us (0.977)
  Pallas kernels: 298 us -> 276 us
  waiting for transfers between devices: 49.4 us -> 63.1 us
    pallas_call x4 -> x2, Pallas kernels: 32.7 us -> 20.8 us  [pull(): pl.pallas_call(partial(pull_kernel, blocks), out_shape=(jax.ShapeDtypeStr...]
    ppermute x11, waiting for transfers between devices: 45.8 us -> 53.7 us  [send_on(): return lax.ppermute(array, 'narrow', onward)]
    pallas_call x1, Pallas kernels: 54.8 us -> 49.5 us  [finish(): pl.pallas_call(partial(finish_kernel, narrow_count, wide_count, own_units...]
  transfers between devices with their start and end apart: 20 -> 20, of which waited for: 7 -> 10; matrix products, arithmetic and copies ran while one was open for 10% -> 10% of each run, Pallas kernels for 67% -> 64%
where the time goes in v3:
time: 423 us; the launch traced here: 426 us
  Pallas kernels  276 us (65%)
  waiting for transfers between devices  63.1 us (15%)
  other arithmetic  35 us (8%)
  starting transfers between devices  19.1 us (5%)
  between operations  15.1 us (4%)
  local copies, waits for them, and re-layouts  12.9 us (3%)
  matrix products  4.57 us (1%)
    ppermute x11, waiting for transfers between devices, send_on(): return lax.ppermute(array, 'narrow', onward)  53.7 us
    pallas_call x1, Pallas kernels, finish(): pl.pallas_call(partial(finish_kernel, narrow_count, wide_count, own_units...  49.5 us
    pallas_call x1, Pallas kernels, attend_back(): pl.pallas_call(partial(attend_back_kernel, block_q, block_k, heads_in), o...  34 us
    pallas_call x2, Pallas kernels, outer(): pl.pallas_call(partial(outer_kernel, bool(blocks)), out_shape=jax.ShapeDt...  28.6 us
    pallas_call x2, Pallas kernels, attend(): pl.pallas_call(partial(attend_kernel, block_q, block_k, heads_in), out_sh...  28.3 us
    pallas_call x4, Pallas kernels, feed(): pl.pallas_call(feed_kernel, out_shape=(jax.ShapeDtypeStruct((slots * rows...  27.7 us
    pallas_call x1, Pallas kernels, adam_all(): pl.pallas_call(adam_kernel, out_shape=tuple(shapes), grid=(count,), in_sp...  25.7 us
    pallas_call x2, Pallas kernels, pull(): pl.pallas_call(partial(pull_kernel, blocks), out_shape=(jax.ShapeDtypeStr...  20.8 us
  transfers between devices with their start and end apart: 20, of which 10 were waited for; matrix products, arithmetic and copies ran while one was open for 10% of the time, Pallas kernels for 64%

profile of v3, /device:TPU:0, one launch (start us, length us, event | category | flops | bytes accessed | tf_op | source)
XLA Modules:
  0.0 425.9 jit_solution(1329076769508411073)
XLA Ops:
  20.8 6.9 %feed.4 = (bf16[2048,1024]{1,0:T(8,128)(2,1)}, bf16[2048,1024]{1,0:T(8,128)(2,1)}, f32[2048,1024]{1,0:T(8,128)}) custom-call(bf16[512,1024]{1,0:T(8,128)(2,1)} %tokens_ref.3, f32[2,1024]{1,0:T(2,128)} %params_ref.9, bf16[1024,1024]{1,0:T(8,128)(2,1)} %convert_element_type.70.weight_ref.up_ref), custom_call_target="tpu_custom_call" | custom-call | tf_op jit(solution)/shard_map/feed/pallas_call | solution.py:153
  27.7 25.3 %collective-permute-done.tokens_ref.refs_0_ = bf16[512,1024]{1,0:T(8,128)(2,1)S(1)} collective-permute-done((bf16[512,1024]{1,0:T(8,128)(2,1)}, bf16[512,1024]{1,0:T(8,128)(2,1)S(1)}, u32[]{:S(2)}, u32[]{:S(2)}) %collective-permute-start) | collective-permute-done | bytes 1048608 | tf_op jit(solution)/shard_map/ppermute | solution.py:1089
  60.0 6.9 %feed.5 = (bf16[2048,1024]{1,0:T(8,128)(2,1)}, bf16[2048,1024]{1,0:T(8,128)(2,1)}, f32[2048,1024]{1,0:T(8,128)}) custom-call(bf16[512,1024]{1,0:T(8,128)(2,1)} %copy-done.5, f32[2,1024]{1,0:T(2,128)} %params_ref.9, bf16[1024,1024]{1,0:T(8,128)(2,1)} %convert_element_type.70.weight_ref.up_ref, ...), custom_call_target="tpu_custom_call", output_to_operand_aliasing={{0}: (3, {}), {1}: (4, {}), {2}: (5, {})} | custom-call | tf_op jit(solution)/shard_map/feed/pallas_call | solution.py:153
  73.5 5.6 %fusion = (f32[2048,128]{1,0:T(8,128)}, f32[2048,128]{1,0:T(8,128)}) fusion(f32[128]{0:T(128)S(1)} %compare_select_fusion.2, f32[128]{0:T(128)S(1)} %mul.51, f32[2048]{0:T(1024)S(1)} %subtract_convert_fusion), kind=kLoop, calls=%fused_computation.11 | loop fusion | flops 524288 | bytes 2106368 | tf_op jit(solution)/shard_map/mul | solution.py:77
  79.1 7.7 %collective-permute-done.1.tokens_ref.refs_1_ = bf16[512,1024]{1,0:T(8,128)(2,1)S(1)} collective-permute-done((bf16[512,1024]{1,0:T(8,128)(2,1)S(1)}, bf16[512,1024]{1,0:T(8,128)(2,1)S(1)}, u32[]{:S(2)}, u32[]{:S(2)}) %collective-permute-start.1) | collective-permute-done | bytes 1048608 | tf_op jit(solution)/shard_map/ppermute | solution.py:1089
  87.8 6.9 %feed.6 = (bf16[2048,1024]{1,0:T(8,128)(2,1)}, bf16[2048,1024]{1,0:T(8,128)(2,1)}, f32[2048,1024]{1,0:T(8,128)}) custom-call(bf16[512,1024]{1,0:T(8,128)(2,1)} %copy-done.6, f32[2,1024]{1,0:T(2,128)} %params_ref.9, bf16[1024,1024]{1,0:T(8,128)(2,1)} %convert_element_type.70.weight_ref.up_ref, ...), custom_call_target="tpu_custom_call", output_to_operand_aliasing={{0}: (3, {}), {1}: (4, {}), {2}: (5, {})} | custom-call | tf_op jit(solution)/shard_map/feed/pallas_call | solution.py:153
  103.9 6.5 %pick_merge.1 = bf16[1024,1024]{1,0:T(8,128)(2,1)} custom-call(s32[4]{0:T(128)} %copy-done.15, bf16[8,4,256,128]{3,2,1,0:T(8,128)(2,1)} %bitcast.29), custom_call_target="tpu_custom_call" | custom-call | tf_op jit(solution)/shard_map/pick_merge/pallas_call | solution.py:437
  113.8 7.0 %feed.7 = (bf16[2048,1024]{1,0:T(8,128)(2,1)}, bf16[2048,1024]{1,0:T(8,128)(2,1)}, f32[2048,1024]{1,0:T(8,128)}) custom-call(bf16[512,1024]{1,0:T(8,128)(2,1)} %copy-done.7, f32[2,1024]{1,0:T(2,128)} %params_ref.9, bf16[1024,1024]{1,0:T(8,128)(2,1)} %convert_element_type.70.weight_ref.up_ref, ...), custom_call_target="tpu_custom_call", output_to_operand_aliasing={{0}: (3, {}), {1}: (4, {}), {2}: (5, {})} | custom-call | tf_op jit(solution)/shard_map/feed/pallas_call | solution.py:153
  125.3 5.0 %push.4 = (bf16[2048,1024]{1,0:T(8,128)(2,1)}, bf16[2048,1024]{1,0:T(8,128)(2,1)}, bf16[2048,256]{1,0:T(8,128)(2,1)}) custom-call(s32[1]{0:T(128)} %bitcast.4.index_ref, bf16[512,1024]{1,0:T(8,128)(2,1)} %cotangent_ref.1, f32[2048,1024]{1,0:T(8,128)} %get-tuple-element.230.slope_ref, bf16[1024,1024]{1,0:T(8,128)(2,1)} %convert_element_type.73.down_ref, ...), custom_call_target="tpu_custom_call" | custom-call | tf_op jit(solution)/shard_map/push/pallas_call | solution.py:290
  132.5 11.7 %project_all.1 = (bf16[2048,768]{1,0:T(8,128)(2,1)}, bf16[1024,768]{1,0:T(8,128)(2,1)}) custom-call(s32[1]{0:T(128)} %bitcast.4.index_ref, bf16[2048,1024]{1,0:T(8,128)(2,1)} %get-tuple-element.209.rows_ref.first_left, f32[2048,128]{1,0:T(8,128)} %get-tuple-element.210.cos_ref, f32[2048,128]{1,0:T(8,128)} %get-tuple-element.211.sin_ref, ...), custom_call_target="tpu_custom_call" | custom-call | tf_op jit(solution)/shard_map/project_all/pallas_call | solution.py:401
  146.0 5.0 %push.5 = (bf16[2048,1024]{1,0:T(8,128)(2,1)}, bf16[2048,1024]{1,0:T(8,128)(2,1)}, bf16[2048,256]{1,0:T(8,128)(2,1)}) custom-call(s32[1]{0:T(128)} %bitcast.4.index_ref, bf16[512,1024]{1,0:T(8,128)(2,1)} %collective-permute-done.3.grad_ref, f32[2048,1024]{1,0:T(8,128)} %get-tuple-element.230.slope_ref, ...), custom_call_target="tpu_custom_call", output_to_operand_aliasing={{0}: (5, {}), {1}: (6, {}), {2}: (7, {})} | custom-call | tf_op jit(solution)/shard_map/push/pallas_call | solution.py:290
  151.0 14.2 %attend.2 = (bf16[2048,256]{1,0:T(8,128)(2,1)}, f32[256,2048]{1,0:T(8,128)}, f32[2,8,2048]{2,1,0:T(8,128)}) custom-call(s32[4]{0:T(128)} %copy-done.15, s32[4]{0:T(128)} %select_reduce_fusion.3.first_ref, s32[4]{0:T(128)} %get-tuple-element.225.last_ref, s32[1,2048]{1,0:T(1,128)} %bitcast.36, ...), custom_call_target="tpu_custom_call" | custom-call | tf_op jit(solution)/shard_map/attend/pallas_call | solution.py:553
  165.2 6.7 %collective-permute-done.5.grad_ref = bf16[512,1024]{1,0:T(8,128)(2,1)S(1)} collective-permute-done((bf16[512,1024]{1,0:T(8,128)(2,1)}, bf16[512,1024]{1,0:T(8,128)(2,1)S(1)}, u32[]{:S(2)}, u32[]{:S(2)}) %collective-permute-start.5) | collective-permute-done | bytes 1048608 | tf_op jit(solution)/shard_map/ppermute | solution.py:1089
  173.0 5.0 %push.6 = (bf16[2048,1024]{1,0:T(8,128)(2,1)}, bf16[2048,1024]{1,0:T(8,128)(2,1)}, bf16[2048,256]{1,0:T(8,128)(2,1)}) custom-call(s32[1]{0:T(128)} %bitcast.4.index_ref, bf16[512,1024]{1,0:T(8,128)(2,1)} %copy-done.10, f32[2048,1024]{1,0:T(8,128)} %get-tuple-element.230.slope_ref, ...), custom_call_target="tpu_custom_call", output_to_operand_aliasing={{0}: (5, {}), {1}: (6, {}), {2}: (7, {})} | custom-call | tf_op jit(solution)/shard_map/push/pallas_call | solution.py:290
  178.0 14.1 %attend.3 = (bf16[2048,256]{1,0:T(8,128)(2,1)}, f32[256,2048]{1,0:T(8,128)}, f32[2,8,2048]{2,1,0:T(8,128)}) custom-call(s32[4]{0:T(128)} %copy-done.15, s32[4]{0:T(128)} %select_reduce_fusion.3.first_ref, s32[4]{0:T(128)} %get-tuple-element.225.last_ref, s32[1,2048]{1,0:T(1,128)} %bitcast.37, ...), custom_call_target="tpu_custom_call", output_to_operand_aliasing={{0}: (7, {}), {1}: (8, {}), {2}: (9, {})} | custom-call | tf_op jit(solution)/shard_map/attend/pallas_call | solution.py:553
  192.1 7.6 %collective-permute-done.6.grad_ref = bf16[512,1024]{1,0:T(8,128)(2,1)S(1)} collective-permute-done((bf16[512,1024]{1,0:T(8,128)(2,1)S(1)}, bf16[512,1024]{1,0:T(8,128)(2,1)S(1)}, u32[]{:S(2)}, u32[]{:S(2)}) %collective-permute-start.6) | collective-permute-done | bytes 1048608 | tf_op jit(solution)/shard_map/ppermute | solution.py:1089
  205.6 16.8 %outer.2 = bf16[8,2,128,1024]{3,2,1,0:T(8,128)(2,1)} custom-call(bf16[2048,1024]{1,0:T(8,128)(2,1)} %get-tuple-element.209.rows_ref.first_left, bf16[2048,1024]{1,0:T(8,128)(2,1)} %get-tuple-element.255.first_right.hidden_ref, bf16[2048,1024]{1,0:T(8,128)(2,1)} %get-tuple-element.256.active_ref.second_left, ...), custom_call_target="tpu_custom_call" | custom-call | tf_op jit(solution)/shard_map/outer/pallas_call | solution.py:244
  231.9 34.0 %attend_back.1.first_right.mixed_ref = bf16[2048,768]{1,0:T(8,128)(2,1)} custom-call(s32[4]{0:T(128)} %copy-done.15, s32[4]{0:T(128)} %get-tuple-element.225.last_ref, s32[4]{0:T(128)} %get-tuple-element.265.end_ref, s32[1,2048]{1,0:T(1,128)} %bitcast.38, f32[2048,128]{1,0:T(8,128)} %get-tuple-element.210.cos_ref, f32[2048,128]{1,0:T(8,128)} %get-tuple-element.211.sin_ref, ...), custom_call_target="tpu_custom_call" | custom-call | tf_op jit(solution)/shard_map/attend_back/pallas_call | solution.py:698
  266.0 11.7 %outer.3 = bf16[1024,1024]{1,0:T(8,128)(2,1)} custom-call(bf16[2048,1024]{1,0:T(8,128)(2,1)} %get-tuple-element.209.rows_ref.first_left, bf16[2048,768]{1,0:T(8,128)(2,1)} %attend_back.1.first_right.mixed_ref, bf16[2048,1024]{1,0:T(8,128)(2,1)} %get-tuple-element.257.second_right.second_left, bf16[2048,256]{1,0:T(8,128)(2,1)} %get-tuple-element.250.second_right), custom_call_target="tpu_custom_call" | custom-call | tf_op jit(solution)/shard_map/outer/pallas_call | solution.py:244
  284.2 14.0 %pull.2 = (bf16[512,1024]{1,0:T(8,128)(2,1)}, f32[1536,1024]{1,0:T(8,128)}, f32[2,1024]{1,0:T(2,128)}) custom-call(bf16[2048,768]{1,0:T(8,128)(2,1)} %attend_back.1.first_right.mixed_ref, bf16[2048,1024]{1,0:T(8,128)(2,1)} %get-tuple-element.255.first_right.hidden_ref, bf16[1024,768]{1,0:T(8,128)(2,1)} %get-tuple-element.278.proj_ref, ...), custom_call_target="tpu_custom_call" | custom-call | tf_op jit(solution)/shard_map/pull/pallas_call | solution.py:351
  305.0 6.8 %pull.3 = (bf16[512,1024]{1,0:T(8,128)(2,1)}, f32[512,1024]{1,0:T(8,128)}, f32[2,1024]{1,0:T(2,128)}) custom-call(bf16[2048,768]{1,0:T(8,128)(2,1)} %attend_back.1.first_right.mixed_ref, bf16[2048,1024]{1,0:T(8,128)(2,1)} %get-tuple-element.255.first_right.hidden_ref, bf16[1024,768]{1,0:T(8,128)(2,1)} %get-tuple-element.278.proj_ref, ...), custom_call_target="tpu_custom_call" | custom-call | tf_op jit(solution)/shard_map/pull/pallas_call | solution.py:351
  331.8 49.5 %finish.1 = (f32[24,128]{1,0:T(8,128)}, f32[8,128]{1,0:T(8,128)}, bf16[512,1024]{1,0:T(8,128)(2,1)}, bf16[256,384]{1,0:T(8,128)(2,1)}) custom-call(f32[24,128]{1,0:T(8,128)} %select_maximum_fusion.refs_0_, bf16[128,1024]{1,0:T(8,128)(2,1)} %reduce-scatter.5.cloned.1.call-done.refs_1_.merge_ref, bf16[256,1024]{1,0:T(8,128)(2,1)} %reduce-scatter.3.cloned.1.call-done.refs_2_, ...), custom_call_target="tpu_custom_call" | custom-call | tf_op jit(solution)/shard_map/finish/pallas_call | solution.py:914
  387.2 25.7 %adam_all.1 = (f32[1024,1024]{1,0:T(8,128)}, f32[1024,1024]{1,0:T(8,128)}, f32[1024,1024]{1,0:T(8,128)}, bf16[1024,1024]{1,0:T(8,128)(2,1)}, f32[1024,1024]{1,0:...) custom-call(f32[1,4]{1,0:T(1,128)} %maximum_bitcast_fusion.scale_ref, ...), custom_call_target="tpu_custom_call" | custom-call | tf_op jit(solution)/shard_map/adam_all/pallas_call | solution.py:998
  413.9 5.1 %settle.1 = f32[512,1024]{1,0:T(8,128)} custom-call(bf16[512,1024]{1,0:T(8,128)(2,1)} %copy-done.13, f32[512,1024]{1,0:T(8,128)} %get-tuple-element.308.term_ref, bf16[512,1024]{1,0:T(8,128)(2,1)} %tokens_ref.3, bf16[512,1024]{1,0:T(8,128)(2,1)} %cotangent_ref.1, f32[2,1024]{1,0:T(2,128)} %params_ref.9), custom_call_target="tpu_custom_call" | custom-call | tf_op jit(solution)/shard_map/settle/pallas_call | solution.py:1032
  (128 shorter events, 105.1 us)
Async XLA Ops:
  7.2 48.5 %all-gather.8.cloned.1.call-start = ((), (), s32[]{:S(2)}) async-start(), calls=%async_computation.2 | async-start | bytes 1310720 | tf_op jit(solution)/shard_map/all_gather | solution.py:1098
  9.9 94.0 %all-gather.10.cloned.1.call-start = ((), (), s32[]{:S(2)}) async-start(), calls=%async_computation.5 | async-start | bytes 2359296 | tf_op jit(solution)/shard_map/all_gather | solution.py:1103
  10.0 42.9 %collective-permute-start = (bf16[512,1024]{1,0:T(8,128)(2,1)}, bf16[512,1024]{1,0:T(8,128)(2,1)S(1)}, u32[]{:S(2)}, u32[]{:S(2)}) collective-permute-start(bf16[512,1024]{1,0:T(8,128)(2,1)} %tokens_ref.3), channel_id=1, source_target_pairs={{0,1},{1,2},{2,3},{3,0},{4,5},{5,6},{6,7},{7,4},{8,9},{9,10},{10,1... | collective-permute-start | bytes 3145736 | tf_op jit(solution)/shard_map/ppermute | solution.py:1089
  27.6 39.3 %copy-start.15 = (s32[4]{0:T(128)}, s32[4]{0:T(128)S(1)}, u32[]{:S(2)}) copy-start(s32[4]{0:T(128)S(1)} %compare_select_fusion.slots_ref) | copy-start | bytes 52
  57.4 75.1 %all-gather.12.cloned.1.call-start = ((), (), s32[]{:S(2)}) async-start(), calls=%async_computation.6 | async-start | bytes 7077888 | tf_op jit(solution)/shard_map/all_gather | solution.py:1103
  59.6 218.2 %reduce-scatter.3.cloned.1.call-start = ((), (), s32[]{:S(2)}) async-start(), calls=%async_computation.3 | async-start | bytes 4718592 | tf_op jit(solution)/shard_map/reduce_scatter | solution.py:1198
  59.8 26.9 %collective-permute-start.1 = (bf16[512,1024]{1,0:T(8,128)(2,1)S(1)}, bf16[512,1024]{1,0:T(8,128)(2,1)S(1)}, u32[]{:S(2)}, u32[]{:S(2)}) collective-permute-start(bf16[512,1024]{1,0:T(8,128)(2,1)S(1)} %collective-permute-done.tokens_ref.refs_0_), channel_id=1, source_target_pairs={{0,1},{1,2},{2,3},{3,0},{4,5},{5,6},{6,7},{7,4},{8,9},{9,10},{10,1... | collective-permute-start | bytes 3145736 | tf_op jit(solution)/shard_map/ppermute | solution.py:1089
  73.4 21.3 %copy-start.14 = (s32[2048]{0:T(1024)}, s32[2048]{0:T(1024)S(1)}, u32[]{:S(2)}) copy-start(s32[2048]{0:T(1024)S(1)} %select_reduce_fusion) | copy-start | bytes 24580
  86.8 26.0 %collective-permute-start.2 = (bf16[512,1024]{1,0:T(8,128)(2,1)S(1)}, bf16[512,1024]{1,0:T(8,128)(2,1)S(1)}, u32[]{:S(2)}, u32[]{:S(2)}) collective-permute-start(bf16[512,1024]{1,0:T(8,128)(2,1)S(1)} %collective-permute-done.1.tokens_ref.refs_1_), channel_id=1, source_target_pairs={{0,1},{1,2},{2,3},{3,0},{4,5},{5,6},{6,7},{7,4},{8,9},{9,10},{10,1... | collective-permute-start | bytes 3145736 | tf_op jit(solution)/shard_map/ppermute | solution.py:1089
  112.8 31.5 %collective-permute-start.3 = (bf16[512,1024]{1,0:T(8,128)(2,1)S(1)}, bf16[512,1024]{1,0:T(8,128)(2,1)}, u32[]{:S(2)}, u32[]{:S(2)}) collective-permute-start(bf16[512,1024]{1,0:T(8,128)(2,1)S(1)} %copy-done.8), channel_id=1, source_target_pairs={{0,1},{1,2},{2,3},{3,0},{4,5},{5,6},{6,7},{7,4},{8,9},{9,10},{10,1... | collective-permute-start | bytes 3145736 | tf_op jit(solution)/shard_map/ppermute | solution.py:1089
  144.3 27.6 %collective-permute-start.5 = (bf16[512,1024]{1,0:T(8,128)(2,1)}, bf16[512,1024]{1,0:T(8,128)(2,1)S(1)}, u32[]{:S(2)}, u32[]{:S(2)}) collective-permute-start(bf16[512,1024]{1,0:T(8,128)(2,1)} %collective-permute-done.3.grad_ref), channel_id=1, source_target_pairs={{0,1},{1,2},{2,3},{3,0},{4,5},{5,6},{6,7},{7,4},{8,9},{9,10},{10,1... | collective-permute-start | bytes 3145736 | tf_op jit(solution)/shard_map/ppermute | solution.py:1089
  151.0 20.9 %copy-start.9 = (bf16[512,1024]{1,0:T(8,128)(2,1)S(1)}, bf16[512,1024]{1,0:T(8,128)(2,1)}, u32[]{:S(2)}) copy-start(bf16[512,1024]{1,0:T(8,128)(2,1)} %down_term.5) | copy-start | bytes 3145732
  171.8 27.8 %collective-permute-start.6 = (bf16[512,1024]{1,0:T(8,128)(2,1)S(1)}, bf16[512,1024]{1,0:T(8,128)(2,1)S(1)}, u32[]{:S(2)}, u32[]{:S(2)}) collective-permute-start(bf16[512,1024]{1,0:T(8,128)(2,1)S(1)} %collective-permute-done.5.grad_ref), channel_id=1, source_target_pairs={{0,1},{1,2},{2,3},{3,0},{4,5},{5,6},{6,7},{7,4},{8,9},{9,10},{10,1... | collective-permute-start | bytes 3145736 | tf_op jit(solution)/shard_map/ppermute | solution.py:1089
  171.8 51.5 %collective-permute-start.4 = (bf16[512,1024]{1,0:T(8,128)(2,1)S(1)}, bf16[512,1024]{1,0:T(8,128)(2,1)}, u32[]{:S(2)}, u32[]{:S(2)}) collective-permute-start(bf16[512,1024]{1,0:T(8,128)(2,1)S(1)} %copy-done.9), channel_id=1, source_target_pairs={{0,1},{1,2},{2,3},{3,0},{4,5},{5,6},{6,7},{7,4},{8,9},{9,10},{10,1... | collective-permute-start | bytes 3145736 | tf_op jit(solution)/shard_map/ppermute | solution.py:1089
  205.6 16.9 %copy-start.1 = (bf16[2048,256]{1,0:T(8,128)(2,1)S(1)}, bf16[2048,256]{1,0:T(8,128)(2,1)}, u32[]{:S(2)}) copy-start(bf16[2048,256]{1,0:T(8,128)(2,1)} %get-tuple-element.250.second_right) | copy-start | bytes 3145732
  223.4 105.2 %reduce-scatter.5.cloned.1.call-start = ((), (), s32[]{:S(2)}) async-start(), calls=%async_computation.4 | async-start | bytes 2359296 | tf_op jit(solution)/shard_map/reduce_scatter | solution.py:1198
  227.5 50.2 %collective-permute-start.7 = (bf16[512,1024]{1,0:T(8,128)(2,1)}, bf16[512,1024]{1,0:T(8,128)(2,1)S(1)}, u32[]{:S(2)}, u32[]{:S(2)}) collective-permute-start(bf16[512,1024]{1,0:T(8,128)(2,1)} %add_convert_fusion.3), channel_id=1, source_target_pairs={{0,1},{1,2},{2,3},{3,0},{4,5},{5,6},{6,7},{7,4},{8,9},{9,10},{10,1... | collective-permute-start | bytes 3145736 | tf_op jit(solution)/shard_map/ppermute | solution.py:1089
  227.5 50.2 %collective-permute-start.10 = (bf16[512,256]{1,0:T(8,128)(2,1)}, bf16[512,256]{1,0:T(8,128)(2,1)}, u32[]{:S(2)}, u32[]{:S(2)}) collective-permute-start(bf16[512,256]{1,0:T(8,128)(2,1)} %get-tuple-element.264), channel_id=1, source_target_pairs={{0,3},{1,0},{2,1},{3,2},{4,7},{5,4},{6,5},{7,6},{8,11},{9,8},{10,9... | collective-permute-start | bytes 786440 | tf_op jit(solution)/shard_map/ppermute | solution.py:1243
  231.3 46.4 %collective-permute-start.8 = (bf16[512,256]{1,0:T(8,128)(2,1)}, bf16[512,256]{1,0:T(8,128)(2,1)}, u32[]{:S(2)}, u32[]{:S(2)}) collective-permute-start(bf16[512,256]{1,0:T(8,128)(2,1)} %get-tuple-element.262), channel_id=1, source_target_pairs={{0,1},{1,2},{2,3},{3,0},{4,5},{5,6},{6,7},{7,4},{8,9},{9,10},{10,1... | collective-permute-start | bytes 786440 | tf_op jit(solution)/shard_map/ppermute | solution.py:1243
  231.3 46.4 %collective-permute-start.9 = (bf16[512,256]{1,0:T(8,128)(2,1)}, bf16[512,256]{1,0:T(8,128)(2,1)}, u32[]{:S(2)}, u32[]{:S(2)}) collective-permute-start(bf16[512,256]{1,0:T(8,128)(2,1)} %get-tuple-element.263), channel_id=1, source_target_pairs={{0,2},{1,3},{2,0},{3,1},{4,6},{5,7},{6,4},{7,5},{8,10},{9,11},{10,... | collective-permute-start | bytes 786440 | tf_op jit(solution)/shard_map/ppermute | solution.py:1243
  277.8 109.4 %all-gather.14.cloned.1.call-start = ((), (), s32[]{:S(2)}) async-start(), calls=%async_computation.7 | async-start | bytes 4718592 | tf_op jit(solution)/shard_map/all_gather | solution.py:1297
  280.6 20.7 %collective-permute-start.11 = (bf16[512,1024]{1,0:T(8,128)(2,1)}, bf16[512,1024]{1,0:T(8,128)(2,1)S(1)}, u32[]{:S(2)}, u32[]{:S(2)}) collective-permute-start(bf16[512,1024]{1,0:T(8,128)(2,1)} %add_convert_fusion.2), channel_id=1, source_target_pairs={{0,1},{1,2},{2,3},{3,0},{4,5},{5,6},{6,7},{7,4},{8,9},{9,10},{10,1... | collective-permute-start | bytes 3145736 | tf_op jit(solution)/shard_map/ppermute | solution.py:1089
  302.1 22.2 %collective-permute-start.12 = (bf16[512,1024]{1,0:T(8,128)(2,1)}, bf16[512,1024]{1,0:T(8,128)(2,1)}, u32[]{:S(2)}, u32[]{:S(2)}) collective-permute-start(bf16[512,1024]{1,0:T(8,128)(2,1)} %get-tuple-element.285), channel_id=1, source_target_pairs={{0,1},{1,2},{2,3},{3,0},{4,5},{5,6},{6,7},{7,4},{8,9},{9,10},{10,1... | collective-permute-start | bytes 3145736 | tf_op jit(solution)/shard_map/ppermute | solution.py:1089
  383.5 29.4 %collective-permute-start.13 = (bf16[512,1024]{1,0:T(8,128)(2,1)S(1)}, bf16[512,1024]{1,0:T(8,128)(2,1)S(1)}, u32[]{:S(2)}, u32[]{:S(2)}) collective-permute-start(bf16[512,1024]{1,0:T(8,128)(2,1)S(1)} %add_convert_fusion), channel_id=1, source_target_pairs={{0,1},{1,2},{2,3},{3,0},{4,5},{5,6},{6,7},{7,4},{8,9},{9,10},{10,1... | collective-permute-start | bytes 3145736 | tf_op jit(solution)/shard_map/ppermute | solution.py:1089
  (16 other events, 55.8 us)
Sparse Core Ops, SparseCore 0:
  10.2 45.5 all-gather.7
  58.2 26.3 all-gather.9
  87.1 45.3 all-gather.11
  223.5 49.7 reduce-scatter.2
  277.9 50.6 reduce-scatter.4
  330.3 36.6 all-gather.13

commit v4 on v3

--- a/solution.py
+++ b/solution.py
@@ -88,19 +88,16 @@
 
 
 def project_kernel(rows_ref, weight_ref, cos_ref, sin_ref, out_ref):
-    def pair(index, carry):
-        first = pl.multiple_of(index * 3 * LANES, LANES)
-        projected = dot_plain(rows_ref[...], weight_ref[:, pl.ds(first, 3 * LANES)])
-        for part in range(3):
-            piece = projected[:, part * LANES : (part + 1) * LANES]
-            if part < 2:
-                piece = piece * cos_ref[...] + partner(piece) * sin_ref[...]
-            if part == 0:
-                piece = piece * HEAD ** (-0.5)
-            out_ref[:, pl.ds(first + part * LANES, LANES)] = piece.astype(jnp.bfloat16)
-        return carry
-
-    lax.fori_loop(0, out_ref.shape[1] // (3 * LANES), pair, 0)
+    width = out_ref.shape[1]
+    projected = dot_plain(rows_ref[...], weight_ref[...])
+    for first in range(0, width, LANES):
+        piece = projected[:, first : first + LANES]
+        part = first // LANES % 3
+        if part < 2:
+            piece = piece * cos_ref[...] + partner(piece) * sin_ref[...]
+        if part == 0:
+            piece = piece * HEAD ** (-0.5)
+        out_ref[:, first : first + LANES] = piece.astype(jnp.bfloat16)
 
 
 def project(rows, weight, cosine, sine):
@@ -179,7 +176,7 @@
     def column(cols):
         out_ref[:, cols] = dot_plain(active_ref[...], down_ref[:, cols]).astype(out_ref.dtype)
 
-    in_chunks(out_ref.shape[1], 512, column)
+    in_chunks(out_ref.shape[1], 256, column)
 
 
 def down_term(slot, slots, activated, down, kept):
@@ -1111,23 +1108,14 @@
     for slot in range(narrow_count - 1):
         moving = send_on(token_blocks[slot])
         held = feed(slot, narrow_count, token_blocks[slot], norm_params, up_slice, held)
+        if slot == 1:
+            held, weight_rows = meet(held, weight_rows)
+            merge_all = wide_all(weight_rows[:, proj_cols:])
         if slot > 0:
             ready = [slot - 1, slot] if slot == narrow_count - 2 else [slot - 1]
             for block in ready:
                 kept = jnp.bfloat16 if block == 1 else jnp.float32
                 branch_terms.append(down_term(block, narrow_count, held[1], down_slice, kept))
-            if slot == 2:
-                if direct:
-                    merge_turn = pick_merge(merge_all, slots, own_width)
-                else:
-                    merge_turn = jnp.take(
-                        jnp.transpose(merge_all, (1, 2, 0, 3)).reshape(
-                            narrow_count, own_width, D
-                        ),
-                        slots,
-                        axis=0,
-                    ).reshape(D, D)
-                moving, merge_turn = meet(moving, merge_turn)
             moving, held, branch_terms, down_slice = meet(moving, held, branch_terms, down_slice)
         else:
             moving, held = meet(moving, held)
@@ -1135,8 +1123,8 @@
             lengths, slots, moving, weight_rows, down_slice = meet(
                 lengths, slots, moving, weight_rows, down_slice
             )
-            proj_all = wide_all(weight_rows[:, :proj_cols])
-            merge_all = wide_all(weight_rows[:, proj_cols:])
+            proj_rows, weight_rows = meet(weight_rows[:, :proj_cols], weight_rows)
+            proj_all = wide_all(proj_rows)
             branch_terms = []
         if slot == 1:
             places = (
@@ -1185,6 +1173,7 @@
             push_held,
         )
 
+    packed, grad_blocks[0] = meet(packed, grad_blocks[0])
     push_held = push_slot(0, ())
     branch_terms.append(
         down_term(narrow_count - 1, narrow_count, activated, down_slice, jnp.float32)
@@ -1290,8 +1279,8 @@
             heads_part = wide_sum(heads_grad)
         else:
             norm_part = pull_more(order[:-1][len(terms) : len(terms) + 3], norm_part)
-            moving, term_blocks[:], norm_part, feed_part = meet(
-                moving, term_blocks, norm_part, feed_part
+            moving, term_blocks[:], norm_part, feed_part, merge_all, slots = meet(
+                moving, term_blocks, norm_part, feed_part, merge_all, slots
             )
         if place == narrow_count - 3:
             feed_all = lax.all_gather(feed_part, "wide", axis=0).reshape(
@@ -1302,6 +1291,14 @@
     norm_part = pull_more(order[len(terms) : -1], norm_part)
     norm_part = pull_more([0], norm_part)
     branch = branch_moving.astype(jnp.float32) + branch_terms[0]
+    if direct:
+        merge_turn = pick_merge(merge_all, slots, own_width)
+    else:
+        merge_turn = jnp.take(
+            jnp.transpose(merge_all, (1, 2, 0, 3)).reshape(narrow_count, own_width, D),
+            slots,
+            axis=0,
+        ).reshape(D, D)
     merged = dot_plain(jnp.concatenate(pieces, axis=1), merge_turn)
     output_rows = tokens.astype(jnp.float32) + merged + branch
     layer_out = output_rows.astype(jnp.bfloat16)

time: 423 us -> 418 us (0.988); the launches traced: 426 us -> 411 us
  Pallas kernels: 276 us -> 266 us
    pallas_call x1, Pallas kernels: 49.5 us -> 39.5 us  [finish(): pl.pallas_call(partial(finish_kernel, narrow_count, wide_count, own_units...]
    ppermute x11, waiting for transfers between devices: 53.7 us -> 58 us  [send_on(): return lax.ppermute(array, 'narrow', onward)]
    reduce_scatter x2, waiting for transfers between devices: 4.29 us -> 0.02 us  [wide_sum(): return lax.psum_scatter(grad, 'wide', scatter_dimension=0, tiled=True)]
  transfers between devices with their start and end apart: 20 -> 20, of which waited for: 10 -> 8; matrix products, arithmetic and copies ran while one was open for 10% -> 9% of each run, Pallas kernels for 64% -> 63%
where the time goes in v4:
time: 418 us; the launch traced here: 411 us
  Pallas kernels  266 us (64%)
  waiting for transfers between devices  61.1 us (15%)
  other arithmetic  33.5 us (8%)
  starting transfers between devices  19.3 us (5%)
  between operations  15.1 us (4%)
  local copies, waits for them, and re-layouts  12.9 us (3%)
    ppermute x11, waiting for transfers between devices, send_on(): return lax.ppermute(array, 'narrow', onward)  58 us
    pallas_call x1, Pallas kernels, finish(): pl.pallas_call(partial(finish_kernel, narrow_count, wide_count, own_units...  39.5 us
    pallas_call x1, Pallas kernels, attend_back(): pl.pallas_call(partial(attend_back_kernel, block_q, block_k, heads_in), o...  33.8 us
    pallas_call x2, Pallas kernels, outer(): pl.pallas_call(partial(outer_kernel, bool(blocks)), out_shape=jax.ShapeDt...  28.6 us
    pallas_call x2, Pallas kernels, attend(): pl.pallas_call(partial(attend_kernel, block_q, block_k, heads_in), out_sh...  28.3 us
    pallas_call x4, Pallas kernels, feed(): pl.pallas_call(feed_kernel, out_shape=(jax.ShapeDtypeStruct((slots * rows...  27.8 us
    pallas_call x1, Pallas kernels, adam_all(): pl.pallas_call(adam_kernel, out_shape=tuple(shapes), grid=(count,), in_sp...  25.7 us
    pallas_call x4, Pallas kernels, down_term(): pl.pallas_call(down_kernel, out_shape=jax.ShapeDtypeStruct((rows, depth),...  21.2 us
  transfers between devices with their start and end apart: 20, of which 8 were waited for; matrix products, arithmetic and copies ran while one was open for 9% of the time, Pallas kernels for 63%

profile of v4, /device:TPU:0, one launch (start us, length us, event | category | flops | bytes accessed | tf_op | source)
XLA Modules:
  0.0 410.9 jit_solution(11852866535238849083)
XLA Ops:
  20.8 6.9 %feed.4 = (bf16[2048,1024]{1,0:T(8,128)(2,1)}, bf16[2048,1024]{1,0:T(8,128)(2,1)}, f32[2048,1024]{1,0:T(8,128)}) custom-call(bf16[512,1024]{1,0:T(8,128)(2,1)} %tokens_ref.3, f32[2,1024]{1,0:T(2,128)} %params_ref.9, bf16[1024,1024]{1,0:T(8,128)(2,1)} %convert_element_type.70.weight_ref.up_ref), custom_call_target="tpu_custom_call" | custom-call | tf_op jit(solution)/shard_map/feed/pallas_call | solution.py:150
  27.7 25.3 %collective-permute-done.tokens_ref.refs_0_ = bf16[512,1024]{1,0:T(8,128)(2,1)S(1)} collective-permute-done((bf16[512,1024]{1,0:T(8,128)(2,1)}, bf16[512,1024]{1,0:T(8,128)(2,1)S(1)}, u32[]{:S(2)}, u32[]{:S(2)}) %collective-permute-start) | collective-permute-done | bytes 1048608 | tf_op jit(solution)/shard_map/ppermute | solution.py:1086
  58.2 6.9 %feed.5 = (bf16[2048,1024]{1,0:T(8,128)(2,1)}, bf16[2048,1024]{1,0:T(8,128)(2,1)}, f32[2048,1024]{1,0:T(8,128)}) custom-call(bf16[512,1024]{1,0:T(8,128)(2,1)} %copy-done.5, f32[2,1024]{1,0:T(2,128)} %params_ref.9, bf16[1024,1024]{1,0:T(8,128)(2,1)} %convert_element_type.70.weight_ref.up_ref, ...), custom_call_target="tpu_custom_call", output_to_operand_aliasing={{0}: (3, {}), {1}: (4, {}), {2}: (5, {})} | custom-call | tf_op jit(solution)/shard_map/feed/pallas_call | solution.py:150
  66.9 5.3 %down_term.4 = f32[512,1024]{1,0:T(8,128)} custom-call(bf16[2048,1024]{1,0:T(8,128)(2,1)} %get-tuple-element.207.active_ref.refs_1_, bf16[1024,1024]{1,0:T(8,128)(2,1)} %convert_element_type.73.down_ref), custom_call_target="tpu_custom_call" | custom-call | tf_op jit(solution)/shard_map/down_term/pallas_call | solution.py:186
  74.2 5.6 %fusion = (f32[2048,128]{1,0:T(8,128)}, f32[2048,128]{1,0:T(8,128)}) fusion(f32[128]{0:T(128)S(1)} %compare_select_fusion.2, f32[128]{0:T(128)S(1)} %mul.51, f32[2048]{0:T(1024)S(1)} %subtract_convert_fusion), kind=kLoop, calls=%fused_computation.11 | loop fusion | flops 524288 | bytes 2106368 | tf_op jit(solution)/shard_map/mul | solution.py:77
  86.0 6.9 %feed.6 = (bf16[2048,1024]{1,0:T(8,128)(2,1)}, bf16[2048,1024]{1,0:T(8,128)(2,1)}, f32[2048,1024]{1,0:T(8,128)}) custom-call(bf16[512,1024]{1,0:T(8,128)(2,1)} %copy-done.6, f32[2,1024]{1,0:T(2,128)} %params_ref.9, bf16[1024,1024]{1,0:T(8,128)(2,1)} %convert_element_type.70.weight_ref.up_ref, ...), custom_call_target="tpu_custom_call", output_to_operand_aliasing={{0}: (3, {}), {1}: (4, {}), {2}: (5, {})} | custom-call | tf_op jit(solution)/shard_map/feed/pallas_call | solution.py:150
  92.9 5.4 %down_term.6 = f32[512,1024]{1,0:T(8,128)} custom-call(bf16[2048,1024]{1,0:T(8,128)(2,1)} %get-tuple-element.218.active_ref.refs_1_, bf16[1024,1024]{1,0:T(8,128)(2,1)} %convert_element_type.73.down_ref), custom_call_target="tpu_custom_call" | custom-call | tf_op jit(solution)/shard_map/down_term/pallas_call | solution.py:186
  103.5 7.5 %collective-permute-done.2.tokens_ref.refs_2_ = bf16[512,1024]{1,0:T(8,128)(2,1)S(1)} collective-permute-done((bf16[512,1024]{1,0:T(8,128)(2,1)S(1)}, bf16[512,1024]{1,0:T(8,128)(2,1)S(1)}, u32[]{:S(2)}, u32[]{:S(2)}) %collective-permute-start.2) | collective-permute-done | bytes 1048608 | tf_op jit(solution)/shard_map/ppermute | solution.py:1086
  112.0 7.1 %feed.7 = (bf16[2048,1024]{1,0:T(8,128)(2,1)}, bf16[2048,1024]{1,0:T(8,128)(2,1)}, f32[2048,1024]{1,0:T(8,128)}) custom-call(bf16[512,1024]{1,0:T(8,128)(2,1)} %copy-done.7, f32[2,1024]{1,0:T(2,128)} %params_ref.9, bf16[1024,1024]{1,0:T(8,128)(2,1)} %convert_element_type.70.weight_ref.up_ref, ...), custom_call_target="tpu_custom_call", output_to_operand_aliasing={{0}: (3, {}), {1}: (4, {}), {2}: (5, {})} | custom-call | tf_op jit(solution)/shard_map/feed/pallas_call | solution.py:150
  119.1 5.3 %down_term.7 = f32[512,1024]{1,0:T(8,128)} custom-call(bf16[2048,1024]{1,0:T(8,128)(2,1)} %get-tuple-element.271.active_ref.second_left, bf16[1024,1024]{1,0:T(8,128)(2,1)} %convert_element_type.73.down_ref), custom_call_target="tpu_custom_call" | custom-call | tf_op jit(solution)/shard_map/down_term/pallas_call | solution.py:186
  124.4 8.5 %project_all.1 = (bf16[2048,768]{1,0:T(8,128)(2,1)}, bf16[1024,768]{1,0:T(8,128)(2,1)}) custom-call(s32[1]{0:T(128)} %bitcast.3.index_ref, bf16[2048,1024]{1,0:T(8,128)(2,1)} %get-tuple-element.220.rows_ref.first_left, f32[2048,128]{1,0:T(8,128)} %get-tuple-element.221.cos_ref, f32[2048,128]{1,0:T(8,128)} %get-tuple-element.222.sin_ref, ...), custom_call_target="tpu_custom_call" | custom-call | tf_op jit(solution)/shard_map/project_all/pallas_call | solution.py:398
  144.8 14.2 %attend.2 = (bf16[2048,256]{1,0:T(8,128)(2,1)}, f32[256,2048]{1,0:T(8,128)}, f32[2,8,2048]{2,1,0:T(8,128)}) custom-call(s32[4]{0:T(128)} %copy-done.14, s32[4]{0:T(128)} %select_reduce_fusion.3.first_ref, s32[4]{0:T(128)} %get-tuple-element.240.last_ref, s32[1,2048]{1,0:T(1,128)} %bitcast.36, ...), custom_call_target="tpu_custom_call" | custom-call | tf_op jit(solution)/shard_map/attend/pallas_call | solution.py:550
  159.0 6.6 %collective-permute-done.5.grad_ref = bf16[512,1024]{1,0:T(8,128)(2,1)S(1)} collective-permute-done((bf16[512,1024]{1,0:T(8,128)(2,1)}, bf16[512,1024]{1,0:T(8,128)(2,1)S(1)}, u32[]{:S(2)}, u32[]{:S(2)}) %collective-permute-start.5) | collective-permute-done | bytes 1048608 | tf_op jit(solution)/shard_map/ppermute | solution.py:1086
  171.8 14.1 %attend.3 = (bf16[2048,256]{1,0:T(8,128)(2,1)}, f32[256,2048]{1,0:T(8,128)}, f32[2,8,2048]{2,1,0:T(8,128)}) custom-call(s32[4]{0:T(128)} %copy-done.14, s32[4]{0:T(128)} %select_reduce_fusion.3.first_ref, s32[4]{0:T(128)} %get-tuple-element.240.last_ref, s32[1,2048]{1,0:T(1,128)} %bitcast.37, ...), custom_call_target="tpu_custom_call", output_to_operand_aliasing={{0}: (7, {}), {1}: (8, {}), {2}: (9, {})} | custom-call | tf_op jit(solution)/shard_map/attend/pallas_call | solution.py:550
  185.9 7.6 %collective-permute-done.6.grad_ref = bf16[512,1024]{1,0:T(8,128)(2,1)S(1)} collective-permute-done((bf16[512,1024]{1,0:T(8,128)(2,1)S(1)}, bf16[512,1024]{1,0:T(8,128)(2,1)S(1)}, u32[]{:S(2)}, u32[]{:S(2)}) %collective-permute-start.6) | collective-permute-done | bytes 1048608 | tf_op jit(solution)/shard_map/ppermute | solution.py:1086
  199.4 16.9 %outer.2 = bf16[8,2,128,1024]{3,2,1,0:T(8,128)(2,1)} custom-call(bf16[2048,1024]{1,0:T(8,128)(2,1)} %get-tuple-element.220.rows_ref.first_left, bf16[2048,1024]{1,0:T(8,128)(2,1)} %get-tuple-element.270.first_right.hidden_ref, bf16[2048,1024]{1,0:T(8,128)(2,1)} %get-tuple-element.271.active_ref.second_left, ...), custom_call_target="tpu_custom_call" | custom-call | tf_op jit(solution)/shard_map/outer/pallas_call | solution.py:241
  225.8 33.8 %attend_back.1.first_right.mixed_ref = bf16[2048,768]{1,0:T(8,128)(2,1)} custom-call(s32[4]{0:T(128)} %copy-done.14, s32[4]{0:T(128)} %get-tuple-element.240.last_ref, s32[4]{0:T(128)} %get-tuple-element.280.end_ref, s32[1,2048]{1,0:T(1,128)} %bitcast.38, f32[2048,128]{1,0:T(8,128)} %get-tuple-element.221.cos_ref, f32[2048,128]{1,0:T(8,128)} %get-tuple-element.222.sin_ref, ...), custom_call_target="tpu_custom_call" | custom-call | tf_op jit(solution)/shard_map/attend_back/pallas_call | solution.py:695
  259.6 11.7 %outer.3 = bf16[1024,1024]{1,0:T(8,128)(2,1)} custom-call(bf16[2048,1024]{1,0:T(8,128)(2,1)} %get-tuple-element.220.rows_ref.first_left, bf16[2048,768]{1,0:T(8,128)(2,1)} %attend_back.1.first_right.mixed_ref, bf16[2048,1024]{1,0:T(8,128)(2,1)} %get-tuple-element.272.second_right.second_left, bf16[2048,256]{1,0:T(8,128)(2,1)} %get-tuple-element.265.second_right), custom_call_target="tpu_custom_call" | custom-call | tf_op jit(solution)/shard_map/outer/pallas_call | solution.py:241
  277.9 14.4 %pull.2 = (bf16[512,1024]{1,0:T(8,128)(2,1)}, f32[1536,1024]{1,0:T(8,128)}, f32[2,1024]{1,0:T(2,128)}) custom-call(bf16[2048,768]{1,0:T(8,128)(2,1)} %attend_back.1.first_right.mixed_ref, bf16[2048,1024]{1,0:T(8,128)(2,1)} %get-tuple-element.270.first_right.hidden_ref, bf16[1024,768]{1,0:T(8,128)(2,1)} %get-tuple-element.292.proj_ref, ...), custom_call_target="tpu_custom_call" | custom-call | tf_op jit(solution)/shard_map/pull/pallas_call | solution.py:348
  292.2 5.8 %collective-permute-done.11 = bf16[512,1024]{1,0:T(8,128)(2,1)S(1)} collective-permute-done((bf16[512,1024]{1,0:T(8,128)(2,1)}, bf16[512,1024]{1,0:T(8,128)(2,1)S(1)}, u32[]{:S(2)}, u32[]{:S(2)}) %collective-permute-start.11) | collective-permute-done | bytes 1048608 | tf_op jit(solution)/shard_map/ppermute | solution.py:1086
  301.8 6.8 %pull.3 = (bf16[512,1024]{1,0:T(8,128)(2,1)}, f32[512,1024]{1,0:T(8,128)}, f32[2,1024]{1,0:T(2,128)}) custom-call(bf16[2048,768]{1,0:T(8,128)(2,1)} %attend_back.1.first_right.mixed_ref, bf16[2048,1024]{1,0:T(8,128)(2,1)} %get-tuple-element.270.first_right.hidden_ref, bf16[1024,768]{1,0:T(8,128)(2,1)} %get-tuple-element.292.proj_ref, ...), custom_call_target="tpu_custom_call" | custom-call | tf_op jit(solution)/shard_map/pull/pallas_call | solution.py:348
  309.3 6.3 %pick_merge.1 = bf16[1024,1024]{1,0:T(8,128)(2,1)} custom-call(s32[4]{0:T(128)} %copy-done.14, bf16[8,4,256,128]{3,2,1,0:T(8,128)(2,1)} %bitcast.33), custom_call_target="tpu_custom_call" | custom-call | tf_op jit(solution)/shard_map/pick_merge/pallas_call | solution.py:434
  326.8 39.5 %finish.1 = (f32[24,128]{1,0:T(8,128)}, f32[8,128]{1,0:T(8,128)}, bf16[512,1024]{1,0:T(8,128)(2,1)}, bf16[256,384]{1,0:T(8,128)(2,1)}) custom-call(f32[24,128]{1,0:T(8,128)} %select_maximum_fusion.refs_0_, bf16[128,1024]{1,0:T(8,128)(2,1)} %reduce-scatter.5.cloned.1.call-done.refs_1_.merge_ref, bf16[256,1024]{1,0:T(8,128)(2,1)} %reduce-scatter.3.cloned.1.call-done.refs_2_, ...), custom_call_target="tpu_custom_call" | custom-call | tf_op jit(solution)/shard_map/finish/pallas_call | solution.py:911
  372.2 25.7 %adam_all.1 = (f32[1024,1024]{1,0:T(8,128)}, f32[1024,1024]{1,0:T(8,128)}, f32[1024,1024]{1,0:T(8,128)}, bf16[1024,1024]{1,0:T(8,128)(2,1)}, f32[1024,1024]{1,0:...) custom-call(f32[1,4]{1,0:T(1,128)} %maximum_bitcast_fusion.scale_ref, ...), custom_call_target="tpu_custom_call" | custom-call | tf_op jit(solution)/shard_map/adam_all/pallas_call | solution.py:995
  (124 shorter events, 101.8 us)
Async XLA Ops:
  7.2 48.5 %all-gather.8.cloned.1.call-start = ((), (), s32[]{:S(2)}) async-start(), calls=%async_computation.2 | async-start | bytes 1310720 | tf_op jit(solution)/shard_map/all_gather | solution.py:1095
  9.9 114.4 %all-gather.10.cloned.1.call-start = ((), (), s32[]{:S(2)}) async-start(), calls=%async_computation.5 | async-start | bytes 7077888 | tf_op jit(solution)/shard_map/all_gather | solution.py:1100
  10.0 42.9 %collective-permute-start = (bf16[512,1024]{1,0:T(8,128)(2,1)}, bf16[512,1024]{1,0:T(8,128)(2,1)S(1)}, u32[]{:S(2)}, u32[]{:S(2)}) collective-permute-start(bf16[512,1024]{1,0:T(8,128)(2,1)} %tokens_ref.3), channel_id=1, source_target_pairs={{0,1},{1,2},{2,3},{3,0},{4,5},{5,6},{6,7},{7,4},{8,9},{9,10},{10,1... | collective-permute-start | bytes 3145736 | tf_op jit(solution)/shard_map/ppermute | solution.py:1086
  27.6 39.1 %copy-start.14 = (s32[4]{0:T(128)}, s32[4]{0:T(128)S(1)}, u32[]{:S(2)}) copy-start(s32[4]{0:T(128)S(1)} %compare_select_fusion.slots_ref) | copy-start | bytes 52
  57.8 75.3 %all-gather.12.cloned.1.call-start = ((), (), s32[]{:S(2)}) async-start(), calls=%async_computation.6 | async-start | bytes 2359296 | tf_op jit(solution)/shard_map/all_gather | solution.py:1100
  58.1 26.9 %collective-permute-start.1 = (bf16[512,1024]{1,0:T(8,128)(2,1)S(1)}, bf16[512,1024]{1,0:T(8,128)(2,1)S(1)}, u32[]{:S(2)}, u32[]{:S(2)}) collective-permute-start(bf16[512,1024]{1,0:T(8,128)(2,1)S(1)} %collective-permute-done.tokens_ref.refs_0_), channel_id=1, source_target_pairs={{0,1},{1,2},{2,3},{3,0},{4,5},{5,6},{6,7},{7,4},{8,9},{9,10},{10,1... | collective-permute-start | bytes 3145736 | tf_op jit(solution)/shard_map/ppermute | solution.py:1086
  66.8 204.6 %reduce-scatter.3.cloned.1.call-start = ((), (), s32[]{:S(2)}) async-start(), calls=%async_computation.3 | async-start | bytes 4718592 | tf_op jit(solution)/shard_map/reduce_scatter | solution.py:1187
  74.2 18.7 %copy-start.13 = (s32[2048]{0:T(1024)}, s32[2048]{0:T(1024)S(1)}, u32[]{:S(2)}) copy-start(s32[2048]{0:T(1024)S(1)} %select_reduce_fusion) | copy-start | bytes 24580
  85.0 26.0 %collective-permute-start.2 = (bf16[512,1024]{1,0:T(8,128)(2,1)S(1)}, bf16[512,1024]{1,0:T(8,128)(2,1)S(1)}, u32[]{:S(2)}, u32[]{:S(2)}) collective-permute-start(bf16[512,1024]{1,0:T(8,128)(2,1)S(1)} %collective-permute-done.1.tokens_ref.refs_1_), channel_id=1, source_target_pairs={{0,1},{1,2},{2,3},{3,0},{4,5},{5,6},{6,7},{7,4},{8,9},{9,10},{10,1... | collective-permute-start | bytes 3145736 | tf_op jit(solution)/shard_map/ppermute | solution.py:1086
  111.0 27.1 %collective-permute-start.3 = (bf16[512,1024]{1,0:T(8,128)(2,1)S(1)}, bf16[512,1024]{1,0:T(8,128)(2,1)}, u32[]{:S(2)}, u32[]{:S(2)}) collective-permute-start(bf16[512,1024]{1,0:T(8,128)(2,1)S(1)} %copy-done.8), channel_id=1, source_target_pairs={{0,1},{1,2},{2,3},{3,0},{4,5},{5,6},{6,7},{7,4},{8,9},{9,10},{10,1... | collective-permute-start | bytes 3145736 | tf_op jit(solution)/shard_map/ppermute | solution.py:1086
  138.1 27.5 %collective-permute-start.5 = (bf16[512,1024]{1,0:T(8,128)(2,1)}, bf16[512,1024]{1,0:T(8,128)(2,1)S(1)}, u32[]{:S(2)}, u32[]{:S(2)}) collective-permute-start(bf16[512,1024]{1,0:T(8,128)(2,1)} %collective-permute-done.3.grad_ref), channel_id=1, source_target_pairs={{0,1},{1,2},{2,3},{3,0},{4,5},{5,6},{6,7},{7,4},{8,9},{9,10},{10,1... | collective-permute-start | bytes 3145736 | tf_op jit(solution)/shard_map/ppermute | solution.py:1086
  144.8 20.9 %copy-start.9 = (bf16[512,1024]{1,0:T(8,128)(2,1)S(1)}, bf16[512,1024]{1,0:T(8,128)(2,1)}, u32[]{:S(2)}) copy-start(bf16[512,1024]{1,0:T(8,128)(2,1)} %down_term.5) | copy-start | bytes 3145732
  165.6 27.8 %collective-permute-start.6 = (bf16[512,1024]{1,0:T(8,128)(2,1)S(1)}, bf16[512,1024]{1,0:T(8,128)(2,1)S(1)}, u32[]{:S(2)}, u32[]{:S(2)}) collective-permute-start(bf16[512,1024]{1,0:T(8,128)(2,1)S(1)} %collective-permute-done.5.grad_ref), channel_id=1, source_target_pairs={{0,1},{1,2},{2,3},{3,0},{4,5},{5,6},{6,7},{7,4},{8,9},{9,10},{10,1... | collective-permute-start | bytes 3145736 | tf_op jit(solution)/shard_map/ppermute | solution.py:1086
  165.7 51.5 %collective-permute-start.4 = (bf16[512,1024]{1,0:T(8,128)(2,1)S(1)}, bf16[512,1024]{1,0:T(8,128)(2,1)}, u32[]{:S(2)}, u32[]{:S(2)}) collective-permute-start(bf16[512,1024]{1,0:T(8,128)(2,1)S(1)} %copy-done.9), channel_id=1, source_target_pairs={{0,1},{1,2},{2,3},{3,0},{4,5},{5,6},{6,7},{7,4},{8,9},{9,10},{10,1... | collective-permute-start | bytes 3145736 | tf_op jit(solution)/shard_map/ppermute | solution.py:1086
  199.4 16.9 %copy-start.1 = (bf16[2048,256]{1,0:T(8,128)(2,1)S(1)}, bf16[2048,256]{1,0:T(8,128)(2,1)}, u32[]{:S(2)}) copy-start(bf16[2048,256]{1,0:T(8,128)(2,1)} %get-tuple-element.265.second_right) | copy-start | bytes 3145732
  217.2 106.7 %reduce-scatter.5.cloned.1.call-start = ((), (), s32[]{:S(2)}) async-start(), calls=%async_computation.4 | async-start | bytes 2359296 | tf_op jit(solution)/shard_map/reduce_scatter | solution.py:1187
  221.4 50.0 %collective-permute-start.7 = (bf16[512,1024]{1,0:T(8,128)(2,1)}, bf16[512,1024]{1,0:T(8,128)(2,1)S(1)}, u32[]{:S(2)}, u32[]{:S(2)}) collective-permute-start(bf16[512,1024]{1,0:T(8,128)(2,1)} %add_convert_fusion.3), channel_id=1, source_target_pairs={{0,1},{1,2},{2,3},{3,0},{4,5},{5,6},{6,7},{7,4},{8,9},{9,10},{10,1... | collective-permute-start | bytes 3145736 | tf_op jit(solution)/shard_map/ppermute | solution.py:1086
  221.4 50.0 %collective-permute-start.10 = (bf16[512,256]{1,0:T(8,128)(2,1)}, bf16[512,256]{1,0:T(8,128)(2,1)}, u32[]{:S(2)}, u32[]{:S(2)}) collective-permute-start(bf16[512,256]{1,0:T(8,128)(2,1)} %get-tuple-element.279), channel_id=1, source_target_pairs={{0,3},{1,0},{2,1},{3,2},{4,7},{5,4},{6,5},{7,6},{8,11},{9,8},{10,9... | collective-permute-start | bytes 786440 | tf_op jit(solution)/shard_map/ppermute | solution.py:1232
  225.2 46.1 %collective-permute-start.8 = (bf16[512,256]{1,0:T(8,128)(2,1)}, bf16[512,256]{1,0:T(8,128)(2,1)}, u32[]{:S(2)}, u32[]{:S(2)}) collective-permute-start(bf16[512,256]{1,0:T(8,128)(2,1)} %get-tuple-element.277), channel_id=1, source_target_pairs={{0,1},{1,2},{2,3},{3,0},{4,5},{5,6},{6,7},{7,4},{8,9},{9,10},{10,1... | collective-permute-start | bytes 786440 | tf_op jit(solution)/shard_map/ppermute | solution.py:1232
  225.2 46.1 %collective-permute-start.9 = (bf16[512,256]{1,0:T(8,128)(2,1)}, bf16[512,256]{1,0:T(8,128)(2,1)}, u32[]{:S(2)}, u32[]{:S(2)}) collective-permute-start(bf16[512,256]{1,0:T(8,128)(2,1)} %get-tuple-element.278), channel_id=1, source_target_pairs={{0,2},{1,3},{2,0},{3,1},{4,6},{5,7},{6,4},{7,5},{8,10},{9,11},{10,... | collective-permute-start | bytes 786440 | tf_op jit(solution)/shard_map/ppermute | solution.py:1232
  271.4 100.8 %all-gather.14.cloned.1.call-start = ((), (), s32[]{:S(2)}) async-start(), calls=%async_computation.7 | async-start | bytes 4718592 | tf_op jit(solution)/shard_map/all_gather | solution.py:1286
  274.2 23.8 %collective-permute-start.11 = (bf16[512,1024]{1,0:T(8,128)(2,1)}, bf16[512,1024]{1,0:T(8,128)(2,1)S(1)}, u32[]{:S(2)}, u32[]{:S(2)}) collective-permute-start(bf16[512,1024]{1,0:T(8,128)(2,1)} %add_convert_fusion.2), channel_id=1, source_target_pairs={{0,1},{1,2},{2,3},{3,0},{4,5},{5,6},{6,7},{7,4},{8,9},{9,10},{10,1... | collective-permute-start | bytes 3145736 | tf_op jit(solution)/shard_map/ppermute | solution.py:1086
  298.8 25.1 %collective-permute-start.12 = (bf16[512,1024]{1,0:T(8,128)(2,1)}, bf16[512,1024]{1,0:T(8,128)(2,1)S(1)}, u32[]{:S(2)}, u32[]{:S(2)}) collective-permute-start(bf16[512,1024]{1,0:T(8,128)(2,1)} %get-tuple-element.301), channel_id=1, source_target_pairs={{0,1},{1,2},{2,3},{3,0},{4,5},{5,6},{6,7},{7,4},{8,9},{9,10},{10,1... | collective-permute-start | bytes 3145736 | tf_op jit(solution)/shard_map/ppermute | solution.py:1086
  368.5 29.4 %collective-permute-start.13 = (bf16[512,1024]{1,0:T(8,128)(2,1)S(1)}, bf16[512,1024]{1,0:T(8,128)(2,1)S(1)}, u32[]{:S(2)}, u32[]{:S(2)}) collective-permute-start(bf16[512,1024]{1,0:T(8,128)(2,1)S(1)} %add_convert_fusion), channel_id=1, source_target_pairs={{0,1},{1,2},{2,3},{3,0},{4,5},{5,6},{6,7},{7,4},{8,9},{9,10},{10,1... | collective-permute-start | bytes 3145736 | tf_op jit(solution)/shard_map/ppermute | solution.py:1086
  (14 other events, 49.6 us)
Sparse Core Ops, SparseCore 0:
  10.2 45.5 all-gather.7
  58.2 44.5 all-gather.9
  105.3 27.8 all-gather.11
  217.3 48.3 reduce-scatter.2
  271.6 41.4 reduce-scatter.4
  314.8 36.5 all-gather.13
